TPU v7x, 512 devices: a whole 4x4x16 slice. The times are simulated.
512 devices in a mesh: rep: 4 (over y), blk: 32 (over z, core), tp: 4 (over x).
Axes of the slice: x: 4, y: 4, z: 16, core: 2. Of those that a mesh axis runs over, the one named last changes fastest.
Arguments:
- hidden: bfloat16 [16, 2048], P('rep', 'blk'), may hold values from -64 to 64
- ln_gain: float32 [2, 2048], P(None, 'blk'), may hold values from 0.1 to 1.9
- w_qkv: bfloat16 [2, 2048, 3, 2048], P(None, 'blk', None, 'tp'), may hold values from -0.125 to 0.125
- w_fc1: bfloat16 [2, 2048, 8192], P(None, 'blk', 'tp'), may hold values from -0.125 to 0.125
- w_out: bfloat16 [2, 2048, 2048], P(None, 'tp', 'blk'), may hold values from -0.125 to 0.125
- w_fc2: bfloat16 [2, 8192, 2048], P(None, 'tp', 'blk'), may hold values from -0.0625 to 0.0625
- caches: bfloat16 [2, 2, 1024, 32, 2048], P(None, None, ('rep', 'blk'), None, 'tp'), may hold values from -110 to 110
- page_owner: int32 [1024], P(('rep', 'blk')), may hold values from 0 to 15, as said below
- page_used: int32 [1024], P(('rep', 'blk')), may hold values from 0 to 1, as said below
- page_fill: int32 [1024], P(('rep', 'blk')), may hold values from 0 to 32, as said below
- page_tail: int32 [1024], P(('rep', 'blk')), may hold values from 0 to 1
- positions: int32 [16], P('rep'), may hold values from 0 to 4095
Outputs:
- hidden_out: bfloat16 [16, 2048], P('rep', 'blk')
- caches_out: bfloat16 [2, 2, 1024, 32, 2048], P(None, None, ('rep', 'blk'), None, 'tp')
Inputs may be any that keep to these rules, and one draw needn't show every extreme that they name: `page_owner`: requests are numbered replica by replica, 4 to a replica. Each request has exactly one page with page_tail 1, which is used and lies among the pages of its own replica; other pages of a request may lie on any replica. `page_used`: every page with page_tail 1 is used. `page_fill`: A used page with page_tail 0 is full; a page with page_tail 1 holds fewer than 32 tokens; an unused page holds 0.
All inputs are finite; a program needn't handle non-finite values.
Results may differ from a plain program's by a relative error of at most 0.012.
The roundings to bfloat16 on the way count: a program that leaves them out, or rounds other values in their place, can miss the bound.
Values may be sent and summed in bfloat16 or wider, within the bound.
No kernel may reach another device: no remote copies, remote signals or barrier semaphores. Data moves between devices by JAX's collectives and lax.ppermute only.
A program may use at most 64 MiB of HBM per device.

v0:
```python
import jax
import jax.numpy as jnp
from jax import lax
from jax.sharding import PartitionSpec as P

D = 2048
HD = 64
ROT = 32
LAYERS = 2
PAGE = 32


EPSILON = 1e-05
LOWEST = -1e30


def combined_all(value, axis, join):
    pieces = jax.tree.map(lambda part: lax.all_gather(part, axis), value)
    head = jax.tree.map(lambda part: part[0], pieces)
    tail = jax.tree.map(lambda part: part[1:], pieces)
    so_far, _ = lax.scan(lambda so_far, piece: (join(so_far, piece), None), head, tail)
    return so_far


def rotate_heads(tensor, positions):
    half_rot = ROT // 2
    steps_f = jnp.arange(half_rot, dtype=jnp.float32)
    inverse = 10000.0 ** (-2.0 * steps_f / ROT)
    angles = positions.astype(jnp.float32)[:, None] * inverse[None, :]
    cosine = jnp.cos(angles)[:, None, :]
    sine_val = jnp.sin(angles)[:, None, :]
    first_half = tensor[..., :half_rot]
    second_half = tensor[..., half_rot:ROT]
    return jnp.concatenate(
        [
            first_half * cosine - second_half * sine_val,
            second_half * cosine + first_half * sine_val,
            tensor[..., ROT:],
        ],
        axis=-1,
    )


def page_partials(query_rows, key_pages, value_pages, valid):
    scores = jnp.einsum(
        "shd,sphd->shp", query_rows, key_pages, preferred_element_type=jnp.float32
    ) * HD ** (-0.5)
    scores = jnp.where(valid[:, None, :], scores, LOWEST)
    highest = jnp.max(scores, axis=-1)
    weights = jnp.where(valid[:, None, :], jnp.exp(scores - highest[..., None]), 0.0)
    totals = jnp.sum(weights, axis=-1)
    rounded = weights.astype(jnp.bfloat16)
    outputs = jnp.einsum("shp,sphd->shd", rounded, value_pages, preferred_element_type=jnp.float32)
    return (highest, totals, outputs)


def merge_parts(left_part, right_part):
    left_high, left_total, left_out = left_part
    right_high, right_total, right_out = right_part
    joined = jnp.maximum(left_high, right_high)
    left_factor = jnp.exp(left_high - joined)
    right_factor = jnp.exp(right_high - joined)
    return (
        joined,
        left_total * left_factor + right_total * right_factor,
        left_out * left_factor[..., None] + right_out * right_factor[..., None],
    )


def per_device(
    hidden,
    ln_gain,
    w_qkv,
    w_fc1,
    w_out,
    w_fc2,
    caches,
    page_owner,
    page_used,
    page_fill,
    page_tail,
    positions,
):
    req_rows = hidden.shape[0]
    slot_count = page_owner.shape[0]
    width = w_out.shape[1]
    heads = width // HD
    rep_count = lax.axis_size("rep")
    rep_index = lax.axis_index("rep")
    all_reqs = req_rows * rep_count
    offsets = jnp.arange(PAGE, dtype=jnp.int32)
    is_tail = page_tail == 1
    is_used = page_used == 1
    write_at = (offsets[None, :] == page_fill[:, None]) & is_tail[:, None]
    valid = is_used[:, None] & (offsets[None, :] < (page_fill + page_tail)[:, None])
    home_rows = page_owner - rep_index * req_rows
    pick_home = (
        (home_rows[:, None] == jnp.arange(req_rows, dtype=jnp.int32)[None, :]) & is_tail[:, None]
    ).astype(jnp.bfloat16)
    pick_owner = page_owner[:, None] == jnp.arange(all_reqs, dtype=jnp.int32)[None, :]
    pick_query = pick_owner.astype(jnp.bfloat16)
    own_mask = pick_owner & is_used[:, None]
    own_map = own_mask.astype(jnp.float32)
    state = hidden
    cache_list = []
    for layer in range(LAYERS):
        resid = state.astype(jnp.float32)
        average = lax.psum(jnp.sum(resid, axis=-1), "blk") / D
        centered = resid - average[:, None]
        variance = lax.psum(jnp.sum(centered * centered, axis=-1), "blk") / D
        normed = (
            centered * lax.rsqrt(variance + EPSILON)[:, None] * ln_gain[layer][None, :]
        ).astype(jnp.bfloat16)
        qkv_part = jnp.dot(
            normed,
            w_qkv[layer].reshape(normed.shape[1], 3 * width),
            preferred_element_type=jnp.float32,
        )
        inner_part = jnp.dot(normed, w_fc1[layer], preferred_element_type=jnp.float32)
        qkv_full, inner = lax.psum((qkv_part, inner_part), "blk")
        mlp_act = jax.nn.gelu(inner, approximate=True).astype(jnp.bfloat16)
        qkv_full = qkv_full.reshape(req_rows, 3, heads, HD)
        mlp_part = jnp.dot(mlp_act, w_fc2[layer], preferred_element_type=jnp.float32)
        queries = (
            rotate_heads(qkv_full[:, 0], positions).astype(jnp.bfloat16).reshape(req_rows, width)
        )
        new_keys = (
            rotate_heads(qkv_full[:, 1], positions).astype(jnp.bfloat16).reshape(req_rows, width)
        )
        new_values = qkv_full[:, 2].astype(jnp.bfloat16).reshape(req_rows, width)
        gathered = lax.all_gather(queries, "rep", axis=0, tiled=True)
        fresh = jnp.dot(
            pick_home,
            jnp.concatenate([new_keys, new_values], axis=1),
            preferred_element_type=jnp.float32,
        ).astype(jnp.bfloat16)
        key_pages = jnp.where(write_at[:, :, None], fresh[:, None, :width], caches[layer, 0])
        value_pages = jnp.where(write_at[:, :, None], fresh[:, None, width:], caches[layer, 1])
        cache_list.append(jnp.stack([key_pages, value_pages]))
        query_rows = (
            jnp.dot(pick_query, gathered, preferred_element_type=jnp.float32)
            .astype(jnp.bfloat16)
            .reshape(slot_count, heads, HD)
        )
        highest, totals, outputs = page_partials(
            query_rows,
            key_pages.reshape(slot_count, PAGE, heads, HD),
            value_pages.reshape(slot_count, PAGE, heads, HD),
            valid,
        )
        masked_high = jnp.where(is_used[:, None], highest, LOWEST)
        local_high = jnp.max(
            jnp.where(own_mask[:, :, None], masked_high[:, None, :], LOWEST), axis=0
        )
        slot_high = jnp.sum(jnp.where(own_mask[:, :, None], local_high[None, :, :], 0.0), axis=1)
        scale_w = jnp.where(is_used[:, None], jnp.exp(highest - slot_high), 0.0)
        local_total = jnp.einsum(
            "sr,sh->rh", own_map, totals * scale_w, precision=lax.Precision.HIGHEST
        )
        local_out = jnp.einsum(
            "sr,shd->rhd", own_map, outputs * scale_w[..., None], precision=lax.Precision.HIGHEST
        )
        merged_high, merged_total, merged_out = combined_all(
            (local_high, local_total, local_out), ("rep", "blk"), merge_parts
        )
        req_total = lax.dynamic_slice_in_dim(merged_total, rep_index * req_rows, req_rows, 0)
        req_out = lax.dynamic_slice_in_dim(merged_out, rep_index * req_rows, req_rows, 0)
        attended = (req_out / req_total[..., None]).reshape(req_rows, width).astype(jnp.bfloat16)
        attn_part = jnp.dot(attended, w_out[layer], preferred_element_type=jnp.float32)
        branch_total = lax.psum(attn_part + mlp_part, "tp")
        state = (resid + branch_total).astype(jnp.bfloat16)
    return (state, jnp.stack(cache_list))


def solution(mesh):
    in_specs = (
        P("rep", "blk"),
        P(None, "blk"),
        P(None, "blk", None, "tp"),
        P(None, "blk", "tp"),
        P(None, "tp", "blk"),
        P(None, "tp", "blk"),
        P(None, None, ("rep", "blk"), None, "tp"),
        P(("rep", "blk")),
        P(("rep", "blk")),
        P(("rep", "blk")),
        P(("rep", "blk")),
        P("rep"),
    )
    out_specs = (P("rep", "blk"), P(None, None, ("rep", "blk"), None, "tp"))
    return jax.shard_map(
        per_device, mesh=mesh, in_specs=in_specs, out_specs=out_specs, check_vma=False
    )
```

profile of v0, /device:TPU:1, one launch (start us, length us, event | category | flops | bytes accessed | tf_op | source)
XLA Modules:
  0.0 1090.7 jit_solution(14421208025836142521)
XLA Ops:
  8.0 53.3 %psum.70 = f32[4]{0:T(128)S(1)} all-reduce(f32[4]{0:T(128)S(1)} %convert_reduce_fusion.1), channel_id=1, replica_groups=mesh['rep'=4,'blk'=32,'tp'=4] {'blk'}, use_global_device_ids=true, to_apply=%region_1.0 | all-reduce | flops 4 | bytes 32 | tf_op jit(solution)/shard_map/psum | solution.py:108
  61.3 0.9 fusion.97
  62.2 48.1 %psum.71 = f32[4]{0:T(128)S(1)} all-reduce(f32[4]{0:T(128)S(1)} %fusion.97), channel_id=1, replica_groups=mesh['rep'=4,'blk'=32,'tp'=4] {'blk'}, use_global_device_ids=true, to_apply=%region_3.0 | all-reduce | flops 4 | bytes 32 | tf_op jit(solution)/shard_map/psum | solution.py:110
  111.0 1.0 fusion.132
  112.3 1.2 fusion.20
  113.5 0.9 fusion.119
  114.5 87.2 %all-reduce.1 = (f32[4,3,8,64]{3,2,1,0:T(8,128)S(1)}, f32[4,2048]{1,0:T(4,128)S(1)}) all-reduce(f32[4,3,8,64]{3,2,1,0:T(8,128)S(1)} %reshape.328, f32[4,2048]{1,0:T(4,128)S(1)} %fusion.20), channel_id=1, replica_groups=mesh['rep'=4,'blk'=32,'tp'=4] {'blk'}, use_global_device_ids=true, to_apply=%region_4.0 | all-reduce | flops 14336 | bytes 114688 | tf_op jit(solution)/shard_map/psum | solution.py:120
  207.5 9.6 all-gather.6
  218.1 1.3 fusion.131
  221.7 0.9 fusion.47
  224.1 88.4 %all-gather.8 = f32[128,16,8]{1,2,0:T(8,128)S(1)} all-gather(f32[1,16,8]{1,2,0:T(8,128)S(1)} %convolution_bitcast_fusion.1), channel_id=3, replica_groups=mesh['rep'=4,'blk'=32,'tp'=4] {'rep','blk'}, dimensions={0}, use_global_device_ids=true | all-gather | bytes 66048 | tf_op jit(solution)/shard_map/all_gather | solution.py:18
  312.5 80.5 %all-gather.7 = f32[128,16,8]{1,2,0:T(8,128)S(1)} all-gather(f32[1,16,8]{1,2,0:T(8,128)S(1)} %bitcast.159), channel_id=2, replica_groups=mesh['rep'=4,'blk'=32,'tp'=4] {'rep','blk'}, dimensions={0}, use_global_device_ids=true | all-gather | bytes 66048 | tf_op jit(solution)/shard_map/all_gather | solution.py:18
  393.1 0.8 slice.231
  394.0 7.1 slice.234
  401.1 145.0 %while.28 = (s32[]{:T(128)}, f32[16,8]{0,1:T(8,128)S(1)}, f32[16,8]{0,1:T(8,128)S(1)}, f32[16,8,64]{2,1,0:T(8,128)S(1)}, f32[127,16,8]{1,2,0:T(8,128)S(1)}, /*in...) while((s32[]{:T(128)}, f32[16,8]{0,1:T(8,128)S(1)}, f32[16,8]{0,1:T(8,128)S(1)}, ...), condition=%wide.region_10.11_spmd, body=%wide.region_9.10_spmd.sunk | while | flops 25346 | bytes 171109 | solution.py:21
  401.3 0.9 constant_dynamic-slice_fusion.6
  546.6 1.1 convolution_add_fusion.1
  547.7 8.5 psum.74
  556.3 47.3 %psum.75 = f32[4]{0:T(128)S(1)} all-reduce(f32[4]{0:T(128)S(1)} %get-tuple-element.178), channel_id=1, replica_groups=mesh['rep'=4,'blk'=32,'tp'=4] {'blk'}, use_global_device_ids=true, to_apply=%region_14.15 | all-reduce | flops 4 | bytes 32 | tf_op jit(solution)/shard_map/psum | solution.py:108
  604.1 46.2 %psum.76 = f32[4]{0:T(128)S(1)} all-reduce(f32[4]{0:T(128)S(1)} %fusion.94), channel_id=1, replica_groups=mesh['rep'=4,'blk'=32,'tp'=4] {'blk'}, use_global_device_ids=true, to_apply=%region_16.17 | all-reduce | flops 4 | bytes 32 | tf_op jit(solution)/shard_map/psum | solution.py:110
  650.3 1.2 fusion.17
  651.5 1.1 fusion.122
  652.7 87.4 %all-reduce = (f32[4,3,8,64]{3,2,0,1:T(8,128)S(1)}, f32[4,2048]{1,0:T(4,128)S(1)}) all-reduce(f32[4,3,8,64]{3,2,0,1:T(8,128)S(1)} %copy.83, f32[4,2048]{1,0:T(4,128)S(1)} %fusion.17), channel_id=1, replica_groups=mesh['rep'=4,'blk'=32,'tp'=4] {'blk'}, use_global_device_ids=true, to_apply=%region_17.18 | all-reduce | flops 14336 | bytes 114688 | tf_op jit(solution)/shard_map/psum | solution.py:120
  741.0 9.0 all-gather.9
  752.2 0.9 fusion.46
  753.4 88.0 %all-gather.11 = f32[128,16,8]{1,2,0:T(8,128)S(1)} all-gather(f32[1,16,8]{1,2,0:T(8,128)S(1)} %convolution_bitcast_fusion), channel_id=6, replica_groups=mesh['rep'=4,'blk'=32,'tp'=4] {'rep','blk'}, dimensions={0}, use_global_device_ids=true | all-gather | bytes 66048 | tf_op jit(solution)/shard_map/all_gather | solution.py:18
  841.4 80.9 %all-gather.10 = f32[128,16,8]{1,2,0:T(8,128)S(1)} all-gather(f32[1,16,8]{1,2,0:T(8,128)S(1)} %bitcast.160), channel_id=5, replica_groups=mesh['rep'=4,'blk'=32,'tp'=4] {'rep','blk'}, dimensions={0}, use_global_device_ids=true | all-gather | bytes 66048 | tf_op jit(solution)/shard_map/all_gather | solution.py:18
  922.6 1.1 pad_maximum_fusion
  924.6 7.2 slice.251
  931.7 144.9 %while.29 = (s32[]{:T(128)}, f32[16,8]{0,1:T(8,128)S(1)}, f32[16,8]{0,1:T(8,128)S(1)}, f32[16,8,64]{2,1,0:T(8,128)S(1)}, f32[127,16,8]{1,2,0:T(8,128)S(1)}, /*in...) while((s32[]{:T(128)}, f32[16,8]{0,1:T(8,128)S(1)}, f32[16,8]{0,1:T(8,128)S(1)}, ...), condition=%wide.region_23.24_spmd, body=%wide.region_22.23_spmd.sunk | while | flops 25346 | bytes 171109 | solution.py:21
  931.9 0.8 constant_dynamic-slice_fusion.7
  1077.3 6.0 psum.79
  (1396 shorter events, 301.0 us)
Async XLA Ops:
  7.2 214.5 %copy-start.4 = (s32[8]{0:T(128)S(1)}, s32[8]{0:T(128)}, u32[]{:S(2)}) copy-start(s32[8]{0:T(128)} %param.23) | copy-start | bytes 100
  7.2 385.9 %all-gather.15.cloned.1.call-start = ((), (), s32[]{:S(2)}) async-start(), calls=%async_computation | async-start | bytes 8454144 | tf_op jit(solution)/shard_map/all_gather | solution.py:18
  222.7 701.0 %all-gather.17.cloned.1.call-start = ((), (), s32[]{:S(2)}) async-start(), calls=%async_computation.1 | async-start | bytes 8454144 | tf_op jit(solution)/shard_map/all_gather | solution.py:18
  394.0 152.5 %copy-start.1 = (bf16[2,512,64]{1,2,0:T(8,128)(2,1)S(1)}, bf16[2,512,64]{1,2,0:T(8,128)(2,1)}, u32[]{:S(2)}) copy-start(bf16[2,512,64]{1,2,0:T(8,128)(2,1)} %param.20) | copy-start | bytes 393220
  394.0 162.2 %copy-start.3 = (bf16[4,64]{1,0:T(4,128)(2,1)S(1)}, bf16[4,64]{1,0:T(4,128)(2,1)}, u32[]{:S(2)}) copy-start(bf16[4,64]{1,0:T(4,128)(2,1)} %param.16) | copy-start | bytes 1540
  401.1 521.2 %copy-start = (bf16[2,2,8,32,512]{4,3,2,1,0:T(8,128)(2,1)S(1)}, bf16[2,2,8,32,512]{4,3,2,1,0:T(8,128)(2,1)}, u32[]{:S(2)}) copy-start(bf16[2,2,8,32,512]{4,3,2,1,0:T(8,128)(2,1)} %param.22) | copy-start | bytes 3145732
  924.5 152.4 %copy-start.2 = (bf16[2,512,64]{1,2,0:T(8,128)(2,1)S(1)}, bf16[2,512,64]{1,2,0:T(8,128)(2,1)}, u32[]{:S(2)}) copy-start(bf16[2,512,64]{1,2,0:T(8,128)(2,1)} %param.20) | copy-start | bytes 393220
  924.5 152.5 %copy-start.5 = (bf16[2,2048,64]{1,2,0:T(8,128)(2,1)S(1)}, bf16[2,2048,64]{1,2,0:T(8,128)(2,1)}, u32[]{:S(2)}) copy-start(bf16[2,2048,64]{1,2,0:T(8,128)(2,1)} %param.21) | copy-start | bytes 1572868
Sparse Core Ops, SparseCore 0:
  222.8 149.7 all-gather.14
  753.3 146.6 all-gather.16
where the time goes:
time: 1100 us; the launch traced here: 1090 us
  blocking collectives  740 us (67%)
  local copies, waits for them, and re-layouts  275 us (25%)
  other arithmetic  43.7 us (4%)
  between operations  14.3 us (1%)
    all_gather x4, blocking collectives, combined_all(): pieces = jax.tree.map(lambda part: lax.all_gather(part, axis), value)  338 us
    dynamic_slice x254, local copies, waits for them, and re-layouts, combined_all(): lax.scan(lambda so_far, piece: (join(so_far, piece), None), head, tail)  215 us
    psum x2, blocking collectives, per_device(): qkv_full, inner = lax.psum((qkv_part, inner_part), 'blk')  175 us
    psum x2, blocking collectives, per_device(): average = lax.psum(jnp.sum(resid, axis=-1), 'blk') / D  101 us
    psum x2, blocking collectives, per_device(): variance = lax.psum(jnp.sum(centered * centered, axis=-1), 'blk') / D  94.3 us
    add x254, other arithmetic, merge_parts(): left_out * left_factor[..., None] + right_out * right_factor[..., None]  28.1 us
  transfers between devices with their start and end apart: 2, of which 0 were waited for; matrix products, arithmetic and copies ran while one was open for 0% of the time, Pallas kernels for 0%

commit v1 on v0

v1 whole, which is shorter than its diff:
```python
import jax
import jax.numpy as jnp
from jax import lax
from jax.sharding import PartitionSpec as P

D = 2048
HD = 64
ROT = 32
LAYERS = 2
PAGE = 32
EPSILON = 1e-05
LOWEST = -1e30
F32 = jnp.float32
BF16 = jnp.bfloat16


def exchange(value, axis, groups=None):
    return lax.all_to_all(value, axis, 0, 0, tiled=True, axis_index_groups=groups)


def spread(value, count, axis, groups=None):
    return exchange(jnp.broadcast_to(value[None], (count,) + value.shape), axis, groups)


def rope_tables(positions):
    lane = jnp.arange(128, dtype=jnp.int32) % HD
    steps_f = (lane % (ROT // 2)).astype(F32)
    inverse = 10000.0 ** (-2.0 * steps_f / ROT)
    angles = positions[:, None] * inverse[None, :]
    cosine = jnp.where(lane[None, :] < ROT, jnp.cos(angles), 1.0)
    sine = jnp.sin(angles)
    sine_up = jnp.where(lane[None, :] < ROT // 2, -sine, 0.0)
    sine_down = jnp.where((lane[None, :] >= ROT // 2) & (lane[None, :] < ROT), sine, 0.0)
    return cosine, sine_up, sine_down


def rotate(rows, tables):
    cosine, sine_up, sine_down = tables
    half = ROT // 2
    return (
        rows * cosine
        + jnp.roll(rows, -half, axis=-1) * sine_up
        + jnp.roll(rows, half, axis=-1) * sine_down
    )


def split_in_two(value):
    head = lax.reduce_precision(value, 8, 7)
    return head.astype(BF16), (value - head).astype(BF16)


def split_in_three(value):
    head = lax.reduce_precision(value, 8, 7)
    rest = value - head
    middle = lax.reduce_precision(rest, 8, 7)
    return head.astype(BF16), middle.astype(BF16), (rest - middle).astype(BF16)


def dot32(left, right):
    return jnp.dot(left, right, preferred_element_type=F32)


def merge(parts):
    high = parts[:, :, HD + 1 : HD + 2]
    top = jnp.max(high, axis=0)
    factor = jnp.exp(high - top[None])
    return jnp.sum(parts[:, :, : HD + 1] * factor, axis=0), top


def per_device(
    hidden,
    ln_gain,
    w_qkv,
    w_fc1,
    w_out,
    w_fc2,
    caches,
    page_owner,
    page_used,
    page_fill,
    page_tail,
    positions,
):
    rep = lax.axis_index("rep")
    blk = lax.axis_index("blk")
    zs = [[2 * z + c for z in range(16)] for c in range(2)]
    pairs = [[2 * z, 2 * z + 1] for z in range(16)]
    rep_core = [[r * 32 + 2 * z + c for r in range(4) for c in range(2)] for z in range(16)]

    offsets = jnp.arange(PAGE, dtype=jnp.int32)
    is_tail = page_tail == 1
    is_used = page_used == 1
    write_at = (offsets[None, :] == page_fill[:, None]) & is_tail[:, None]
    valid = is_used[:, None] & (offsets[None, :] < (page_fill + page_tail)[:, None])
    home_rows = page_owner - rep * 4
    pick_home = (
        (home_rows[:, None] == jnp.arange(4, dtype=jnp.int32)[None, :]) & is_tail[:, None]
    ).astype(BF16)
    pair_req = jnp.arange(128, dtype=jnp.int32) // 8
    allowed = (
        (pair_req[:, None, None] == page_owner[None, :, None]) & valid[None]
    ).reshape(128, 8 * PAGE)
    head_lane = (
        jnp.arange(512, dtype=jnp.int32)[None, :] // HD == jnp.arange(8, dtype=jnp.int32)[:, None]
    )

    first = jnp.concatenate(
        [
            hidden.astype(F32),
            jnp.broadcast_to(positions.astype(F32)[:, None], (4, 64)),
        ],
        axis=1,
    )
    first = spread(first, 4, "rep").reshape(16, 128)
    state = first[:, :64]
    all_pos = first[:, 64]
    q_rows = (blk % 8) * 2
    kv_row = rep * 4 + blk % 4
    fc_rows = rep * 4 + (blk % 2) * 2
    is_key = blk // 4 < 4
    rows_pos = jnp.concatenate(
        [
            lax.dynamic_slice_in_dim(all_pos, q_rows, 2),
            jnp.where(is_key, lax.dynamic_slice_in_dim(all_pos, kv_row, 1), 0.0),
        ]
    )
    tables = rope_tables(rows_pos)

    cache_list = []
    for layer in range(LAYERS):
        gain = ln_gain[layer][None, :]
        mean = jnp.mean(state, axis=1, keepdims=True)
        centered = state - mean
        square = jnp.sum(centered * centered, axis=1, keepdims=True)
        scaled_hi, scaled_lo = split_in_two(centered * gain)
        gain_parts = split_in_three(gain)
        rows = jnp.concatenate([scaled_hi, scaled_lo, *gain_parts], axis=0)
        own_hi = lax.dynamic_slice_in_dim(scaled_hi, rep * 4, 4)
        own_lo = lax.dynamic_slice_in_dim(scaled_lo, rep * 4, 4)
        own_mean = lax.dynamic_slice_in_dim(mean, rep * 4, 4)
        own_rows = jnp.concatenate([own_hi, own_lo, *gain_parts], axis=0)
        w_all = w_qkv[layer].reshape(64, 1536)
        q_prod = dot32(rows, w_all[:, :512])
        kv_prod = dot32(own_rows, w_all[:, 512:])
        fc_prod = dot32(own_rows, w_fc1[layer])
        q_col = jnp.sum(q_prod[32:], axis=0, keepdims=True)
        kv_col = jnp.sum(kv_prod[8:], axis=0, keepdims=True)
        fc_col = jnp.sum(fc_prod[8:], axis=0, keepdims=True)
        q_sum = q_prod[:16] + q_prod[16:32] + mean * q_col
        kv_sum = kv_prod[:4] + kv_prod[4:8] + own_mean * kv_col
        fc_sum = fc_prod[:4] + fc_prod[4:8] + own_mean * fc_col
        stats = jnp.concatenate([mean.reshape(1, 16), square.reshape(1, 16)], axis=1)
        send = jnp.concatenate(
            [
                q_sum.reshape(8, 2, 4, 128).transpose(2, 0, 1, 3).reshape(32, 256),
                kv_sum.reshape(4, 8, 128).transpose(1, 0, 2).reshape(32, 128),
                fc_sum.reshape(2, 2, 16, 128).transpose(2, 0, 1, 3).reshape(32, 256),
                jnp.repeat(q_col.reshape(4, 128), 8, axis=0),
                jnp.repeat(kv_col.reshape(8, 128), 4, axis=0),
                jnp.repeat(fc_col.reshape(16, 128), 2, axis=0),
                jnp.broadcast_to(jnp.pad(stats, ((0, 0), (0, 96))), (32, 128)),
            ],
            axis=1,
        )
        got = exchange(send, "blk")
        means = got[:, 1024:1040]
        squares = got[:, 1040:1056]
        average = jnp.mean(means, axis=0)
        variance = (
            jnp.sum(squares, axis=0) + 64.0 * jnp.sum((means - average[None]) ** 2, axis=0)
        ) / D
        rstd = lax.rsqrt(variance + EPSILON)
        total = jnp.sum(got[:, :1024], axis=0).reshape(8, 128)
        row_ids = jnp.concatenate(
            [q_rows + jnp.arange(2), kv_row[None], fc_rows + jnp.arange(2)]
        )
        pick = (row_ids[:, None] == jnp.arange(16)[None, :]).astype(F32)
        row_avg = jnp.sum(pick * average[None], axis=1, keepdims=True)
        row_rstd = jnp.sum(pick * rstd[None], axis=1, keepdims=True)
        columns = jnp.concatenate(
            [total[5:6], total[5:6], total[6:7], total[7:8], total[7:8]], axis=0
        )
        values = row_rstd * (total[:5] - row_avg * columns)
        turned = rotate(values[:3], tables)
        act = jax.nn.gelu(values[3:], approximate=True)
        packed = jnp.concatenate([turned, act], axis=0).astype(BF16).reshape(640)
        spread_out = spread(packed, 32, "blk")
        queries = (
            spread_out[:, :256].reshape(4, 8, 2, 128).transpose(1, 2, 0, 3).reshape(16, 512)
        )
        new_kv = spread_out[:, 256:384].reshape(8, 4, 128).transpose(1, 0, 2).reshape(4, 1024)
        mlp_act = (
            spread_out[:, 384:].reshape(16, 2, 2, 128).transpose(1, 2, 0, 3).reshape(4, 2048)
        )
        fresh = dot32(pick_home, new_kv).astype(BF16)
        key_pages = jnp.where(write_at[:, :, None], fresh[:, None, :512], caches[layer, 0])
        value_pages = jnp.where(write_at[:, :, None], fresh[:, None, 512:], caches[layer, 1])
        cache_list.append(jnp.stack([key_pages, value_pages]))
        wide = jnp.where(head_lane[None], queries[:, None, :], jnp.zeros((), BF16)).reshape(128, 512)
        scores = (
            lax.dot_general(
                wide,
                key_pages.reshape(256, 512),
                (((1,), (1,)), ((), ())),
                preferred_element_type=F32,
            )
            * HD ** (-0.5)
        )
        scores = jnp.where(allowed, scores, LOWEST)
        high = jnp.max(scores, axis=1, keepdims=True)
        weights = jnp.where(allowed, jnp.exp(scores - high), 0.0)
        sums = jnp.sum(weights, axis=1, keepdims=True)
        mixed = dot32(weights.astype(BF16), value_pages.reshape(256, 512))
        picked = jnp.sum(
            jnp.where(
                jnp.eye(8, dtype=bool)[None, :, :, None], mixed.reshape(16, 8, 8, 64), 0.0
            ),
            axis=2,
        ).reshape(128, 64)
        parts = jnp.concatenate([picked, sums, high, jnp.zeros((128, 62), F32)], axis=1)
        parts = exchange(parts.reshape(8, 16, 128), ("rep", "blk"), rep_core)
        sums_in, top = merge(parts)
        parts = jnp.concatenate([sums_in, top, jnp.zeros((16, 62), F32)], axis=1)
        parts = spread(parts, 16, "blk", zs)
        sums_in, _ = merge(parts)
        attended = (sums_in[:, :HD] / sums_in[:, HD:]).astype(BF16).reshape(2, 512)
        attended = lax.all_gather(attended, "blk", axis_index_groups=pairs, tiled=True)
        out_part = dot32(attended, w_out[layer]) + dot32(mlp_act, w_fc2[layer])
        if layer + 1 < LAYERS:
            everyone = spread(out_part.reshape(256), 16, ("rep", "tp")).reshape(4, 4, 4, 64)
            branch = jnp.sum(everyone, axis=1).reshape(16, 64)
            state = lax.reduce_precision(state + branch, 8, 7)
        else:
            branch = lax.psum(out_part, "tp")
            own = lax.dynamic_slice_in_dim(state, rep * 4, 4)
            result = (own + branch).astype(BF16)
    return (result, jnp.stack(cache_list))


def solution(mesh):
    in_specs = (
        P("rep", "blk"),
        P(None, "blk"),
        P(None, "blk", None, "tp"),
        P(None, "blk", "tp"),
        P(None, "tp", "blk"),
        P(None, "tp", "blk"),
        P(None, None, ("rep", "blk"), None, "tp"),
        P(("rep", "blk")),
        P(("rep", "blk")),
        P(("rep", "blk")),
        P(("rep", "blk")),
        P("rep"),
    )
    out_specs = (P("rep", "blk"), P(None, None, ("rep", "blk"), None, "tp"))
    return jax.shard_map(
        per_device, mesh=mesh, in_specs=in_specs, out_specs=out_specs, check_vma=False
    )
```

time: 1100 us -> 200 us (0.18)
  blocking collectives: 740 us -> 74.8 us
  local copies, waits for them, and re-layouts: 275 us -> 14.3 us
  waiting for transfers between devices: 0.05 us -> 56.1 us
  starting transfers between devices: 0.08 us -> 38.7 us
  other arithmetic: 43.7 us -> 10.1 us
  between operations: 14.3 us -> 2.16 us
    psum x8 -> x1, blocking collectives: 384 us -> 6.88 us  [per_device(): branch = lax.psum(out_part, 'tp')]
    all_gather x6 -> x2, blocking collectives: 356 us -> 9.88 us  [per_device(): lax.all_gather(attended, 'blk', axis_index_groups=pairs, tiled=True)]
    dynamic_slice x258 -> x5, local copies, waits for them, and re-layouts: 215 us -> 0.67 us  [the longest x1 0.52 us: per_device(): lax.dynamic_slice_in_dim(all_pos, kv_row, 1)]
    all_to_all x0 -> x4, blocking collectives: none -> 58.1 us  [exchange(): lax.all_to_all(value, axis, 0, 0, tiled=True, axis_index_groups=groups)]
    all_to_all x0 -> x6, waiting for transfers between devices: none -> 56.1 us  [exchange(): lax.all_to_all(value, axis, 0, 0, tiled=True, axis_index_groups=groups)]
    all_to_all x0 -> x6, starting transfers between devices: none -> 38.7 us  [exchange(): lax.all_to_all(value, axis, 0, 0, tiled=True, axis_index_groups=groups)]
    exp x508 -> x0, local copies, waits for them, and re-layouts: 36.4 us -> none  [the longest x254 18.3 us: merge_parts(): right_factor = jnp.exp(right_high - joined)]
    add x508 -> x7, other arithmetic: 32.2 us -> 0.46 us  [the longest x2 0.15 us: per_device(): fc_sum = fc_prod[:4] + fc_prod[4:8] + own_mean * fc_col]
  transfers between devices with their start and end apart: 2 -> 6, of which waited for: 0 -> 5; matrix products, arithmetic and copies ran while one was open for 0% -> 2% of each run, Pallas kernels for 0% -> 0%
where the time goes in v1:
time: 200 us; the launch traced here: 199 us
  blocking collectives  74.8 us (37%)
  waiting for transfers between devices  56.1 us (28%)
  starting transfers between devices  38.7 us (19%)
  local copies, waits for them, and re-layouts  14.3 us (7%)
  other arithmetic  10.1 us (5%)
  matrix products  3.04 us (2%)
  between operations  2.16 us (1%)
    all_to_all x4, blocking collectives, exchange(): lax.all_to_all(value, axis, 0, 0, tiled=True, axis_index_groups=groups)  58.1 us
    all_to_all x6, waiting for transfers between devices, exchange(): lax.all_to_all(value, axis, 0, 0, tiled=True, axis_index_groups=groups)  56.1 us
    all_to_all x6, starting transfers between devices, exchange(): lax.all_to_all(value, axis, 0, 0, tiled=True, axis_index_groups=groups)  38.7 us
    all_gather x2, blocking collectives, per_device(): lax.all_gather(attended, 'blk', axis_index_groups=pairs, tiled=True)  9.88 us
    psum x1, blocking collectives, per_device(): branch = lax.psum(out_part, 'tp')  6.88 us
    unnamed x52, local copies, waits for them, and re-layouts  4.61 us
  transfers between devices with their start and end apart: 6, of which 5 were waited for; matrix products, arithmetic and copies ran while one was open for 2% of the time, Pallas kernels for 0%

profile of v1, /device:TPU:1, one launch (start us, length us, event | category | flops | bytes accessed | tf_op | source)
XLA Modules:
  0.0 199.2 jit_solution(9043583412041458383)
XLA Ops:
  0.6 0.7 convert_element_type.87
  1.5 0.6 broadcast_in_dim.286
  2.1 5.0 %all-to-all-start = ((f32[4,4,128]{2,1,0:T(4,128)}), f32[4,4,128]{2,1,0:T(4,128)S(1)}, u32[]{:S(2)}, u32[]{:S(2)}) async-start(f32[4,4,128]{2,1,0:T(4,128)} %broadcast_in_dim.286), calls=%async_computation | async-start | bytes 16384 | tf_op jit(solution)/shard_map/all_to_all | solution.py:18
  7.2 0.6 copy-done.9
  7.8 0.6 copy-done.8
  9.9 0.6 copy-done.6
  10.5 1.1 fusion.126
  13.5 0.8 copy.136
  14.3 16.6 %all-to-all-start.1 = ((f32[32,1,1152]{2,1,0:T(1,128)}), f32[32,1,1152]{2,1,0:T(1,128)S(1)}, u32[]{:S(2)}, u32[]{:S(2)}) async-start(f32[32,1,1152]{2,1,0:T(1,128)} %copy.136), calls=%async_computation.1 | async-start | bytes 294912 | tf_op jit(solution)/shard_map/all_to_all | solution.py:18
  32.5 14.9 %all-to-all-done.1 = f32[32,1,1152]{2,1,0:T(1,128)S(1)} async-done(((f32[32,1,1152]{2,1,0:T(1,128)}), f32[32,1,1152]{2,1,0:T(1,128)S(1)}, u32[]{:S(2)}, u32[]{:S(2)}) %all-to-all-start.1) | async-done | bytes 147488 | tf_op jit(solution)/shard_map/all_to_all | solution.py:18
  48.8 0.9 reduce.15
  49.6 0.7 reshape.737
  50.4 5.2 %all-to-all-start.2 = ((bf16[32,2,320]{2,1,0:T(2,128)(2,1)}), bf16[32,2,320]{2,1,0:T(2,128)(2,1)S(1)}, u32[]{:S(2)}, u32[]{:S(2)}) async-start(bf16[32,2,320]{2,1,0:T(2,128)(2,1)} %reshape.737), calls=%async_computation.2 | async-start | bytes 98304 | tf_op jit(solution)/shard_map/all_to_all | solution.py:18
  55.8 12.5 %all-to-all-done.2 = bf16[32,2,320]{2,1,0:T(2,128)(2,1)S(1)} async-done(((bf16[32,2,320]{2,1,0:T(2,128)(2,1)}), bf16[32,2,320]{2,1,0:T(2,128)(2,1)S(1)}, u32[]{:S(2)}, u32[]{:S(2)}) %all-to-all-start.2) | async-done | bytes 40992 | tf_op jit(solution)/shard_map/all_to_all | solution.py:18
  70.4 10.5 %all_to_all.73 = f32[8,16,128]{2,1,0:T(8,128)S(1)} all-to-all(f32[8,16,128]{2,1,0:T(8,128)S(1)} %maximum_maximum_fusion), channel_id=1, replica_groups={{0,4,128,132,256,260,384,388},{8,12,136,140,264,268,392,396},{16,20,144..., dimensions={0} | all-to-all | bytes 131072 | tf_op jit(solution)/shard_map/all_to_all | solution.py:18
  81.5 0.7 broadcast_in_dim.312
  82.1 3.6 %all-to-all-start.4 = ((f32[16,16,128]{2,1,0:T(8,128)}), f32[16,16,128]{2,1,0:T(8,128)S(1)}, u32[]{:S(2)}, u32[]{:S(2)}) async-start(f32[16,16,128]{2,1,0:T(8,128)} %broadcast_in_dim.312), calls=%async_computation.4 | async-start | bytes 262144 | tf_op jit(solution)/shard_map/all_to_all | solution.py:18
  85.8 11.9 %all-to-all-done.4 = f32[16,16,128]{2,1,0:T(8,128)S(1)} async-done(((f32[16,16,128]{2,1,0:T(8,128)}), f32[16,16,128]{2,1,0:T(8,128)S(1)}, u32[]{:S(2)}, u32[]{:S(2)}) %all-to-all-start.4) | async-done | bytes 131104 | tf_op jit(solution)/shard_map/all_to_all | solution.py:18
  98.6 4.9 %all-gather = bf16[2,2,512]{2,1,0:T(2,128)(2,1)S(1)} all-gather(bf16[1,2,512]{2,1,0:T(2,128)(2,1)S(1)} %reshape.716), channel_id=1, replica_groups={{0,4},{8,12},{16,20},{24,28},{32,36},{40,44},{48,52},{56,60},{64,68},{7..., dimensions={0}, use_global_device_ids=true | all-gather | bytes 6144 | tf_op jit(solution)/shard_map/all_gather | solution.py:227
  103.9 0.6 broadcast_in_dim.314
  104.5 4.7 %all-to-all-start.5 = ((f32[16,1,256]{2,1,0:T(1,128)}), f32[16,1,256]{2,1,0:T(1,128)S(1)}, u32[]{:S(2)}, u32[]{:S(2)}) async-start(f32[16,1,256]{2,1,0:T(1,128)} %broadcast_in_dim.314), calls=%async_computation.5 | async-start | bytes 32768 | tf_op jit(solution)/shard_map/all_to_all | solution.py:18
  109.5 6.2 %all-to-all-done.5 = f32[16,1,256]{2,1,0:T(1,128)S(1)} async-done(((f32[16,1,256]{2,1,0:T(1,128)}), f32[16,1,256]{2,1,0:T(1,128)S(1)}, u32[]{:S(2)}, u32[]{:S(2)}) %all-to-all-start.5) | async-done | bytes 16416 | tf_op jit(solution)/shard_map/all_to_all | solution.py:18
  117.5 22.1 %all_to_all.74 = f32[32,1,1152]{2,1,0:T(1,128)S(1)} all-to-all(f32[32,1,1152]{2,1,0:T(1,128)S(1)} %copy.149), channel_id=1, replica_groups=mesh['rep'=4,'blk'=32,'tp'=4] {'blk'}, dimensions={0} | all-to-all | bytes 294912 | tf_op jit(solution)/shard_map/all_to_all | solution.py:18
  140.3 0.9 reduce.16
  141.3 17.0 %all_to_all.75 = bf16[32,2,320]{2,1,0:T(2,128)(2,1)S(1)} all-to-all(bf16[32,2,320]{2,1,0:T(2,128)(2,1)S(1)} %reshape.739), channel_id=1, replica_groups=mesh['rep'=4,'blk'=32,'tp'=4] {'blk'}, dimensions={0} | all-to-all | bytes 81920 | tf_op jit(solution)/shard_map/all_to_all | solution.py:18
  160.4 8.5 %all_to_all.76 = f32[8,16,128]{2,1,0:T(8,128)S(1)} all-to-all(f32[8,16,128]{2,1,0:T(8,128)S(1)} %maximum_maximum_fusion.1), channel_id=1, replica_groups={{0,4,128,132,256,260,384,388},{8,12,136,140,264,268,392,396},{16,20,144..., dimensions={0} | all-to-all | bytes 131072 | tf_op jit(solution)/shard_map/all_to_all | solution.py:18
  169.6 0.7 broadcast_in_dim.326
  170.2 3.5 %all-to-all-start.9 = ((f32[16,16,128]{2,1,0:T(8,128)}), f32[16,16,128]{2,1,0:T(8,128)S(1)}, u32[]{:S(2)}, u32[]{:S(2)}) async-start(f32[16,16,128]{2,1,0:T(8,128)} %broadcast_in_dim.326), calls=%async_computation.9 | async-start | bytes 262144 | tf_op jit(solution)/shard_map/all_to_all | solution.py:18
  174.1 1.1 pad_maximum_fusion
  175.1 10.6 %all-to-all-done.9 = f32[16,16,128]{2,1,0:T(8,128)S(1)} async-done(((f32[16,16,128]{2,1,0:T(8,128)}), f32[16,16,128]{2,1,0:T(8,128)S(1)}, u32[]{:S(2)}, u32[]{:S(2)}) %all-to-all-start.9) | async-done | bytes 131104 | tf_op jit(solution)/shard_map/all_to_all | solution.py:18
  186.5 4.9 %all-gather.1 = bf16[2,2,512]{2,1,0:T(2,128)(2,1)S(1)} all-gather(bf16[1,2,512]{2,1,0:T(2,128)(2,1)S(1)} %reshape.718), channel_id=1, replica_groups={{0,4},{8,12},{16,20},{24,28},{32,36},{40,44},{48,52},{56,60},{64,68},{7..., dimensions={0}, use_global_device_ids=true | all-gather | bytes 6144 | tf_op jit(solution)/shard_map/all_gather | solution.py:227
  191.8 6.9 %psum.7 = f32[4,64]{1,0:T(4,128)S(1)} all-reduce(f32[4,64]{1,0:T(4,128)S(1)} %convolution_add_fusion), channel_id=1, replica_groups=mesh['rep'=4,'blk'=32,'tp'=4] {'tp'}, use_global_device_ids=true, to_apply=%region_37.38 | all-reduce | flops 256 | bytes 2048 | tf_op jit(solution)/shard_map/psum | solution.py:234
  (227 shorter events, 17.0 us)
Async XLA Ops:
  0.6 0.7 copy-start.5
  2.1 9.8 %all-to-all-start = ((f32[4,4,128]{2,1,0:T(4,128)}), f32[4,4,128]{2,1,0:T(4,128)S(1)}, u32[]{:S(2)}, u32[]{:S(2)}) async-start(f32[4,4,128]{2,1,0:T(4,128)} %broadcast_in_dim.286), calls=%async_computation | async-start | bytes 16384 | tf_op jit(solution)/shard_map/all_to_all | solution.py:18
  7.2 0.7 copy-start.9
  7.8 0.7 copy-start.8
  8.6 0.7 copy-start.4
  9.8 0.7 copy-start.6
  11.6 1.0 copy-start.1
  12.4 18.7 %copy-start = (bf16[2,2,8,32,512]{4,3,2,1,0:T(8,128)(2,1)S(1)}, bf16[2,2,8,32,512]{4,3,2,1,0:T(8,128)(2,1)}, u32[]{:S(2)}) copy-start(bf16[2,2,8,32,512]{4,3,2,1,0:T(8,128)(2,1)} %param.18) | copy-start | bytes 3145732
  14.3 16.6 %copy-start.7 = (s32[8]{0:T(128)S(1)}, s32[8]{0:T(128)}, u32[]{:S(2)}) copy-start(s32[8]{0:T(128)} %param.19) | copy-start | bytes 100
  14.3 33.1 %all-to-all-start.1 = ((f32[32,1,1152]{2,1,0:T(1,128)}), f32[32,1,1152]{2,1,0:T(1,128)S(1)}, u32[]{:S(2)}, u32[]{:S(2)}) async-start(f32[32,1,1152]{2,1,0:T(1,128)} %copy.136), calls=%async_computation.1 | async-start | bytes 294912 | tf_op jit(solution)/shard_map/all_to_all | solution.py:18
  50.4 17.9 %all-to-all-start.2 = ((bf16[32,2,320]{2,1,0:T(2,128)(2,1)}), bf16[32,2,320]{2,1,0:T(2,128)(2,1)S(1)}, u32[]{:S(2)}, u32[]{:S(2)}) async-start(bf16[32,2,320]{2,1,0:T(2,128)(2,1)} %reshape.737), calls=%async_computation.2 | async-start | bytes 98304 | tf_op jit(solution)/shard_map/all_to_all | solution.py:18
  82.1 21.5 %copy-start.2 = (bf16[2,2048,64]{1,2,0:T(8,128)(2,1)S(1)}, bf16[2,2048,64]{1,2,0:T(8,128)(2,1)}, u32[]{:S(2)}) copy-start(bf16[2,2048,64]{1,2,0:T(8,128)(2,1)} %param.17) | copy-start | bytes 1572868
  82.1 15.6 %all-to-all-start.4 = ((f32[16,16,128]{2,1,0:T(8,128)}), f32[16,16,128]{2,1,0:T(8,128)S(1)}, u32[]{:S(2)}, u32[]{:S(2)}) async-start(f32[16,16,128]{2,1,0:T(8,128)} %broadcast_in_dim.312), calls=%async_computation.4 | async-start | bytes 262144 | tf_op jit(solution)/shard_map/all_to_all | solution.py:18
  98.1 5.4 %copy-start.3 = (bf16[2,512,64]{1,2,0:T(8,128)(2,1)S(1)}, bf16[2,512,64]{1,2,0:T(8,128)(2,1)}, u32[]{:S(2)}) copy-start(bf16[2,512,64]{1,2,0:T(8,128)(2,1)} %param.16) | copy-start | bytes 393220
  104.5 11.2 %all-to-all-start.5 = ((f32[16,1,256]{2,1,0:T(1,128)}), f32[16,1,256]{2,1,0:T(1,128)S(1)}, u32[]{:S(2)}, u32[]{:S(2)}) async-start(f32[16,1,256]{2,1,0:T(1,128)} %broadcast_in_dim.314), calls=%async_computation.5 | async-start | bytes 32768 | tf_op jit(solution)/shard_map/all_to_all | solution.py:18
  170.2 15.5 %all-to-all-start.9 = ((f32[16,16,128]{2,1,0:T(8,128)}), f32[16,16,128]{2,1,0:T(8,128)S(1)}, u32[]{:S(2)}, u32[]{:S(2)}) async-start(f32[16,16,128]{2,1,0:T(8,128)} %broadcast_in_dim.326), calls=%async_computation.9 | async-start | bytes 262144 | tf_op jit(solution)/shard_map/all_to_all | solution.py:18

commit v2 on v1

v2 whole, which is shorter than its diff:
```python
import functools
import math

import jax
import jax.numpy as jnp
from jax import lax
from jax.experimental import pallas as pl
from jax.experimental.pallas import tpu as pltpu
from jax.sharding import PartitionSpec as P

D = 2048
HD = 64
ROT = 32
LAYERS = 2
PAGE = 32
EPSILON = 1e-05
LOWEST = -1e30
F32 = jnp.float32
BF16 = jnp.bfloat16
INTERPRET = False
WIRE = 10
BACK = 6


def exchange(value, axis, groups=None):
    return lax.all_to_all(value, axis, 0, 0, tiled=True, axis_index_groups=groups)


def spread(value, count, axis, groups=None):
    return exchange(jnp.broadcast_to(value[None], (count,) + value.shape), axis, groups)


def rope_tables(positions):
    lane = jnp.arange(128, dtype=jnp.int32) % HD
    steps_f = (lane % (ROT // 2)).astype(F32)
    inverse = 10000.0 ** (-2.0 * steps_f / ROT)
    angles = positions[:, None] * inverse[None, :]
    cosine = jnp.where(lane[None, :] < ROT, jnp.cos(angles), 1.0)
    sine = jnp.sin(angles)
    sine_up = jnp.where(lane[None, :] < ROT // 2, -sine, 0.0)
    sine_down = jnp.where((lane[None, :] >= ROT // 2) & (lane[None, :] < ROT), sine, 0.0)
    return jnp.concatenate([cosine, sine_up, sine_down], axis=0)


def iota(shape, axis):
    return lax.broadcasted_iota(jnp.int32, shape, axis)


def dot32(left, right):
    return jnp.dot(left, right, preferred_element_type=F32)


def parts_of(value, count):
    found = []
    for _ in range(count):
        part = value.astype(BF16).astype(F32)
        found.append(part)
        value = value - part
    return found


def project_kernel(with_branch, rep_ref, *refs):
    if with_branch:
        x_ref, gain_ref, wq_ref, wf_ref, branch_ref, send_ref, state_ref, wire = refs
        sums = []
        for rep in range(4):
            total = branch_ref[rep * 16 : rep * 16 + 4, :HD]
            for tp in range(1, 4):
                start = rep * 16 + tp * 4
                total = total + branch_ref[start : start + 4, :HD]
            sums.append(total)
        x = (x_ref[:, :HD] + jnp.concatenate(sums, axis=0)).astype(BF16).astype(F32)
    else:
        x_ref, gain_ref, wq_ref, wf_ref, send_ref, state_ref, wire = refs
        x = x_ref[:, :HD]
    state_ref[...] = jnp.concatenate([x, jnp.zeros_like(x)], axis=1)
    gain = gain_ref[...]
    mean = jnp.sum(x, axis=1, keepdims=True) * (1.0 / HD)
    centered = x - mean
    square = jnp.sum(centered * centered, axis=1, keepdims=True)
    scaled = centered * gain
    row = iota((48, 24), 0)
    col = iota((48, 24), 1)
    own = rep_ref[0] * 4
    within = row % 8
    want = jnp.where(
        row < 8,
        2 * within,
        jnp.where(
            row < 16,
            2 * within + 1,
            jnp.where(
                row < 24,
                own + within % 4,
                jnp.where(
                    row < 32,
                    own + 2 * (within % 2),
                    jnp.where(row < 40, own + 2 * (within % 2) + 1, 16),
                ),
            ),
        ),
    )
    choose = (col == want).astype(BF16)
    rows = jnp.concatenate([scaled, jnp.broadcast_to(gain, (8, HD))], axis=0)
    high, low = parts_of(rows, 2)
    left_high = dot32(choose, high.astype(BF16)).astype(BF16)
    left_low = dot32(choose, low.astype(BF16)).astype(BF16)

    def product(first, last, weights):
        return dot32(left_high[first:last], weights) + dot32(left_low[first:last], weights)

    wq = wq_ref[...]
    wf = wf_ref[0]
    every_q = product(0, 48, wq[:, :512])
    every_kv = product(16, 48, wq[:, 512:])
    every_fc = product(24, 48, wf)
    sub = iota((8, 128), 0)

    def stack_q(block):
        return jnp.concatenate([block[:, 128 * j : 128 * j + 128] for j in range(4)], axis=0)

    def stack_kv(block):
        return jnp.concatenate(
            [
                jnp.where(
                    sub < 4,
                    block[:, 256 * j : 256 * j + 128],
                    block[:, 256 * j + 128 : 256 * j + 256],
                )
                for j in range(4)
            ],
            axis=0,
        )

    def stack_fc(block):
        tiles = []
        for j in range(4):
            tile = block[:, 512 * j : 512 * j + 128]
            for k in range(1, 4):
                start = 512 * j + 128 * k
                tile = jnp.where(sub // 2 == k, block[:, start : start + 128], tile)
            tiles.append(tile)
        return jnp.concatenate(tiles, axis=0)

    lane = iota((16, 128), 1)
    request = iota((16, 128), 0)
    stats = jnp.zeros((16, 128), F32)
    for k, part in enumerate(parts_of(mean, 3) + parts_of(square, 3)):
        stats = jnp.where(lane == request + 16 * k, part, stats)
    stats = jnp.sum(stats, axis=0, keepdims=True)
    pieces = [
        stack_q(every_q[0:8]),
        stack_q(every_q[8:16]),
        stack_kv(every_kv[0:8]),
        stack_fc(every_fc[0:8]),
        stack_fc(every_fc[8:16]),
        stack_q(every_q[40:48]),
        stack_kv(every_kv[24:32]),
        stack_fc(every_fc[16:24]),
        jnp.broadcast_to(stats, (32, 128)),
        jnp.zeros((32, 128), F32),
    ]
    for k, piece in enumerate(pieces):
        wire[pl.ds(k, 32, stride=WIRE), :] = piece
    send_ref[...] = wire[...].astype(BF16)


def project(layer, rep, x, gain, wq, wf, branch=None):
    args = [rep, x, gain, wq, wf] + ([] if branch is None else [branch])
    full = lambda shape: pl.BlockSpec(shape, lambda i: (0,) * len(shape))
    specs = [
        pl.BlockSpec(memory_space=pltpu.SMEM),
        full((16, 128)),
        full((1, HD)),
        full((HD, 1536)),
        pl.BlockSpec((1, HD, D), lambda i: (layer, 0, 0)),
    ] + ([] if branch is None else [full((64, 128))])
    return pl.pallas_call(
        functools.partial(project_kernel, branch is not None),
        grid=(1,),
        in_specs=specs,
        out_specs=(full((32 * WIRE, 128)), full((16, 128))),
        out_shape=(
            jax.ShapeDtypeStruct((32 * WIRE, 128), BF16),
            jax.ShapeDtypeStruct((16, 128), F32),
        ),
        scratch_shapes=[pltpu.VMEM((32 * WIRE, 128), F32)],
        name="project",
        interpret=INTERPRET,
    )(*args)


def finish_kernel(rows_ref, got_ref, table_ref, out_ref, wire, back):
    wire[...] = got_ref[...].astype(F32)
    take = lambda k: wire[pl.ds(k, 32, stride=WIRE), :]
    stats = take(8)
    stats = stats + pltpu.roll(stats, 112, 1) + pltpu.roll(stats, 96, 1)
    average = jnp.sum(stats, axis=0, keepdims=True) * (1.0 / 32)
    offset = stats - average
    spread_sum = 64.0 * jnp.sum(offset * offset, axis=0, keepdims=True)
    square_sum = pltpu.roll(jnp.sum(stats, axis=0, keepdims=True), 80, 1)
    rstd = lax.rsqrt((square_sum + spread_sum) * (1.0 / D) + EPSILON)
    lane = iota((32, 128), 1)
    lane_one = iota((1, 128), 1)
    columns = [take(5), take(6), take(7)]
    half = ROT // 2
    for k, column in enumerate((0, 0, 1, 2, 2)):
        request = rows_ref[k]
        row_offset = jnp.sum(jnp.where(lane == request, offset, 0.0), axis=1, keepdims=True)
        row_rstd = jnp.sum(jnp.where(lane_one == request, rstd, 0.0), axis=1, keepdims=True)
        value = row_rstd * jnp.sum(take(k) + row_offset * columns[column], axis=0, keepdims=True)
        if k < 3:
            value = (
                value * table_ref[k : k + 1]
                + pltpu.roll(value, 128 - half, 1) * table_ref[3 + k : 4 + k]
                + pltpu.roll(value, half, 1) * table_ref[6 + k : 7 + k]
            )
        else:
            cubed = value * value * value
            value = (
                0.5 * value * (1.0 + jnp.tanh(math.sqrt(2.0 / math.pi) * (value + 0.044715 * cubed)))
            )
        back[pl.ds(k, 32, stride=BACK), :] = jnp.broadcast_to(value, (32, 128))
    back[pl.ds(5, 32, stride=BACK), :] = jnp.zeros((32, 128), F32)
    out_ref[...] = back[...].astype(BF16)


def finish(rows, got, table):
    return pl.pallas_call(
        finish_kernel,
        in_specs=[
            pl.BlockSpec(memory_space=pltpu.SMEM),
            pl.BlockSpec(memory_space=pltpu.VMEM),
            pl.BlockSpec(memory_space=pltpu.VMEM),
        ],
        out_specs=pl.BlockSpec(memory_space=pltpu.VMEM),
        out_shape=jax.ShapeDtypeStruct((32 * BACK, 128), BF16),
        scratch_shapes=[
            pltpu.VMEM((32 * WIRE, 128), F32),
            pltpu.VMEM((32 * BACK, 128), F32),
        ],
        name="finish",
        interpret=INTERPRET,
    )(rows, got, table)


def attend_kernel(aliased, meta_ref, got_ref, cache_ref, *refs):
    if aliased:
        _, pages_ref, out_ref, back, kv = refs
    else:
        pages_ref, out_ref, back, kv = refs
    back[...] = got_ref[...].astype(F32)
    take = lambda k: back[pl.ds(k, 32, stride=BACK), :]
    new = take(2)
    for j in range(4):
        for part in range(2):
            chunk = 2 * j + part
            kv[chunk // 4, :, 128 * (chunk % 4) : 128 * (chunk % 4) + 128] = new[
                8 * j + 4 * part : 8 * j + 4 * part + 4
            ]
    spot = iota((PAGE, 512), 0)
    for side in range(2):
        for page in range(8):
            home = jnp.clip(meta_ref[0, page] - meta_ref[4, 0], 0, 3)
            place = jnp.where(meta_ref[3, page] == 1, meta_ref[2, page], -1)
            fresh = kv[side, pl.ds(home, 1), :]
            old = cache_ref[0, side, page].astype(F32)
            pages_ref[0, side, page] = jnp.where(spot == place, fresh, old).astype(BF16)
    head_of = iota((8, 512), 1) // HD == iota((8, 512), 0)
    sides = []
    for k in range(2):
        tall = take(k)
        sides.append(jnp.concatenate([tall[8 * j : 8 * j + 8] for j in range(4)], axis=1))
    wide = jnp.concatenate(
        [
            jnp.where(head_of, jnp.broadcast_to(sides[k][p : p + 1], (8, 512)), 0.0)
            for p in range(8)
            for k in range(2)
        ],
        axis=0,
    ).astype(BF16)
    keys = pages_ref[0, 0].reshape(8 * PAGE, 512)
    values = pages_ref[0, 1].reshape(8 * PAGE, 512)
    scores = (
        lax.dot_general(wide, keys, (((1,), (1,)), ((), ())), preferred_element_type=F32)
        * HD ** (-0.5)
    )
    page_of = iota((1, 256), 1) // PAGE
    owner = jnp.zeros((1, 256), jnp.int32)
    limit = jnp.zeros((1, 256), jnp.int32)
    for page in range(8):
        length = jnp.where(meta_ref[1, page] == 1, meta_ref[2, page] + meta_ref[3, page], 0)
        owner = jnp.where(page_of == page, meta_ref[0, page], owner)
        limit = jnp.where(page_of == page, length, limit)
    owner = jnp.where(iota((1, 256), 1) % PAGE < limit, owner, -1)
    allowed = iota((128, 256), 0) // 8 == owner
    scores = jnp.where(allowed, scores, LOWEST)
    high = jnp.max(scores, axis=1, keepdims=True)
    weights = jnp.where(allowed, jnp.exp(scores - high), 0.0)
    total = jnp.sum(weights, axis=1, keepdims=True)
    mixed = dot32(weights.astype(BF16), values)
    head = iota((128, 128), 0) % 8
    lane = iota((128, 128), 1)
    picked = mixed[:, :128]
    for k in range(1, 4):
        picked = jnp.where(head // 2 == k, mixed[:, 128 * k : 128 * k + 128], picked)
    picked = jnp.where(head % 2 == 1, pltpu.roll(picked, HD, 1), picked)
    out_ref[...] = jnp.where(
        lane < HD, picked, jnp.where(lane == HD, total, jnp.where(lane == HD + 1, high, 0.0))
    )


def attend(layer, meta, got, caches, pages=None):
    block = pl.BlockSpec((1, 2, 8, PAGE, 512), lambda i: (layer, 0, 0, 0, 0))
    whole = lambda shape: pl.BlockSpec(shape, lambda i: (0,) * len(shape))
    specs = [pl.BlockSpec(memory_space=pltpu.SMEM), whole((32 * BACK, 128)), block]
    args = [meta, got, caches]
    aliases = {}
    if pages is not None:
        specs.append(pl.BlockSpec(memory_space=pl.ANY))
        args.append(pages)
        aliases = {3: 0}
    return pl.pallas_call(
        functools.partial(attend_kernel, pages is not None),
        grid=(1,),
        in_specs=specs,
        out_specs=(block, whole((128, 128))),
        out_shape=(
            jax.ShapeDtypeStruct(caches.shape, BF16),
            jax.ShapeDtypeStruct((128, 128), F32),
        ),
        scratch_shapes=[pltpu.VMEM((32 * BACK, 128), F32), pltpu.VMEM((2, 4, 512), F32)],
        input_output_aliases=aliases,
        name="attend",
        interpret=INTERPRET,
    )(*args)


def join_kernel(got_ref, out_ref):
    got = got_ref[...]
    high = got[:, :, HD + 1 : HD + 2]
    top = jnp.max(high, axis=0)
    total = jnp.sum(got * jnp.exp(high - top[None]), axis=0)
    lane = iota((16, 128), 1)
    out = jnp.where(lane < HD, total, 0.0)
    extra = parts_of(total[:, HD : HD + 1], 3) + parts_of(top, 3)
    for k, part in enumerate(extra):
        out = jnp.where(lane == HD + k, part, out)
    out_ref[...] = jnp.broadcast_to(out.astype(BF16)[None], (16, 16, 128))


def join(got):
    return pl.pallas_call(
        join_kernel,
        out_shape=jax.ShapeDtypeStruct((16, 16, 128), BF16),
        name="join",
        interpret=INTERPRET,
    )(got)


def settle_kernel(got_ref, out_ref):
    got = got_ref[...].astype(F32)
    sums = got[:, :, HD : HD + 1] + got[:, :, HD + 1 : HD + 2] + got[:, :, HD + 2 : HD + 3]
    high = got[:, :, HD + 3 : HD + 4] + got[:, :, HD + 4 : HD + 5] + got[:, :, HD + 5 : HD + 6]
    factor = jnp.exp(high - jnp.max(high, axis=0)[None])
    total = jnp.sum(sums * factor, axis=0)
    mixed = jnp.sum(got * factor, axis=0)
    out_ref[...] = jnp.where(iota((16, 128), 1) < HD, mixed / total, 0.0).astype(BF16)


def settle(got):
    return pl.pallas_call(
        settle_kernel,
        out_shape=jax.ShapeDtypeStruct((16, 128), BF16),
        name="settle",
        interpret=INTERPRET,
    )(got)


def output_kernel(copies, att_ref, got_ref, wo_ref, wf_ref, out_ref, back):
    back[...] = got_ref[...].astype(F32)
    att = att_ref[...].astype(F32)
    att = att + pltpu.roll(att, HD, 1)
    att = jnp.concatenate([att] * 4, axis=1)
    own = iota((32, 512), 1) // HD == iota((32, 512), 0) % 8
    by_head = dot32(jnp.where(own, att, 0.0).astype(BF16), wo_ref[0])
    chunk = iota((32, D), 1) // 128 == iota((32, D), 0) // 2
    mlp = []
    for k in range(2):
        act = back[pl.ds(3 + k, 32, stride=BACK), :]
        act = jnp.concatenate([act] * 16, axis=1)
        mlp.append(dot32(jnp.where(chunk, act, 0.0).astype(BF16), wf_ref[0]))
    odd = iota((32, HD), 0) % 2
    rows = []
    for i in range(4):
        from_mlp = jnp.sum(jnp.where(odd == i // 2, mlp[i % 2], 0.0), axis=0, keepdims=True)
        from_att = jnp.sum(by_head[8 * i : 8 * i + 8], axis=0, keepdims=True)
        rows.append(from_att + from_mlp)
    tile = jnp.concatenate(rows, axis=0)
    tile = jnp.concatenate([tile, jnp.zeros_like(tile)], axis=1)
    for k in range(copies):
        out_ref[4 * k : 4 * k + 4] = tile


def output(layer, copies, att, got, w_out, w_fc2):
    whole = lambda shape: pl.BlockSpec(shape, lambda i: (0,) * len(shape))
    return pl.pallas_call(
        functools.partial(output_kernel, copies),
        grid=(1,),
        in_specs=[
            whole((32, 128)),
            whole((32 * BACK, 128)),
            pl.BlockSpec((1, 512, HD), lambda i: (layer, 0, 0)),
            pl.BlockSpec((1, D, HD), lambda i: (layer, 0, 0)),
        ],
        out_specs=whole((4 * copies, 128)),
        out_shape=jax.ShapeDtypeStruct((4 * copies, 128), F32),
        scratch_shapes=[pltpu.VMEM((32 * BACK, 128), F32)],
        name="output",
        interpret=INTERPRET,
    )(att, got, w_out, w_fc2)


def per_device(
    hidden,
    ln_gain,
    w_qkv,
    w_fc1,
    w_out,
    w_fc2,
    caches,
    page_owner,
    page_used,
    page_fill,
    page_tail,
    positions,
):
    rep = lax.axis_index("rep")
    blk = lax.axis_index("blk")
    zs = [[2 * z + c for z in range(16)] for c in range(2)]
    pairs = [[2 * z, 2 * z + 1] for z in range(16)]
    rep_core = [[r * 32 + 2 * z + c for r in range(4) for c in range(2)] for z in range(16)]

    first = jnp.concatenate(
        [hidden.astype(F32), jnp.broadcast_to(positions.astype(F32)[:, None], (4, 64))], axis=1
    )
    first = spread(first, 4, "rep").reshape(16, 128)
    q_row = (blk % 8) * 2
    kv_row = rep * 4 + blk % 4
    fc_row = rep * 4 + (blk % 2) * 2
    rows = jnp.stack([q_row, q_row + 1, kv_row, fc_row, fc_row + 1])
    pick = rows[:3, None] == jnp.arange(16)[None, :]
    pick = pick & ((jnp.arange(3) < 2) | (blk // 4 < 4))[:, None]
    table = rope_tables(jnp.sum(jnp.where(pick, first[:, 64][None], 0.0), axis=1))
    meta = jnp.stack(
        [page_owner, page_used, page_fill, page_tail, jnp.full((8,), rep * 4, jnp.int32)]
    )
    rep_one = rep.reshape(1)
    weights = [w_qkv[layer].reshape(HD, 1536) for layer in range(LAYERS)]
    gains = [ln_gain[layer : layer + 1] for layer in range(LAYERS)]

    state, branch, pages = first, None, None
    for layer in range(LAYERS):
        send, state = project(layer, rep_one, state, gains[layer], weights[layer], w_fc1, branch)
        got = exchange(send.reshape(32, WIRE // 2, 2, 128), "blk").reshape(32 * WIRE, 128)
        back = finish(rows, got, table)
        got = exchange(back.reshape(32, BACK // 2, 2, 128), "blk").reshape(32 * BACK, 128)
        pages, parts = attend(layer, meta, got, caches, pages)
        parts = exchange(parts.reshape(8, 16, 128), ("rep", "blk"), rep_core)
        parts = exchange(join(parts), "blk", zs)
        att = lax.all_gather(settle(parts), "blk", axis_index_groups=pairs, tiled=True)
        if layer + 1 < LAYERS:
            out = output(layer, 16, att, got, w_out, w_fc2).reshape(16, 4, 128)
            branch = exchange(out, ("rep", "tp")).reshape(64, 128)
        else:
            out = output(layer, 4, att, got, w_out, w_fc2).reshape(4, 4, 128)
            branch = jnp.sum(exchange(out, "tp"), axis=0)[:, :HD]
            own = lax.dynamic_slice(state, (rep * 4, 0), (4, HD))
            result = (own + branch).astype(BF16)
    return (result, pages)


def solution(mesh):
    in_specs = (
        P("rep", "blk"),
        P(None, "blk"),
        P(None, "blk", None, "tp"),
        P(None, "blk", "tp"),
        P(None, "tp", "blk"),
        P(None, "tp", "blk"),
        P(None, None, ("rep", "blk"), None, "tp"),
        P(("rep", "blk")),
        P(("rep", "blk")),
        P(("rep", "blk")),
        P(("rep", "blk")),
        P("rep"),
    )
    out_specs = (P("rep", "blk"), P(None, None, ("rep", "blk"), None, "tp"))
    return jax.shard_map(
        per_device, mesh=mesh, in_specs=in_specs, out_specs=out_specs, check_vma=False
    )
```

time: 200 us -> 207 us (1.035)
  Pallas kernels: 0 us -> 23.7 us
  waiting for transfers between devices: 56.1 us -> 43.5 us
  blocking collectives: 74.8 us -> 84.1 us
  other arithmetic: 10.1 us -> 3.02 us
  matrix products: 3.04 us -> 0 us
  local copies, waits for them, and re-layouts: 14.3 us -> 11.9 us
    pallas_call x0 -> x12, Pallas kernels: none -> 23.7 us  [the longest x2 4.69 us: attend(): pl.pallas_call(functools.partial(attend_kernel, pages is not None), grid=...]
    all_to_all x4 -> x5, blocking collectives: 58.1 us -> 74.2 us  [exchange(): lax.all_to_all(value, axis, 0, 0, tiled=True, axis_index_groups=groups)]
    all_to_all x6, waiting for transfers between devices: 56.1 us -> 43.5 us  [exchange(): lax.all_to_all(value, axis, 0, 0, tiled=True, axis_index_groups=groups)]
    psum x1 -> x0, blocking collectives: 6.88 us -> none  [per_device(): branch = lax.psum(out_part, 'tp')]
    unnamed x52 -> x30, local copies, waits for them, and re-layouts: 4.61 us -> 7.85 us
    dot_general x16 -> x0, matrix products: 3.04 us -> none  [the longest x14 2.43 us: dot32(): return jnp.dot(left, right, preferred_element_type=F32)]
    broadcast_in_dim x8 -> x1, local copies, waits for them, and re-layouts: 3.25 us -> 0.6 us  [spread(): jnp.broadcast_to(value[None], (count,) + value.shape)]
  transfers between devices with their start and end apart: 6 -> 6, of which waited for: 5 -> 6; matrix products, arithmetic and copies ran while one was open for 2% -> 4% of each run, Pallas kernels for 0% -> 0%
where the time goes in v2:
time: 207 us; the launch traced here: 206 us
  blocking collectives  84.1 us (41%)
  waiting for transfers between devices  43.5 us (21%)
  starting transfers between devices  39.1 us (19%)
  Pallas kernels  23.7 us (11%)
  local copies, waits for them, and re-layouts  11.9 us (6%)
  other arithmetic  3.02 us (1%)
    all_to_all x5, blocking collectives, exchange(): lax.all_to_all(value, axis, 0, 0, tiled=True, axis_index_groups=groups)  74.2 us
    all_to_all x6, waiting for transfers between devices, exchange(): lax.all_to_all(value, axis, 0, 0, tiled=True, axis_index_groups=groups)  43.5 us
    all_to_all x6, starting transfers between devices, exchange(): lax.all_to_all(value, axis, 0, 0, tiled=True, axis_index_groups=groups)  39.1 us
    all_gather x2, blocking collectives, per_device(): lax.all_gather(settle(parts), 'blk', axis_index_groups=pairs, tiled=True)  9.83 us
    unnamed x30, local copies, waits for them, and re-layouts  7.85 us
    pallas_call x2, Pallas kernels, attend(): pl.pallas_call(functools.partial(attend_kernel, pages is not None), grid=...  4.69 us
    pallas_call x2, Pallas kernels, project(): pl.pallas_call(functools.partial(project_kernel, branch is not None), gri...  4.33 us
    pallas_call x2, Pallas kernels, output(): pl.pallas_call(functools.partial(output_kernel, copies), grid=(1,), in_sp...  4.25 us
  transfers between devices with their start and end apart: 6, of which 6 were waited for; matrix products, arithmetic and copies ran while one was open for 4% of the time, Pallas kernels for 0%

profile of v2, /device:TPU:1, one launch (start us, length us, event | category | flops | bytes accessed | tf_op | source)
XLA Modules:
  0.0 206.1 jit_solution(4679142286025560665)
XLA Ops:
  2.1 5.0 %all-to-all-start = ((f32[4,4,128]{2,1,0:T(4,128)}), f32[4,4,128]{2,1,0:T(4,128)S(1)}, u32[]{:S(2)}, u32[]{:S(2)}) async-start(f32[4,4,128]{2,1,0:T(4,128)} %broadcast_in_dim.62), calls=%async_computation | async-start | bytes 16384 | tf_op jit(solution)/shard_map/all_to_all | solution.py:26
  11.8 2.2 %project.2 = (bf16[320,128]{1,0:T(8,128)(2,1)}, f32[16,128]{1,0:T(8,128)}) custom-call(s32[1]{0:T(128)} %bitcast.rep_ref, f32[16,128]{1,0:T(8,128)} %bitcast.47, f32[1,64]{1,0:T(1,128)} %get-tuple-element.24.refs_1_, bf16[64,1536]{1,0:T(8,128)(2,1)} %bitcast.32, bf16[2,64,2048]{2,1,0:T(8,128)(2,1)} %refs_3_.3), custom_call_target="tpu_custom_call" | custom-call | tf_op jit(solution)/shard_map/project/pallas_call | solution.py:178
  14.0 17.3 %all-to-all-start.1 = ((bf16[32,5,2,128]{3,2,1,0:T(2,128)(2,1)}), bf16[32,5,2,128]{3,2,1,0:T(2,128)(2,1)S(1)}, u32[]{:S(2)}, u32[]{:S(2)}) async-start(bf16[32,5,2,128]{3,2,1,0:T(2,128)(2,1)} %bitcast.44), calls=%async_computation.1 | async-start | bytes 163840 | tf_op jit(solution)/shard_map/all_to_all | solution.py:26
  32.3 12.8 %all-to-all-done.1 = bf16[32,5,2,128]{3,2,1,0:T(2,128)(2,1)S(1)} async-done(((bf16[32,5,2,128]{3,2,1,0:T(2,128)(2,1)}), bf16[32,5,2,128]{3,2,1,0:T(2,128)(2,1)S(1)}, u32[]{:S(2)}, u32[]{:S(2)}) %all-to-all-start.1) | async-done | bytes 81952 | tf_op jit(solution)/shard_map/all_to_all | solution.py:26
  45.7 1.9 finish.2
  47.6 5.2 %all-to-all-start.2 = ((bf16[32,3,2,128]{3,2,1,0:T(2,128)(2,1)}), bf16[32,3,2,128]{3,2,1,0:T(2,128)(2,1)S(1)}, u32[]{:S(2)}, u32[]{:S(2)}) async-start(bf16[32,3,2,128]{3,2,1,0:T(2,128)(2,1)} %bitcast.40), calls=%async_computation.2 | async-start | bytes 98304 | tf_op jit(solution)/shard_map/all_to_all | solution.py:26
  54.1 11.4 %all-to-all-done.2 = bf16[32,3,2,128]{3,2,1,0:T(2,128)(2,1)S(1)} async-done(((bf16[32,3,2,128]{3,2,1,0:T(2,128)(2,1)}), bf16[32,3,2,128]{3,2,1,0:T(2,128)(2,1)S(1)}, u32[]{:S(2)}, u32[]{:S(2)}) %all-to-all-start.2) | async-done | bytes 49184 | tf_op jit(solution)/shard_map/all_to_all | solution.py:26
  66.1 2.4 %attend.2 = (bf16[2,2,8,32,512]{4,3,2,1,0:T(8,128)(2,1)}, f32[128,128]{1,0:T(8,128)}) custom-call(s32[5,8]{1,0:T(8,128)} %stack.39.meta_ref, bf16[192,128]{1,0:T(8,128)(2,1)} %bitcast.34, bf16[2,2,8,32,512]{4,3,2,1,0:T(8,128)(2,1)} %cache_ref.3), custom_call_target="tpu_custom_call" | custom-call | tf_op jit(solution)/shard_map/attend/pallas_call | solution.py:323
  68.5 10.2 %all_to_all.55.got_ref = f32[8,16,128]{2,1,0:T(8,128)} all-to-all(f32[8,16,128]{2,1,0:T(8,128)} %bitcast.49), channel_id=1, replica_groups={{0,4,128,132,256,260,384,388},{8,12,136,140,264,268,392,396},{16,20,144..., dimensions={0} | all-to-all | bytes 131072 | tf_op jit(solution)/shard_map/all_to_all | solution.py:26
  78.7 1.6 join.2
  80.4 3.5 %all-to-all-start.4 = ((bf16[16,16,128]{2,1,0:T(8,128)(2,1)}), bf16[16,16,128]{2,1,0:T(8,128)(2,1)S(1)}, u32[]{:S(2)}, u32[]{:S(2)}) async-start(bf16[16,16,128]{2,1,0:T(8,128)(2,1)} %join.2), calls=%async_computation.4 | async-start | bytes 131072 | tf_op jit(solution)/shard_map/all_to_all | solution.py:26
  84.7 1.3 copy.30.wf_ref
  86.1 9.4 %all-to-all-done.4.got_ref = bf16[16,16,128]{2,1,0:T(8,128)(2,1)S(1)} async-done(((bf16[16,16,128]{2,1,0:T(8,128)(2,1)}), bf16[16,16,128]{2,1,0:T(8,128)(2,1)S(1)}, u32[]{:S(2)}, u32[]{:S(2)}) %all-to-all-start.4) | async-done | bytes 65568 | tf_op jit(solution)/shard_map/all_to_all | solution.py:26
  96.1 1.7 settle.2
  97.8 4.9 %all_gather.6.att_ref = bf16[32,128]{1,0:T(8,128)(2,1)} all-gather(bf16[16,128]{1,0:T(8,128)(2,1)} %settle.2), channel_id=1, replica_groups={{0,4},{8,12},{16,20},{24,28},{32,36},{40,44},{48,52},{56,60},{64,68},{7..., dimensions={0}, use_global_device_ids=true | all-gather | bytes 12288 | tf_op jit(solution)/shard_map/all_gather | solution.py:471
  102.8 2.1 %output.2 = f32[64,128]{1,0:T(8,128)} custom-call(bf16[32,128]{1,0:T(8,128)(2,1)} %all_gather.6.att_ref, bf16[192,128]{1,0:T(8,128)(2,1)} %bitcast.35, bf16[2,512,64]{2,1,0:T(8,128)(2,1)} %copy.29.wo_ref, bf16[2,2048,64]{2,1,0:T(8,128)(2,1)} %copy.30.wf_ref), custom_call_target="tpu_custom_call" | custom-call | tf_op jit(solution)/shard_map/output/pallas_call | solution.py:407
  104.9 4.7 %all-to-all-start.5 = ((f32[16,4,128]{2,1,0:T(4,128)}), f32[16,4,128]{2,1,0:T(4,128)S(1)}, u32[]{:S(2)}, u32[]{:S(2)}) async-start(f32[16,4,128]{2,1,0:T(4,128)} %bitcast.43), calls=%async_computation.5 | async-start | bytes 65536 | tf_op jit(solution)/shard_map/all_to_all | solution.py:26
  110.5 5.5 %all-to-all-done.5 = f32[16,4,128]{2,1,0:T(4,128)S(1)} async-done(((f32[16,4,128]{2,1,0:T(4,128)}), f32[16,4,128]{2,1,0:T(4,128)S(1)}, u32[]{:S(2)}, u32[]{:S(2)}) %all-to-all-start.5) | async-done | bytes 32800 | tf_op jit(solution)/shard_map/all_to_all | solution.py:26
  116.7 2.2 %project.3 = (bf16[320,128]{1,0:T(8,128)(2,1)}, f32[16,128]{1,0:T(8,128)}) custom-call(s32[1]{0:T(128)} %bitcast.rep_ref, f32[16,128]{1,0:T(8,128)} %get-tuple-element.10.refs_0_, f32[1,64]{1,0:T(1,128)} %get-tuple-element.23.refs_1_, bf16[64,1536]{1,0:T(8,128)(2,1)} %bitcast.33, bf16[2,64,2048]{2,1,0:T(8,128)(2,1)} %refs_3_.3, f32[64,128]{1,0:T(8,128)} %bitcast.42), custom_call_target="tpu_custom_call" | custom-call | tf_op jit(solution)/shard_map/project/pallas_call | solution.py:178
  118.8 19.6 %all_to_all.56 = bf16[32,5,2,128]{3,2,1,0:T(2,128)(2,1)} all-to-all(bf16[32,5,2,128]{3,2,1,0:T(2,128)(2,1)} %bitcast.45), channel_id=1, replica_groups=mesh['rep'=4,'blk'=32,'tp'=4] {'blk'}, dimensions={0} | all-to-all | bytes 163840 | tf_op jit(solution)/shard_map/all_to_all | solution.py:26
  138.4 1.8 finish.3
  140.3 18.5 %all_to_all.57 = bf16[32,3,2,128]{3,2,1,0:T(2,128)(2,1)} all-to-all(bf16[32,3,2,128]{3,2,1,0:T(2,128)(2,1)} %bitcast.41), channel_id=1, replica_groups=mesh['rep'=4,'blk'=32,'tp'=4] {'blk'}, dimensions={0} | all-to-all | bytes 98304 | tf_op jit(solution)/shard_map/all_to_all | solution.py:26
  158.8 2.3 %attend.3 = (bf16[2,2,8,32,512]{4,3,2,1,0:T(8,128)(2,1)}, f32[128,128]{1,0:T(8,128)}) custom-call(s32[5,8]{1,0:T(8,128)} %stack.39.meta_ref, bf16[192,128]{1,0:T(8,128)(2,1)} %bitcast.36, bf16[2,2,8,32,512]{4,3,2,1,0:T(8,128)(2,1)} %cache_ref.3, bf16[2,2,8,32,512]{4,3,2,1,0:T(8,128)(2,1)} %get-tuple-element.15.refs_0_), custom_call_target="tpu_custom_call", output_to_operand_aliasing={{0}: (3, {})} | custom-call | tf_op jit(solution)/shard_map/attend/pallas_call | solution.py:323
  161.1 10.1 %all_to_all.58.got_ref = f32[8,16,128]{2,1,0:T(8,128)} all-to-all(f32[8,16,128]{2,1,0:T(8,128)} %bitcast.48), channel_id=1, replica_groups={{0,4,128,132,256,260,384,388},{8,12,136,140,264,268,392,396},{16,20,144..., dimensions={0} | all-to-all | bytes 131072 | tf_op jit(solution)/shard_map/all_to_all | solution.py:26
  171.2 1.6 join.3
  172.9 15.8 %all_to_all.59.got_ref = bf16[16,16,128]{2,1,0:T(8,128)(2,1)} all-to-all(bf16[16,16,128]{2,1,0:T(8,128)(2,1)} %join.3), channel_id=1, replica_groups={{0,8,16,24,32,40,48,56,64,72,80,88,96,104,112,120},{4,12,20,28,36,44,52..., dimensions={0} | all-to-all | bytes 131072 | tf_op jit(solution)/shard_map/all_to_all | solution.py:26
  188.6 1.7 settle.3
  190.4 4.9 %all_gather.7.att_ref = bf16[32,128]{1,0:T(8,128)(2,1)} all-gather(bf16[16,128]{1,0:T(8,128)(2,1)} %settle.3), channel_id=1, replica_groups={{0,4},{8,12},{16,20},{24,28},{32,36},{40,44},{48,52},{56,60},{64,68},{7..., dimensions={0}, use_global_device_ids=true | all-gather | bytes 12288 | tf_op jit(solution)/shard_map/all_gather | solution.py:471
  195.3 2.1 %output.3 = f32[16,128]{1,0:T(8,128)} custom-call(bf16[32,128]{1,0:T(8,128)(2,1)} %all_gather.7.att_ref, bf16[192,128]{1,0:T(8,128)(2,1)} %bitcast.37, bf16[2,512,64]{2,1,0:T(8,128)(2,1)} %copy.29.wo_ref, bf16[2,2048,64]{2,1,0:T(8,128)(2,1)} %copy.30.wf_ref), custom_call_target="tpu_custom_call" | custom-call | tf_op jit(solution)/shard_map/output/pallas_call | solution.py:407
  197.4 3.2 %all-to-all-start.10 = ((f32[4,4,128]{2,1,0:T(4,128)}), f32[4,4,128]{2,1,0:T(4,128)S(1)}, u32[]{:S(2)}, u32[]{:S(2)}) async-start(f32[4,4,128]{2,1,0:T(4,128)} %bitcast.50), calls=%async_computation.10 | async-start | bytes 16384 | tf_op jit(solution)/shard_map/all_to_all | solution.py:26
  200.7 4.1 %all-to-all-done.10 = f32[4,4,128]{2,1,0:T(4,128)S(1)} async-done(((f32[4,4,128]{2,1,0:T(4,128)}), f32[4,4,128]{2,1,0:T(4,128)S(1)}, u32[]{:S(2)}, u32[]{:S(2)}) %all-to-all-start.10) | async-done | bytes 8224 | tf_op jit(solution)/shard_map/all_to_all | solution.py:26
  204.8 1.2 add_convert_fusion
  (52 shorter events, 12.5 us)
Async XLA Ops:
  0.6 0.7 copy-start.7
  2.1 9.2 %all-to-all-start = ((f32[4,4,128]{2,1,0:T(4,128)}), f32[4,4,128]{2,1,0:T(4,128)S(1)}, u32[]{:S(2)}, u32[]{:S(2)}) async-start(f32[4,4,128]{2,1,0:T(4,128)} %broadcast_in_dim.62), calls=%async_computation | async-start | bytes 16384 | tf_op jit(solution)/shard_map/all_to_all | solution.py:26
  7.1 0.7 copy-start.8
  11.2 0.6 copy-start.6
  14.0 31.1 %all-to-all-start.1 = ((bf16[32,5,2,128]{3,2,1,0:T(2,128)(2,1)}), bf16[32,5,2,128]{3,2,1,0:T(2,128)(2,1)S(1)}, u32[]{:S(2)}, u32[]{:S(2)}) async-start(bf16[32,5,2,128]{3,2,1,0:T(2,128)(2,1)} %bitcast.44), calls=%async_computation.1 | async-start | bytes 163840 | tf_op jit(solution)/shard_map/all_to_all | solution.py:26
  45.1 0.6 copy-start.2
  47.6 5.3 %copy-start.12 = (s32[8]{0:T(128)S(1)}, s32[8]{0:T(128)}, u32[]{:S(2)}) copy-start(s32[8]{0:T(128)} %param.22) | copy-start | bytes 100
  47.6 18.0 %all-to-all-start.2 = ((bf16[32,3,2,128]{3,2,1,0:T(2,128)(2,1)}), bf16[32,3,2,128]{3,2,1,0:T(2,128)(2,1)S(1)}, u32[]{:S(2)}, u32[]{:S(2)}) async-start(bf16[32,3,2,128]{3,2,1,0:T(2,128)(2,1)} %bitcast.40), calls=%async_computation.2 | async-start | bytes 98304 | tf_op jit(solution)/shard_map/all_to_all | solution.py:26
  52.8 0.7 copy-start.9
  52.8 0.7 copy-start.10
  52.9 0.7 copy-start.11
  65.5 0.6 copy-start.1
  66.1 17.7 %copy-start.4 = (bf16[2,512,64]{1,2,0:T(8,128)(2,1)S(1)}, bf16[2,512,64]{1,2,0:T(8,128)(2,1)}, u32[]{:S(2)}) copy-start(bf16[2,512,64]{1,2,0:T(8,128)(2,1)} %param.16) | copy-start | bytes 393220
  68.5 16.2 %copy-start = (bf16[2,2048,64]{1,2,0:T(8,128)(2,1)S(1)}, bf16[2,2048,64]{1,2,0:T(8,128)(2,1)}, u32[]{:S(2)}) copy-start(bf16[2,2048,64]{1,2,0:T(8,128)(2,1)} %param.17) | copy-start | bytes 1572868
  80.4 15.1 %all-to-all-start.4 = ((bf16[16,16,128]{2,1,0:T(8,128)(2,1)}), bf16[16,16,128]{2,1,0:T(8,128)(2,1)S(1)}, u32[]{:S(2)}, u32[]{:S(2)}) async-start(bf16[16,16,128]{2,1,0:T(8,128)(2,1)} %join.2), calls=%async_computation.4 | async-start | bytes 131072 | tf_op jit(solution)/shard_map/all_to_all | solution.py:26
  95.5 0.6 copy-start.3
  104.9 11.2 %all-to-all-start.5 = ((f32[16,4,128]{2,1,0:T(4,128)}), f32[16,4,128]{2,1,0:T(4,128)S(1)}, u32[]{:S(2)}, u32[]{:S(2)}) async-start(f32[16,4,128]{2,1,0:T(4,128)} %bitcast.43), calls=%async_computation.5 | async-start | bytes 65536 | tf_op jit(solution)/shard_map/all_to_all | solution.py:26
  116.1 0.6 copy-start.5
  197.4 7.4 %all-to-all-start.10 = ((f32[4,4,128]{2,1,0:T(4,128)}), f32[4,4,128]{2,1,0:T(4,128)S(1)}, u32[]{:S(2)}, u32[]{:S(2)}) async-start(f32[4,4,128]{2,1,0:T(4,128)} %bitcast.50), calls=%async_computation.10 | async-start | bytes 16384 | tf_op jit(solution)/shard_map/all_to_all | solution.py:26

commit v3 on v2

--- a/solution.py
+++ b/solution.py
@@ -42,12 +42,24 @@
     return jnp.concatenate([cosine, sine_up, sine_down], axis=0)
 
 
+def near(value):
+    return value if INTERPRET else pltpu.with_memory_space_constraint(value, pltpu.VMEM)
+
+
+def near_out(shape, dtype):
+    return jax.ShapeDtypeStruct(shape, dtype) if INTERPRET else pltpu.VMEM(shape, dtype)
+
+
 def iota(shape, axis):
     return lax.broadcasted_iota(jnp.int32, shape, axis)
 
 
 def dot32(left, right):
     return jnp.dot(left, right, preferred_element_type=F32)
+
+
+def dot_t(left, right):
+    return lax.dot_general(left, right, (((1,), (1,)), ((), ())), preferred_element_type=F32)
 
 
 def parts_of(value, count):
@@ -109,10 +121,9 @@
     def product(first, last, weights):
         return dot32(left_high[first:last], weights) + dot32(left_low[first:last], weights)
 
-    wq = wq_ref[...]
     wf = wf_ref[0]
-    every_q = product(0, 48, wq[:, :512])
-    every_kv = product(16, 48, wq[:, 512:])
+    every_q = product(0, 48, wq_ref[0, 0])
+    every_kv = jnp.concatenate([product(16, 48, wq_ref[0, k]) for k in (1, 2)], axis=1)
     every_fc = product(24, 48, wf)
     sub = iota((8, 128), 0)
 
@@ -166,13 +177,13 @@
 
 
 def project(layer, rep, x, gain, wq, wf, branch=None):
-    args = [rep, x, gain, wq, wf] + ([] if branch is None else [branch])
+    args = [rep, near(x), near(gain), wq, wf] + ([] if branch is None else [near(branch)])
     full = lambda shape: pl.BlockSpec(shape, lambda i: (0,) * len(shape))
     specs = [
         pl.BlockSpec(memory_space=pltpu.SMEM),
         full((16, 128)),
         full((1, HD)),
-        full((HD, 1536)),
+        pl.BlockSpec((1, 3, HD, 512), lambda i: (layer, 0, 0, 0)),
         pl.BlockSpec((1, HD, D), lambda i: (layer, 0, 0)),
     ] + ([] if branch is None else [full((64, 128))])
     return pl.pallas_call(
@@ -181,8 +192,8 @@
         in_specs=specs,
         out_specs=(full((32 * WIRE, 128)), full((16, 128))),
         out_shape=(
-            jax.ShapeDtypeStruct((32 * WIRE, 128), BF16),
-            jax.ShapeDtypeStruct((16, 128), F32),
+            near_out((32 * WIRE, 128), BF16),
+            near_out((16, 128), F32),
         ),
         scratch_shapes=[pltpu.VMEM((32 * WIRE, 128), F32)],
         name="project",
@@ -234,14 +245,14 @@
             pl.BlockSpec(memory_space=pltpu.VMEM),
         ],
         out_specs=pl.BlockSpec(memory_space=pltpu.VMEM),
-        out_shape=jax.ShapeDtypeStruct((32 * BACK, 128), BF16),
+        out_shape=near_out((32 * BACK, 128), BF16),
         scratch_shapes=[
             pltpu.VMEM((32 * WIRE, 128), F32),
             pltpu.VMEM((32 * BACK, 128), F32),
         ],
         name="finish",
         interpret=INTERPRET,
-    )(rows, got, table)
+    )(rows, near(got), near(table))
 
 
 def attend_kernel(aliased, meta_ref, got_ref, cache_ref, *refs):
@@ -281,10 +292,7 @@
     ).astype(BF16)
     keys = pages_ref[0, 0].reshape(8 * PAGE, 512)
     values = pages_ref[0, 1].reshape(8 * PAGE, 512)
-    scores = (
-        lax.dot_general(wide, keys, (((1,), (1,)), ((), ())), preferred_element_type=F32)
-        * HD ** (-0.5)
-    )
+    scores = dot_t(wide, keys) * HD ** (-0.5)
     page_of = iota((1, 256), 1) // PAGE
     owner = jnp.zeros((1, 256), jnp.int32)
     limit = jnp.zeros((1, 256), jnp.int32)
@@ -314,7 +322,7 @@
     block = pl.BlockSpec((1, 2, 8, PAGE, 512), lambda i: (layer, 0, 0, 0, 0))
     whole = lambda shape: pl.BlockSpec(shape, lambda i: (0,) * len(shape))
     specs = [pl.BlockSpec(memory_space=pltpu.SMEM), whole((32 * BACK, 128)), block]
-    args = [meta, got, caches]
+    args = [meta, near(got), caches]
     aliases = {}
     if pages is not None:
         specs.append(pl.BlockSpec(memory_space=pl.ANY))
@@ -327,7 +335,7 @@
         out_specs=(block, whole((128, 128))),
         out_shape=(
             jax.ShapeDtypeStruct(caches.shape, BF16),
-            jax.ShapeDtypeStruct((128, 128), F32),
+            near_out((128, 128), F32),
         ),
         scratch_shapes=[pltpu.VMEM((32 * BACK, 128), F32), pltpu.VMEM((2, 4, 512), F32)],
         input_output_aliases=aliases,
@@ -352,10 +360,10 @@
 def join(got):
     return pl.pallas_call(
         join_kernel,
-        out_shape=jax.ShapeDtypeStruct((16, 16, 128), BF16),
+        out_shape=near_out((16, 16, 128), BF16),
         name="join",
         interpret=INTERPRET,
-    )(got)
+    )(near(got))
 
 
 def settle_kernel(got_ref, out_ref):
@@ -371,10 +379,10 @@
 def settle(got):
     return pl.pallas_call(
         settle_kernel,
-        out_shape=jax.ShapeDtypeStruct((16, 128), BF16),
+        out_shape=near_out((16, 128), BF16),
         name="settle",
         interpret=INTERPRET,
-    )(got)
+    )(near(got))
 
 
 def output_kernel(copies, att_ref, got_ref, wo_ref, wf_ref, out_ref, back):
@@ -383,13 +391,13 @@
     att = att + pltpu.roll(att, HD, 1)
     att = jnp.concatenate([att] * 4, axis=1)
     own = iota((32, 512), 1) // HD == iota((32, 512), 0) % 8
-    by_head = dot32(jnp.where(own, att, 0.0).astype(BF16), wo_ref[0])
+    by_head = dot_t(jnp.where(own, att, 0.0).astype(BF16), wo_ref[0])
     chunk = iota((32, D), 1) // 128 == iota((32, D), 0) // 2
     mlp = []
     for k in range(2):
         act = back[pl.ds(3 + k, 32, stride=BACK), :]
         act = jnp.concatenate([act] * 16, axis=1)
-        mlp.append(dot32(jnp.where(chunk, act, 0.0).astype(BF16), wf_ref[0]))
+        mlp.append(dot_t(jnp.where(chunk, act, 0.0).astype(BF16), wf_ref[0]))
     odd = iota((32, HD), 0) % 2
     rows = []
     for i in range(4):
@@ -410,15 +418,15 @@
         in_specs=[
             whole((32, 128)),
             whole((32 * BACK, 128)),
-            pl.BlockSpec((1, 512, HD), lambda i: (layer, 0, 0)),
-            pl.BlockSpec((1, D, HD), lambda i: (layer, 0, 0)),
+            pl.BlockSpec((1, HD, 512), lambda i: (layer, 0, 0)),
+            pl.BlockSpec((1, HD, D), lambda i: (layer, 0, 0)),
         ],
         out_specs=whole((4 * copies, 128)),
-        out_shape=jax.ShapeDtypeStruct((4 * copies, 128), F32),
+        out_shape=near_out((4 * copies, 128), F32),
         scratch_shapes=[pltpu.VMEM((32 * BACK, 128), F32)],
         name="output",
         interpret=INTERPRET,
-    )(att, got, w_out, w_fc2)
+    )(near(att), near(got), w_out, w_fc2)
 
 
 def per_device(
@@ -456,12 +464,14 @@
         [page_owner, page_used, page_fill, page_tail, jnp.full((8,), rep * 4, jnp.int32)]
     )
     rep_one = rep.reshape(1)
-    weights = [w_qkv[layer].reshape(HD, 1536) for layer in range(LAYERS)]
+    w_qkv = w_qkv.transpose(0, 2, 1, 3)
+    w_out = w_out.transpose(0, 2, 1)
+    w_fc2 = w_fc2.transpose(0, 2, 1)
     gains = [ln_gain[layer : layer + 1] for layer in range(LAYERS)]
 
     state, branch, pages = first, None, None
     for layer in range(LAYERS):
-        send, state = project(layer, rep_one, state, gains[layer], weights[layer], w_fc1, branch)
+        send, state = project(layer, rep_one, state, gains[layer], w_qkv, w_fc1, branch)
         got = exchange(send.reshape(32, WIRE // 2, 2, 128), "blk").reshape(32 * WIRE, 128)
         back = finish(rows, got, table)
         got = exchange(back.reshape(32, BACK // 2, 2, 128), "blk").reshape(32 * BACK, 128)

time: 207 us -> 183 us (0.88)
  blocking collectives: 84.1 us -> 98.7 us
  waiting for transfers between devices: 43.5 us -> 31.7 us
  Pallas kernels: 23.7 us -> 14.9 us
  local copies, waits for them, and re-layouts: 11.9 us -> 3.39 us
  starting transfers between devices: 39.1 us -> 30.9 us
    all_to_all x5 -> x7, blocking collectives: 74.2 us -> 91.7 us  [exchange(): lax.all_to_all(value, axis, 0, 0, tiled=True, axis_index_groups=groups)]
    all_to_all x6 -> x4, waiting for transfers between devices: 43.5 us -> 31.7 us  [exchange(): lax.all_to_all(value, axis, 0, 0, tiled=True, axis_index_groups=groups)]
    all_to_all x6 -> x4, starting transfers between devices: 39.1 us -> 30.9 us  [exchange(): lax.all_to_all(value, axis, 0, 0, tiled=True, axis_index_groups=groups)]
    unnamed x30 -> x12, local copies, waits for them, and re-layouts: 7.85 us -> 1.33 us
    pallas_call x4, Pallas kernels: 6.74 us -> 0.94 us  [the longest x2 0.58 us: settle(): pl.pallas_call(settle_kernel, out_shape=near_out((16, 128), BF16), name='...]
    all_gather x2, blocking collectives: 9.83 us -> 7.04 us  [per_device(): lax.all_gather(settle(parts), 'blk', axis_index_groups=pairs, tiled=True)]
  transfers between devices with their start and end apart: 6 -> 4, of which waited for: 6 -> 4; matrix products, arithmetic and copies ran while one was open for 4% -> 1% of each run, Pallas kernels for 0% -> 0%
where the time goes in v3:
time: 183 us; the launch traced here: 182 us
  blocking collectives  98.7 us (54%)
  waiting for transfers between devices  31.7 us (17%)
  starting transfers between devices  30.9 us (17%)
  Pallas kernels  14.9 us (8%)
  local copies, waits for them, and re-layouts  3.39 us (2%)
    all_to_all x7, blocking collectives, exchange(): lax.all_to_all(value, axis, 0, 0, tiled=True, axis_index_groups=groups)  91.7 us
    all_to_all x4, waiting for transfers between devices, exchange(): lax.all_to_all(value, axis, 0, 0, tiled=True, axis_index_groups=groups)  31.7 us
    all_to_all x4, starting transfers between devices, exchange(): lax.all_to_all(value, axis, 0, 0, tiled=True, axis_index_groups=groups)  30.9 us
    all_gather x2, blocking collectives, per_device(): lax.all_gather(settle(parts), 'blk', axis_index_groups=pairs, tiled=True)  7.04 us
    pallas_call x2, Pallas kernels, attend(): pl.pallas_call(functools.partial(attend_kernel, pages is not None), grid=...  4.35 us
    pallas_call x2, Pallas kernels, project(): pl.pallas_call(functools.partial(project_kernel, branch is not None), gri...  3.72 us
  transfers between devices with their start and end apart: 4, of which 4 were waited for; matrix products, arithmetic and copies ran while one was open for 1% of the time, Pallas kernels for 0%

profile of v3, /device:TPU:1, one launch (start us, length us, event | category | flops | bytes accessed | tf_op | source)
XLA Modules:
  0.0 182.1 jit_solution(11403684641301919158)
XLA Ops:
  0.6 0.7 convert_element_type.17
  1.5 0.6 broadcast_in_dim.62
  2.1 5.0 %all-to-all-start = ((f32[4,4,128]{2,1,0:T(4,128)}), f32[4,4,128]{2,1,0:T(4,128)S(1)}, u32[]{:S(2)}, u32[]{:S(2)}) async-start(f32[4,4,128]{2,1,0:T(4,128)} %broadcast_in_dim.62), calls=%async_computation | async-start | bytes 16384 | tf_op jit(solution)/shard_map/all_to_all | solution.py:26
  7.2 0.7 copy-done.1
  7.9 0.6 stack.45.rows_ref
  8.5 2.7 %all-to-all-done = f32[4,4,128]{2,1,0:T(4,128)S(1)} async-done(((f32[4,4,128]{2,1,0:T(4,128)}), f32[4,4,128]{2,1,0:T(4,128)S(1)}, u32[]{:S(2)}, u32[]{:S(2)}) %all-to-all-start) | async-done | bytes 8224 | tf_op jit(solution)/shard_map/all_to_all | solution.py:26
  11.4 2.2 %project.2 = (bf16[320,128]{1,0:T(8,128)(2,1)}, f32[16,128]{1,0:T(8,128)S(1)}) custom-call(s32[1]{0:T(128)} %bitcast.rep_ref, f32[16,128]{1,0:T(8,128)S(1)} %bitcast.38, f32[1,64]{1,0:T(1,128)S(1)} %get-tuple-element.22.refs_1_, bf16[2,3,64,512]{3,2,1,0:T(8,128)(2,1)} %bitcast.43, bf16[2,64,2048]{2,1,0:T(8,128)(2,1)} %refs_3_.3), custom_call_target="tpu_custom_call" | custom-call | tf_op jit(solution)/shard_map/project/pallas_call | solution.py:189
  13.6 17.3 %all-to-all-start.1 = ((bf16[32,5,2,128]{3,2,1,0:T(2,128)(2,1)}), bf16[32,5,2,128]{3,2,1,0:T(2,128)(2,1)S(1)}, u32[]{:S(2)}, u32[]{:S(2)}) async-start(bf16[32,5,2,128]{3,2,1,0:T(2,128)(2,1)} %bitcast.12), calls=%async_computation.1 | async-start | bytes 163840 | tf_op jit(solution)/shard_map/all_to_all | solution.py:26
  31.3 13.4 %all-to-all-done.1 = bf16[32,5,2,128]{3,2,1,0:T(2,128)(2,1)S(1)} async-done(((bf16[32,5,2,128]{3,2,1,0:T(2,128)(2,1)}), bf16[32,5,2,128]{3,2,1,0:T(2,128)(2,1)S(1)}, u32[]{:S(2)}, u32[]{:S(2)}) %all-to-all-start.1) | async-done | bytes 81952 | tf_op jit(solution)/shard_map/all_to_all | solution.py:26
  44.7 1.6 finish.2
  46.3 5.3 %all-to-all-start.2 = ((bf16[32,3,2,128]{3,2,1,0:T(2,128)(2,1)}), bf16[32,3,2,128]{3,2,1,0:T(2,128)(2,1)S(1)}, u32[]{:S(2)}, u32[]{:S(2)}) async-start(bf16[32,3,2,128]{3,2,1,0:T(2,128)(2,1)} %bitcast.14), calls=%async_computation.2 | async-start | bytes 98304 | tf_op jit(solution)/shard_map/all_to_all | solution.py:26
  51.6 0.6 copy-done.2
  52.3 0.6 stack.39.meta_ref
  52.9 11.4 %all-to-all-done.2 = bf16[32,3,2,128]{3,2,1,0:T(2,128)(2,1)S(1)} async-done(((bf16[32,3,2,128]{3,2,1,0:T(2,128)(2,1)}), bf16[32,3,2,128]{3,2,1,0:T(2,128)(2,1)S(1)}, u32[]{:S(2)}, u32[]{:S(2)}) %all-to-all-start.2) | async-done | bytes 49184 | tf_op jit(solution)/shard_map/all_to_all | solution.py:26
  64.3 2.2 %attend.2 = (bf16[2,2,8,32,512]{4,3,2,1,0:T(8,128)(2,1)}, f32[128,128]{1,0:T(8,128)S(1)}) custom-call(s32[5,8]{1,0:T(8,128)} %stack.39.meta_ref, bf16[192,128]{1,0:T(8,128)(2,1)S(1)} %bitcast.27, bf16[2,2,8,32,512]{4,3,2,1,0:T(8,128)(2,1)} %cache_ref.3), custom_call_target="tpu_custom_call" | custom-call | tf_op jit(solution)/shard_map/attend/pallas_call | solution.py:331
  66.5 8.5 %all_to_all.55.got_ref = f32[8,16,128]{2,1,0:T(8,128)S(1)} all-to-all(f32[8,16,128]{2,1,0:T(8,128)S(1)} %bitcast.40), channel_id=1, replica_groups={{0,4,128,132,256,260,384,388},{8,12,136,140,264,268,392,396},{16,20,144..., dimensions={0} | all-to-all | bytes 131072 | tf_op jit(solution)/shard_map/all_to_all | solution.py:26
  75.2 14.2 %all_to_all.56.got_ref = bf16[16,16,128]{2,1,0:T(8,128)(2,1)S(1)} all-to-all(bf16[16,16,128]{2,1,0:T(8,128)(2,1)S(1)} %join.2), channel_id=1, replica_groups={{0,8,16,24,32,40,48,56,64,72,80,88,96,104,112,120},{4,12,20,28,36,44,52..., dimensions={0} | all-to-all | bytes 131072 | tf_op jit(solution)/shard_map/all_to_all | solution.py:26
  89.7 3.5 %all_gather.6.att_ref = bf16[32,128]{1,0:T(8,128)(2,1)S(1)} all-gather(bf16[16,128]{1,0:T(8,128)(2,1)S(1)} %settle.2), channel_id=1, replica_groups={{0,4},{8,12},{16,20},{24,28},{32,36},{40,44},{48,52},{56,60},{64,68},{7..., dimensions={0}, use_global_device_ids=true | all-gather | bytes 12288 | tf_op jit(solution)/shard_map/all_gather | solution.py:481
  93.2 1.3 output.2
  94.5 11.0 %all_to_all.57 = f32[16,4,128]{2,1,0:T(4,128)S(1)} all-to-all(f32[16,4,128]{2,1,0:T(4,128)S(1)} %bitcast.35), channel_id=1, replica_groups=mesh['rep'=4,'blk'=32,'tp'=4] {'rep','tp'}, dimensions={0} | all-to-all | bytes 65536 | tf_op jit(solution)/shard_map/all_to_all | solution.py:26
  105.5 1.5 project.3
  107.1 18.3 %all_to_all.58 = bf16[32,5,2,128]{3,2,1,0:T(2,128)(2,1)S(1)} all-to-all(bf16[32,5,2,128]{3,2,1,0:T(2,128)(2,1)S(1)} %bitcast.36), channel_id=1, replica_groups=mesh['rep'=4,'blk'=32,'tp'=4] {'blk'}, dimensions={0} | all-to-all | bytes 163840 | tf_op jit(solution)/shard_map/all_to_all | solution.py:26
  125.3 1.0 finish.3
  126.3 17.0 %all_to_all.59 = bf16[32,3,2,128]{3,2,1,0:T(2,128)(2,1)S(1)} all-to-all(bf16[32,3,2,128]{3,2,1,0:T(2,128)(2,1)S(1)} %bitcast.33), channel_id=1, replica_groups=mesh['rep'=4,'blk'=32,'tp'=4] {'blk'}, dimensions={0} | all-to-all | bytes 98304 | tf_op jit(solution)/shard_map/all_to_all | solution.py:26
  143.3 2.2 %attend.3 = (bf16[2,2,8,32,512]{4,3,2,1,0:T(8,128)(2,1)}, f32[128,128]{1,0:T(8,128)S(1)}) custom-call(s32[5,8]{1,0:T(8,128)} %stack.39.meta_ref, bf16[192,128]{1,0:T(8,128)(2,1)S(1)} %bitcast.29, bf16[2,2,8,32,512]{4,3,2,1,0:T(8,128)(2,1)} %cache_ref.3, bf16[2,2,8,32,512]{4,3,2,1,0:T(8,128)(2,1)} %get-tuple-element.15.refs_0_), custom_call_target="tpu_custom_call", output_to_operand_aliasing={{0}: (3, {})} | custom-call | tf_op jit(solution)/shard_map/attend/pallas_call | solution.py:331
  145.5 8.5 %all_to_all.60.got_ref = f32[8,16,128]{2,1,0:T(8,128)S(1)} all-to-all(f32[8,16,128]{2,1,0:T(8,128)S(1)} %bitcast.39), channel_id=1, replica_groups={{0,4,128,132,256,260,384,388},{8,12,136,140,264,268,392,396},{16,20,144..., dimensions={0} | all-to-all | bytes 131072 | tf_op jit(solution)/shard_map/all_to_all | solution.py:26
  154.2 14.2 %all_to_all.61.got_ref = bf16[16,16,128]{2,1,0:T(8,128)(2,1)S(1)} all-to-all(bf16[16,16,128]{2,1,0:T(8,128)(2,1)S(1)} %join.3), channel_id=1, replica_groups={{0,8,16,24,32,40,48,56,64,72,80,88,96,104,112,120},{4,12,20,28,36,44,52..., dimensions={0} | all-to-all | bytes 131072 | tf_op jit(solution)/shard_map/all_to_all | solution.py:26
  168.7 3.5 %all_gather.7.att_ref = bf16[32,128]{1,0:T(8,128)(2,1)S(1)} all-gather(bf16[16,128]{1,0:T(8,128)(2,1)S(1)} %settle.3), channel_id=1, replica_groups={{0,4},{8,12},{16,20},{24,28},{32,36},{40,44},{48,52},{56,60},{64,68},{7..., dimensions={0}, use_global_device_ids=true | all-gather | bytes 12288 | tf_op jit(solution)/shard_map/all_gather | solution.py:481
  172.2 1.9 %output.3 = f32[16,128]{1,0:T(8,128)} custom-call(bf16[32,128]{1,0:T(8,128)(2,1)S(1)} %all_gather.7.att_ref, bf16[192,128]{1,0:T(8,128)(2,1)S(1)} %bitcast.30, bf16[2,64,512]{2,1,0:T(8,128)(2,1)} %bitcast.46, bf16[2,64,2048]{2,1,0:T(8,128)(2,1)} %bitcast.42), custom_call_target="tpu_custom_call" | custom-call | tf_op jit(solution)/shard_map/output/pallas_call | solution.py:415
  174.1 3.2 %all-to-all-start.10 = ((f32[4,4,128]{2,1,0:T(4,128)}), f32[4,4,128]{2,1,0:T(4,128)S(1)}, u32[]{:S(2)}, u32[]{:S(2)}) async-start(f32[4,4,128]{2,1,0:T(4,128)} %bitcast.26), calls=%async_computation.10 | async-start | bytes 16384 | tf_op jit(solution)/shard_map/all_to_all | solution.py:26
  177.4 4.1 %all-to-all-done.10 = f32[4,4,128]{2,1,0:T(4,128)S(1)} async-done(((f32[4,4,128]{2,1,0:T(4,128)}), f32[4,4,128]{2,1,0:T(4,128)S(1)}, u32[]{:S(2)}, u32[]{:S(2)}) %all-to-all-start.10) | async-done | bytes 8224 | tf_op jit(solution)/shard_map/all_to_all | solution.py:26
  181.5 0.6 add_convert_fusion
  (29 shorter events, 1.8 us)
Async XLA Ops:
  0.6 0.7 copy-start
  2.1 9.2 %all-to-all-start = ((f32[4,4,128]{2,1,0:T(4,128)}), f32[4,4,128]{2,1,0:T(4,128)S(1)}, u32[]{:S(2)}, u32[]{:S(2)}) async-start(f32[4,4,128]{2,1,0:T(4,128)} %broadcast_in_dim.62), calls=%async_computation | async-start | bytes 16384 | tf_op jit(solution)/shard_map/all_to_all | solution.py:26
  7.1 0.7 copy-start.1
  13.6 31.1 %all-to-all-start.1 = ((bf16[32,5,2,128]{3,2,1,0:T(2,128)(2,1)}), bf16[32,5,2,128]{3,2,1,0:T(2,128)(2,1)S(1)}, u32[]{:S(2)}, u32[]{:S(2)}) async-start(bf16[32,5,2,128]{3,2,1,0:T(2,128)(2,1)} %bitcast.12), calls=%async_computation.1 | async-start | bytes 163840 | tf_op jit(solution)/shard_map/all_to_all | solution.py:26
  46.3 5.3 %copy-start.5 = (s32[8]{0:T(128)S(1)}, s32[8]{0:T(128)}, u32[]{:S(2)}) copy-start(s32[8]{0:T(128)} %param.22) | copy-start | bytes 100
  46.3 18.0 %all-to-all-start.2 = ((bf16[32,3,2,128]{3,2,1,0:T(2,128)(2,1)}), bf16[32,3,2,128]{3,2,1,0:T(2,128)(2,1)S(1)}, u32[]{:S(2)}, u32[]{:S(2)}) async-start(bf16[32,3,2,128]{3,2,1,0:T(2,128)(2,1)} %bitcast.14), calls=%async_computation.2 | async-start | bytes 98304 | tf_op jit(solution)/shard_map/all_to_all | solution.py:26
  51.6 0.7 copy-start.2
  51.6 0.7 copy-start.3
  51.6 0.7 copy-start.4
  174.1 7.4 %all-to-all-start.10 = ((f32[4,4,128]{2,1,0:T(4,128)}), f32[4,4,128]{2,1,0:T(4,128)S(1)}, u32[]{:S(2)}, u32[]{:S(2)}) async-start(f32[4,4,128]{2,1,0:T(4,128)} %bitcast.26), calls=%async_computation.10 | async-start | bytes 16384 | tf_op jit(solution)/shard_map/all_to_all | solution.py:26

commit v4 on v3

--- a/solution.py
+++ b/solution.py
@@ -30,16 +30,12 @@
     return exchange(jnp.broadcast_to(value[None], (count,) + value.shape), axis, groups)
 
 
-def rope_tables(positions):
-    lane = jnp.arange(128, dtype=jnp.int32) % HD
+def rope_factors(positions):
+    lane = jnp.arange(64, dtype=jnp.int32)
     steps_f = (lane % (ROT // 2)).astype(F32)
-    inverse = 10000.0 ** (-2.0 * steps_f / ROT)
-    angles = positions[:, None] * inverse[None, :]
-    cosine = jnp.where(lane[None, :] < ROT, jnp.cos(angles), 1.0)
+    angles = positions.astype(F32)[:, None] * (10000.0 ** (-2.0 * steps_f / ROT))[None, :]
     sine = jnp.sin(angles)
-    sine_up = jnp.where(lane[None, :] < ROT // 2, -sine, 0.0)
-    sine_down = jnp.where((lane[None, :] >= ROT // 2) & (lane[None, :] < ROT), sine, 0.0)
-    return jnp.concatenate([cosine, sine_up, sine_down], axis=0)
+    return jnp.where(lane < 32, jnp.cos(angles), jnp.where(lane < 48, -sine, sine))
 
 
 def near(value):
@@ -71,7 +67,7 @@
     return found
 
 
-def project_kernel(with_branch, rep_ref, *refs):
+def project_kernel(layer, with_branch, meta_ref, *refs):
     if with_branch:
         x_ref, gain_ref, wq_ref, wf_ref, branch_ref, send_ref, state_ref, wire = refs
         sums = []
@@ -86,14 +82,14 @@
         x_ref, gain_ref, wq_ref, wf_ref, send_ref, state_ref, wire = refs
         x = x_ref[:, :HD]
     state_ref[...] = jnp.concatenate([x, jnp.zeros_like(x)], axis=1)
-    gain = gain_ref[...]
+    gain = gain_ref[layer : layer + 1]
     mean = jnp.sum(x, axis=1, keepdims=True) * (1.0 / HD)
     centered = x - mean
     square = jnp.sum(centered * centered, axis=1, keepdims=True)
     scaled = centered * gain
     row = iota((48, 24), 0)
     col = iota((48, 24), 1)
-    own = rep_ref[0] * 4
+    own = meta_ref[4, 0] * 4
     within = row % 8
     want = jnp.where(
         row < 8,
@@ -121,9 +117,9 @@
     def product(first, last, weights):
         return dot32(left_high[first:last], weights) + dot32(left_low[first:last], weights)
 
-    wf = wf_ref[0]
-    every_q = product(0, 48, wq_ref[0, 0])
-    every_kv = jnp.concatenate([product(16, 48, wq_ref[0, k]) for k in (1, 2)], axis=1)
+    wf = wf_ref[layer]
+    every_q = product(0, 48, wq_ref[layer, 0])
+    every_kv = jnp.concatenate([product(16, 48, wq_ref[layer, k]) for k in (1, 2)], axis=1)
     every_fc = product(24, 48, wf)
     sub = iota((8, 128), 0)
 
@@ -176,32 +172,40 @@
     send_ref[...] = wire[...].astype(BF16)
 
 
-def project(layer, rep, x, gain, wq, wf, branch=None):
-    args = [rep, near(x), near(gain), wq, wf] + ([] if branch is None else [near(branch)])
-    full = lambda shape: pl.BlockSpec(shape, lambda i: (0,) * len(shape))
-    specs = [
-        pl.BlockSpec(memory_space=pltpu.SMEM),
-        full((16, 128)),
-        full((1, HD)),
-        pl.BlockSpec((1, 3, HD, 512), lambda i: (layer, 0, 0, 0)),
-        pl.BlockSpec((1, HD, D), lambda i: (layer, 0, 0)),
-    ] + ([] if branch is None else [full((64, 128))])
+def call(kernel, name, outs, scratch, meta, *args, aliases=None):
+    specs = [pl.BlockSpec(memory_space=pltpu.SMEM)]
+    specs += [pl.BlockSpec(memory_space=pltpu.VMEM) for _ in args]
+    place = pl.BlockSpec(memory_space=pltpu.VMEM)
     return pl.pallas_call(
-        functools.partial(project_kernel, branch is not None),
-        grid=(1,),
+        kernel,
         in_specs=specs,
-        out_specs=(full((32 * WIRE, 128)), full((16, 128))),
-        out_shape=(
-            near_out((32 * WIRE, 128), BF16),
-            near_out((16, 128), F32),
-        ),
-        scratch_shapes=[pltpu.VMEM((32 * WIRE, 128), F32)],
-        name="project",
+        out_specs=jax.tree.map(lambda _: place, outs, is_leaf=lambda x: hasattr(x, "shape")),
+        out_shape=outs,
+        scratch_shapes=scratch,
+        input_output_aliases=aliases or {},
+        compiler_params=pltpu.CompilerParams(vmem_limit_bytes=24 * 2**20),
+        name=name,
         interpret=INTERPRET,
-    )(*args)
-
-
-def finish_kernel(rows_ref, got_ref, table_ref, out_ref, wire, back):
+    )(meta, *[near(arg) for arg in args])
+
+
+def project(layer, meta, x, gain, wq, wf, branch=None):
+    args = [x, gain, wq, wf] + ([] if branch is None else [branch])
+    return call(
+        functools.partial(project_kernel, layer, branch is not None),
+        "project",
+        (near_out((32 * WIRE, 128), BF16), near_out((16, 128), F32)),
+        [pltpu.VMEM((32 * WIRE, 128), F32)],
+        meta,
+        *args,
+    )
+
+
+def finish_kernel(meta_ref, got_ref, first_ref, out_ref, wire, back):
+    rep, blk = meta_ref[4, 0], meta_ref[4, 1]
+    q_row = (blk % 8) * 2
+    fc_row = rep * 4 + (blk % 2) * 2
+    requests = (q_row, q_row + 1, rep * 4 + blk % 4, fc_row, fc_row + 1)
     wire[...] = got_ref[...].astype(F32)
     take = lambda k: wire[pl.ds(k, 32, stride=WIRE), :]
     stats = take(8)
@@ -216,16 +220,21 @@
     columns = [take(5), take(6), take(7)]
     half = ROT // 2
     for k, column in enumerate((0, 0, 1, 2, 2)):
-        request = rows_ref[k]
+        request = requests[k]
         row_offset = jnp.sum(jnp.where(lane == request, offset, 0.0), axis=1, keepdims=True)
         row_rstd = jnp.sum(jnp.where(lane_one == request, rstd, 0.0), axis=1, keepdims=True)
         value = row_rstd * jnp.sum(take(k) + row_offset * columns[column], axis=0, keepdims=True)
         if k < 3:
-            value = (
-                value * table_ref[k : k + 1]
-                + pltpu.roll(value, 128 - half, 1) * table_ref[3 + k : 4 + k]
-                + pltpu.roll(value, half, 1) * table_ref[6 + k : 7 + k]
+            factors = first_ref[pl.ds(request, 1), :]
+            place = lane_one % HD
+            turned = place < ROT if k < 2 else (place < ROT) & (blk < 16)
+            left = lane_one < HD
+            cosine = jnp.where(left, pltpu.roll(factors, 64, 1), factors)
+            sine = jnp.where(left, pltpu.roll(factors, 32, 1), pltpu.roll(factors, 96, 1))
+            other = jnp.where(
+                place < half, pltpu.roll(value, 128 - half, 1), pltpu.roll(value, half, 1)
             )
+            value = jnp.where(turned, value * cosine + other * sine, value)
         else:
             cubed = value * value * value
             value = (
@@ -236,26 +245,19 @@
     out_ref[...] = back[...].astype(BF16)
 
 
-def finish(rows, got, table):
-    return pl.pallas_call(
+def finish(meta, got, first):
+    return call(
         finish_kernel,
-        in_specs=[
-            pl.BlockSpec(memory_space=pltpu.SMEM),
-            pl.BlockSpec(memory_space=pltpu.VMEM),
-            pl.BlockSpec(memory_space=pltpu.VMEM),
-        ],
-        out_specs=pl.BlockSpec(memory_space=pltpu.VMEM),
-        out_shape=near_out((32 * BACK, 128), BF16),
-        scratch_shapes=[
-            pltpu.VMEM((32 * WIRE, 128), F32),
-            pltpu.VMEM((32 * BACK, 128), F32),
-        ],
-        name="finish",
-        interpret=INTERPRET,
-    )(rows, near(got), near(table))
-
-
-def attend_kernel(aliased, meta_ref, got_ref, cache_ref, *refs):
+        "finish",
+        near_out((32 * BACK, 128), BF16),
+        [pltpu.VMEM((32 * WIRE, 128), F32), pltpu.VMEM((32 * BACK, 128), F32)],
+        meta,
+        got,
+        first,
+    )
+
+
+def attend_kernel(layer, aliased, meta_ref, got_ref, cache_ref, *refs):
     if aliased:
         _, pages_ref, out_ref, back, kv = refs
     else:
@@ -272,11 +274,11 @@
     spot = iota((PAGE, 512), 0)
     for side in range(2):
         for page in range(8):
-            home = jnp.clip(meta_ref[0, page] - meta_ref[4, 0], 0, 3)
+            home = jnp.clip(meta_ref[0, page] - meta_ref[4, 0] * 4, 0, 3)
             place = jnp.where(meta_ref[3, page] == 1, meta_ref[2, page], -1)
             fresh = kv[side, pl.ds(home, 1), :]
-            old = cache_ref[0, side, page].astype(F32)
-            pages_ref[0, side, page] = jnp.where(spot == place, fresh, old).astype(BF16)
+            old = cache_ref[layer, side, page].astype(F32)
+            pages_ref[layer, side, page] = jnp.where(spot == place, fresh, old).astype(BF16)
     head_of = iota((8, 512), 1) // HD == iota((8, 512), 0)
     sides = []
     for k in range(2):
@@ -290,8 +292,8 @@
         ],
         axis=0,
     ).astype(BF16)
-    keys = pages_ref[0, 0].reshape(8 * PAGE, 512)
-    values = pages_ref[0, 1].reshape(8 * PAGE, 512)
+    keys = pages_ref[layer, 0].reshape(8 * PAGE, 512)
+    values = pages_ref[layer, 1].reshape(8 * PAGE, 512)
     scores = dot_t(wide, keys) * HD ** (-0.5)
     page_of = iota((1, 256), 1) // PAGE
     owner = jnp.zeros((1, 256), jnp.int32)
@@ -319,29 +321,16 @@
 
 
 def attend(layer, meta, got, caches, pages=None):
-    block = pl.BlockSpec((1, 2, 8, PAGE, 512), lambda i: (layer, 0, 0, 0, 0))
-    whole = lambda shape: pl.BlockSpec(shape, lambda i: (0,) * len(shape))
-    specs = [pl.BlockSpec(memory_space=pltpu.SMEM), whole((32 * BACK, 128)), block]
-    args = [meta, near(got), caches]
-    aliases = {}
-    if pages is not None:
-        specs.append(pl.BlockSpec(memory_space=pl.ANY))
-        args.append(pages)
-        aliases = {3: 0}
-    return pl.pallas_call(
-        functools.partial(attend_kernel, pages is not None),
-        grid=(1,),
-        in_specs=specs,
-        out_specs=(block, whole((128, 128))),
-        out_shape=(
-            jax.ShapeDtypeStruct(caches.shape, BF16),
-            near_out((128, 128), F32),
-        ),
-        scratch_shapes=[pltpu.VMEM((32 * BACK, 128), F32), pltpu.VMEM((2, 4, 512), F32)],
-        input_output_aliases=aliases,
-        name="attend",
-        interpret=INTERPRET,
-    )(*args)
+    args = [got, caches] + ([] if pages is None else [pages])
+    return call(
+        functools.partial(attend_kernel, layer, pages is not None),
+        "attend",
+        (near_out(caches.shape, BF16), near_out((128, 128), F32)),
+        [pltpu.VMEM((32 * BACK, 128), F32), pltpu.VMEM((2, 4, 512), F32)],
+        meta,
+        *args,
+        aliases={} if pages is None else {3: 0},
+    )
 
 
 def join_kernel(got_ref, out_ref):
@@ -385,19 +374,19 @@
     )(near(got))
 
 
-def output_kernel(copies, att_ref, got_ref, wo_ref, wf_ref, out_ref, back):
+def output_kernel(layer, copies, meta_ref, att_ref, got_ref, wo_ref, wf_ref, out_ref, back):
     back[...] = got_ref[...].astype(F32)
     att = att_ref[...].astype(F32)
     att = att + pltpu.roll(att, HD, 1)
     att = jnp.concatenate([att] * 4, axis=1)
     own = iota((32, 512), 1) // HD == iota((32, 512), 0) % 8
-    by_head = dot_t(jnp.where(own, att, 0.0).astype(BF16), wo_ref[0])
+    by_head = dot_t(jnp.where(own, att, 0.0).astype(BF16), wo_ref[layer])
     chunk = iota((32, D), 1) // 128 == iota((32, D), 0) // 2
     mlp = []
     for k in range(2):
         act = back[pl.ds(3 + k, 32, stride=BACK), :]
         act = jnp.concatenate([act] * 16, axis=1)
-        mlp.append(dot_t(jnp.where(chunk, act, 0.0).astype(BF16), wf_ref[0]))
+        mlp.append(dot_t(jnp.where(chunk, act, 0.0).astype(BF16), wf_ref[layer]))
     odd = iota((32, HD), 0) % 2
     rows = []
     for i in range(4):
@@ -410,23 +399,18 @@
         out_ref[4 * k : 4 * k + 4] = tile
 
 
-def output(layer, copies, att, got, w_out, w_fc2):
-    whole = lambda shape: pl.BlockSpec(shape, lambda i: (0,) * len(shape))
-    return pl.pallas_call(
-        functools.partial(output_kernel, copies),
-        grid=(1,),
-        in_specs=[
-            whole((32, 128)),
-            whole((32 * BACK, 128)),
-            pl.BlockSpec((1, HD, 512), lambda i: (layer, 0, 0)),
-            pl.BlockSpec((1, HD, D), lambda i: (layer, 0, 0)),
-        ],
-        out_specs=whole((4 * copies, 128)),
-        out_shape=near_out((4 * copies, 128), F32),
-        scratch_shapes=[pltpu.VMEM((32 * BACK, 128), F32)],
-        name="output",
-        interpret=INTERPRET,
-    )(near(att), near(got), w_out, w_fc2)
+def output(layer, copies, meta, att, got, w_out, w_fc2):
+    return call(
+        functools.partial(output_kernel, layer, copies),
+        "output",
+        near_out((4 * copies, 128), F32),
+        [pltpu.VMEM((32 * BACK, 128), F32)],
+        meta,
+        att,
+        got,
+        w_out,
+        w_fc2,
+    )
 
 
 def per_device(
@@ -449,41 +433,29 @@
     pairs = [[2 * z, 2 * z + 1] for z in range(16)]
     rep_core = [[r * 32 + 2 * z + c for r in range(4) for c in range(2)] for z in range(16)]
 
-    first = jnp.concatenate(
-        [hidden.astype(F32), jnp.broadcast_to(positions.astype(F32)[:, None], (4, 64))], axis=1
-    )
+    first = jnp.concatenate([hidden.astype(F32), rope_factors(positions)], axis=1)
     first = spread(first, 4, "rep").reshape(16, 128)
-    q_row = (blk % 8) * 2
-    kv_row = rep * 4 + blk % 4
-    fc_row = rep * 4 + (blk % 2) * 2
-    rows = jnp.stack([q_row, q_row + 1, kv_row, fc_row, fc_row + 1])
-    pick = rows[:3, None] == jnp.arange(16)[None, :]
-    pick = pick & ((jnp.arange(3) < 2) | (blk // 4 < 4))[:, None]
-    table = rope_tables(jnp.sum(jnp.where(pick, first[:, 64][None], 0.0), axis=1))
-    meta = jnp.stack(
-        [page_owner, page_used, page_fill, page_tail, jnp.full((8,), rep * 4, jnp.int32)]
-    )
-    rep_one = rep.reshape(1)
+    place = jnp.where(jnp.arange(8) == 0, rep, blk).astype(jnp.int32)
+    meta = jnp.stack([page_owner, page_used, page_fill, page_tail, place])
     w_qkv = w_qkv.transpose(0, 2, 1, 3)
     w_out = w_out.transpose(0, 2, 1)
     w_fc2 = w_fc2.transpose(0, 2, 1)
-    gains = [ln_gain[layer : layer + 1] for layer in range(LAYERS)]
 
     state, branch, pages = first, None, None
     for layer in range(LAYERS):
-        send, state = project(layer, rep_one, state, gains[layer], w_qkv, w_fc1, branch)
+        send, state = project(layer, meta, state, ln_gain, w_qkv, w_fc1, branch)
         got = exchange(send.reshape(32, WIRE // 2, 2, 128), "blk").reshape(32 * WIRE, 128)
-        back = finish(rows, got, table)
+        back = finish(meta, got, first)
         got = exchange(back.reshape(32, BACK // 2, 2, 128), "blk").reshape(32 * BACK, 128)
         pages, parts = attend(layer, meta, got, caches, pages)
         parts = exchange(parts.reshape(8, 16, 128), ("rep", "blk"), rep_core)
         parts = exchange(join(parts), "blk", zs)
         att = lax.all_gather(settle(parts), "blk", axis_index_groups=pairs, tiled=True)
         if layer + 1 < LAYERS:
-            out = output(layer, 16, att, got, w_out, w_fc2).reshape(16, 4, 128)
+            out = output(layer, 16, meta, att, got, w_out, w_fc2).reshape(16, 4, 128)
             branch = exchange(out, ("rep", "tp")).reshape(64, 128)
         else:
-            out = output(layer, 4, att, got, w_out, w_fc2).reshape(4, 4, 128)
+            out = output(layer, 4, meta, att, got, w_out, w_fc2).reshape(4, 4, 128)
             branch = jnp.sum(exchange(out, "tp"), axis=0)[:, :HD]
             own = lax.dynamic_slice(state, (rep * 4, 0), (4, HD))
             result = (own + branch).astype(BF16)

time: 183 us -> 181 us (0.989)
  blocking collectives: 98.7 us -> 147 us
  waiting for transfers between devices: 31.7 us -> 6.6 us
  starting transfers between devices: 30.9 us -> 8.24 us
  Pallas kernels: 14.9 us -> 9.89 us
  local copies, waits for them, and re-layouts: 3.39 us -> 5.71 us
    all_to_all x7 -> x9, blocking collectives: 91.7 us -> 140 us  [exchange(): lax.all_to_all(value, axis, 0, 0, tiled=True, axis_index_groups=groups)]
    all_to_all x4 -> x2, waiting for transfers between devices: 31.7 us -> 6.6 us  [exchange(): lax.all_to_all(value, axis, 0, 0, tiled=True, axis_index_groups=groups)]
    all_to_all x4 -> x2, starting transfers between devices: 30.9 us -> 8.24 us  [exchange(): lax.all_to_all(value, axis, 0, 0, tiled=True, axis_index_groups=groups)]
    pallas_call x8, Pallas kernels: 14 us -> 8.94 us  [call(): pl.pallas_call(kernel, in_specs=specs, out_specs=jax.tree.map(lambda _: p...]
    unnamed x12 -> x19, local copies, waits for them, and re-layouts: 1.33 us -> 4.38 us
  transfers between devices with their start and end apart: 4 -> 2, of which waited for: 4 -> 2; matrix products, arithmetic and copies ran while one was open for 1% -> 1% of each run, Pallas kernels for 0% -> 0%
where the time goes in v4:
time: 181 us; the launch traced here: 180 us
  blocking collectives  147 us (81%)
  Pallas kernels  9.89 us (5%)
  starting transfers between devices  8.24 us (5%)
  waiting for transfers between devices  6.6 us (4%)
  local copies, waits for them, and re-layouts  5.71 us (3%)
  other arithmetic  2.22 us (1%)
    all_to_all x9, blocking collectives, exchange(): lax.all_to_all(value, axis, 0, 0, tiled=True, axis_index_groups=groups)  140 us
    pallas_call x8, Pallas kernels, call(): pl.pallas_call(kernel, in_specs=specs, out_specs=jax.tree.map(lambda _: p...  8.94 us
    all_to_all x2, starting transfers between devices, exchange(): lax.all_to_all(value, axis, 0, 0, tiled=True, axis_index_groups=groups)  8.24 us
    all_gather x2, blocking collectives, per_device(): lax.all_gather(settle(parts), 'blk', axis_index_groups=pairs, tiled=True)  7.04 us
    all_to_all x2, waiting for transfers between devices, exchange(): lax.all_to_all(value, axis, 0, 0, tiled=True, axis_index_groups=groups)  6.6 us
    unnamed x19, local copies, waits for them, and re-layouts  4.38 us
  transfers between devices with their start and end apart: 2, of which 2 were waited for; matrix products, arithmetic and copies ran while one was open for 1% of the time, Pallas kernels for 0%

profile of v4, /device:TPU:1, one launch (start us, length us, event | category | flops | bytes accessed | tf_op | source)
XLA Modules:
  0.0 180.1 jit_solution(589571667993833015)
XLA Ops:
  0.7 0.7 convert_element_type.17
  1.4 0.7 convert_element_type.16
  2.3 0.6 broadcast_in_dim.27
  2.9 5.0 %all-to-all-start = ((f32[4,4,128]{2,1,0:T(4,128)}), f32[4,4,128]{2,1,0:T(4,128)S(1)}, u32[]{:S(2)}, u32[]{:S(2)}) async-start(f32[4,4,128]{2,1,0:T(4,128)} %broadcast_in_dim.27), calls=%async_computation | async-start | bytes 16384 | tf_op jit(solution)/shard_map/all_to_all | solution.py:26
  7.9 0.7 stack.20.meta_ref
  8.6 3.4 %all-to-all-done = f32[4,4,128]{2,1,0:T(4,128)S(1)} async-done(((f32[4,4,128]{2,1,0:T(4,128)}), f32[4,4,128]{2,1,0:T(4,128)S(1)}, u32[]{:S(2)}, u32[]{:S(2)}) %all-to-all-start) | async-done | bytes 8224 | tf_op jit(solution)/shard_map/all_to_all | solution.py:26
  12.1 1.0 copy-done.1
  13.1 1.0 copy-done.4
  14.1 0.7 copy-done.7
  14.8 1.1 project.2
  15.9 30.9 %all_to_all.55 = bf16[32,5,2,128]{3,2,1,0:T(2,128)(2,1)S(1)} all-to-all(bf16[32,5,2,128]{3,2,1,0:T(2,128)(2,1)S(1)} %bitcast.41), channel_id=1, replica_groups=mesh['rep'=4,'blk'=32,'tp'=4] {'blk'}, dimensions={0} | all-to-all | bytes 163840 | tf_op jit(solution)/shard_map/all_to_all | solution.py:26
  46.7 0.9 finish.2
  47.7 17.0 %all_to_all.56 = bf16[32,3,2,128]{3,2,1,0:T(2,128)(2,1)S(1)} all-to-all(bf16[32,3,2,128]{3,2,1,0:T(2,128)(2,1)S(1)} %bitcast.34), channel_id=1, replica_groups=mesh['rep'=4,'blk'=32,'tp'=4] {'blk'}, dimensions={0} | all-to-all | bytes 98304 | tf_op jit(solution)/shard_map/all_to_all | solution.py:26
  64.6 1.2 attend.2
  65.8 8.5 %all_to_all.57.got_ref = f32[8,16,128]{2,1,0:T(8,128)S(1)} all-to-all(f32[8,16,128]{2,1,0:T(8,128)S(1)} %bitcast.43), channel_id=1, replica_groups={{0,4,128,132,256,260,384,388},{8,12,136,140,264,268,392,396},{16,20,144..., dimensions={0} | all-to-all | bytes 131072 | tf_op jit(solution)/shard_map/all_to_all | solution.py:26
  74.6 14.4 %all_to_all.58.got_ref = bf16[16,16,128]{2,1,0:T(8,128)(2,1)S(1)} all-to-all(bf16[16,16,128]{2,1,0:T(8,128)(2,1)S(1)} %join.2), channel_id=1, replica_groups={{0,8,16,24,32,40,48,56,64,72,80,88,96,104,112,120},{4,12,20,28,36,44,52..., dimensions={0} | all-to-all | bytes 131072 | tf_op jit(solution)/shard_map/all_to_all | solution.py:26
  89.2 3.5 %all_gather.6.att_ref = bf16[32,128]{1,0:T(8,128)(2,1)S(1)} all-gather(bf16[16,128]{1,0:T(8,128)(2,1)S(1)} %settle.2), channel_id=1, replica_groups={{0,4},{8,12},{16,20},{24,28},{32,36},{40,44},{48,52},{56,60},{64,68},{7..., dimensions={0}, use_global_device_ids=true | all-gather | bytes 12288 | tf_op jit(solution)/shard_map/all_gather | solution.py:453
  92.8 0.9 output.2
  93.7 11.0 %all_to_all.59 = f32[16,4,128]{2,1,0:T(4,128)S(1)} all-to-all(f32[16,4,128]{2,1,0:T(4,128)S(1)} %bitcast.39), channel_id=1, replica_groups=mesh['rep'=4,'blk'=32,'tp'=4] {'rep','tp'}, dimensions={0} | all-to-all | bytes 65536 | tf_op jit(solution)/shard_map/all_to_all | solution.py:26
  104.7 0.7 copy-done.8
  105.4 1.1 project.3
  106.5 18.3 %all_to_all.60 = bf16[32,5,2,128]{3,2,1,0:T(2,128)(2,1)S(1)} all-to-all(bf16[32,5,2,128]{3,2,1,0:T(2,128)(2,1)S(1)} %bitcast.40), channel_id=1, replica_groups=mesh['rep'=4,'blk'=32,'tp'=4] {'blk'}, dimensions={0} | all-to-all | bytes 163840 | tf_op jit(solution)/shard_map/all_to_all | solution.py:26
  124.7 0.9 finish.3
  125.7 17.0 %all_to_all.61 = bf16[32,3,2,128]{3,2,1,0:T(2,128)(2,1)S(1)} all-to-all(bf16[32,3,2,128]{3,2,1,0:T(2,128)(2,1)S(1)} %bitcast.33), channel_id=1, replica_groups=mesh['rep'=4,'blk'=32,'tp'=4] {'blk'}, dimensions={0} | all-to-all | bytes 98304 | tf_op jit(solution)/shard_map/all_to_all | solution.py:26
  142.6 1.2 attend.3
  143.8 8.5 %all_to_all.62.got_ref = f32[8,16,128]{2,1,0:T(8,128)S(1)} all-to-all(f32[8,16,128]{2,1,0:T(8,128)S(1)} %bitcast.42), channel_id=1, replica_groups={{0,4,128,132,256,260,384,388},{8,12,136,140,264,268,392,396},{16,20,144..., dimensions={0} | all-to-all | bytes 131072 | tf_op jit(solution)/shard_map/all_to_all | solution.py:26
  152.6 14.2 %all_to_all.63.got_ref = bf16[16,16,128]{2,1,0:T(8,128)(2,1)S(1)} all-to-all(bf16[16,16,128]{2,1,0:T(8,128)(2,1)S(1)} %join.3), channel_id=1, replica_groups={{0,8,16,24,32,40,48,56,64,72,80,88,96,104,112,120},{4,12,20,28,36,44,52..., dimensions={0} | all-to-all | bytes 131072 | tf_op jit(solution)/shard_map/all_to_all | solution.py:26
  167.1 3.5 %all_gather.7.att_ref = bf16[32,128]{1,0:T(8,128)(2,1)S(1)} all-gather(bf16[16,128]{1,0:T(8,128)(2,1)S(1)} %settle.3), channel_id=1, replica_groups={{0,4},{8,12},{16,20},{24,28},{32,36},{40,44},{48,52},{56,60},{64,68},{7..., dimensions={0}, use_global_device_ids=true | all-gather | bytes 12288 | tf_op jit(solution)/shard_map/all_gather | solution.py:453
  170.6 1.5 output.3
  172.2 3.2 %all-to-all-start.10 = ((f32[4,4,128]{2,1,0:T(4,128)}), f32[4,4,128]{2,1,0:T(4,128)S(1)}, u32[]{:S(2)}, u32[]{:S(2)}) async-start(f32[4,4,128]{2,1,0:T(4,128)} %bitcast.20), calls=%async_computation.10 | async-start | bytes 16384 | tf_op jit(solution)/shard_map/all_to_all | solution.py:26
  175.4 1.0 copy.16
  176.4 3.2 %all-to-all-done.10 = f32[4,4,128]{2,1,0:T(4,128)S(1)} async-done(((f32[4,4,128]{2,1,0:T(4,128)}), f32[4,4,128]{2,1,0:T(4,128)S(1)}, u32[]{:S(2)}, u32[]{:S(2)}) %all-to-all-start.10) | async-done | bytes 8224 | tf_op jit(solution)/shard_map/all_to_all | solution.py:26
  (25 shorter events, 1.8 us)
Async XLA Ops:
  0.6 64.0 %copy-start = (bf16[2,2,8,32,512]{4,3,2,1,0:T(8,128)(2,1)S(1)}, bf16[2,2,8,32,512]{4,3,2,1,0:T(8,128)(2,1)}, u32[]{:S(2)}) copy-start(bf16[2,2,8,32,512]{4,3,2,1,0:T(8,128)(2,1)} %cache_ref.3) | copy-start | bytes 3145732
  2.9 9.2 %all-to-all-start = ((f32[4,4,128]{2,1,0:T(4,128)}), f32[4,4,128]{2,1,0:T(4,128)S(1)}, u32[]{:S(2)}, u32[]{:S(2)}) async-start(f32[4,4,128]{2,1,0:T(4,128)} %broadcast_in_dim.27), calls=%async_computation | async-start | bytes 16384 | tf_op jit(solution)/shard_map/all_to_all | solution.py:26
  12.1 1.0 copy-start.1
  13.1 1.0 copy-start.4
  14.1 0.7 copy-start.7
  64.6 28.1 %copy-start.3 = (bf16[2,2048,64]{1,2,0:T(8,128)(2,1)S(1)}, bf16[2,2048,64]{1,2,0:T(8,128)(2,1)}, u32[]{:S(2)}) copy-start(bf16[2,2048,64]{1,2,0:T(8,128)(2,1)} %param.17) | copy-start | bytes 1572868
  74.4 18.4 %copy-start.6 = (bf16[2,512,64]{1,2,0:T(8,128)(2,1)S(1)}, bf16[2,512,64]{1,2,0:T(8,128)(2,1)}, u32[]{:S(2)}) copy-start(bf16[2,512,64]{1,2,0:T(8,128)(2,1)} %param.16) | copy-start | bytes 393220
  74.6 30.1 %copy-start.2 = (bf16[2,64,2048]{2,1,0:T(8,128)(2,1)S(1)}, bf16[2,64,2048]{2,1,0:T(8,128)(2,1)}, u32[]{:S(2)}) copy-start(bf16[2,64,2048]{2,1,0:T(8,128)(2,1)} %refs_3_.3) | copy-start | bytes 1572868
  92.8 11.9 %copy-start.5 = (bf16[2,64,3,512]{3,1,2,0:T(8,128)(2,1)S(1)}, bf16[2,64,3,512]{3,1,2,0:T(8,128)(2,1)}, u32[]{:S(2)}) copy-start(bf16[2,64,3,512]{3,1,2,0:T(8,128)(2,1)} %param.14) | copy-start | bytes 1179652
  104.7 0.7 copy-start.8
  172.2 7.4 %all-to-all-start.10 = ((f32[4,4,128]{2,1,0:T(4,128)}), f32[4,4,128]{2,1,0:T(4,128)S(1)}, u32[]{:S(2)}, u32[]{:S(2)}) async-start(f32[4,4,128]{2,1,0:T(4,128)} %bitcast.20), calls=%async_computation.10 | async-start | bytes 16384 | tf_op jit(solution)/shard_map/all_to_all | solution.py:26

commit v5 on v4

--- a/solution.py
+++ b/solution.py
@@ -19,6 +19,7 @@
 BF16 = jnp.bfloat16
 INTERPRET = False
 WIRE = 10
+CUT = 896
 BACK = 6
 
 
@@ -67,21 +68,30 @@
     return found
 
 
-def project_kernel(layer, with_branch, meta_ref, *refs):
-    if with_branch:
-        x_ref, gain_ref, wq_ref, wf_ref, branch_ref, send_ref, state_ref, wire = refs
-        sums = []
-        for rep in range(4):
-            total = branch_ref[rep * 16 : rep * 16 + 4, :HD]
-            for tp in range(1, 4):
-                start = rep * 16 + tp * 4
-                total = total + branch_ref[start : start + 4, :HD]
-            sums.append(total)
-        x = (x_ref[:, :HD] + jnp.concatenate(sums, axis=0)).astype(BF16).astype(F32)
-    else:
-        x_ref, gain_ref, wq_ref, wf_ref, send_ref, state_ref, wire = refs
-        x = x_ref[:, :HD]
-    state_ref[...] = jnp.concatenate([x, jnp.zeros_like(x)], axis=1)
+def rope(value, factors, turned):
+    lane = iota(value.shape, 1)
+    left = lane < HD
+    half = ROT // 2
+    cosine = jnp.where(left, pltpu.roll(factors, 64, 1), factors)
+    sine = jnp.where(left, pltpu.roll(factors, 32, 1), pltpu.roll(factors, 96, 1))
+    other = jnp.where(
+        lane % HD < half, pltpu.roll(value, 128 - half, 1), pltpu.roll(value, half, 1)
+    )
+    return jnp.where(turned & (lane % HD < ROT), value * cosine + other * sine, value)
+
+
+def gelu(value):
+    cubed = value * value * value
+    return 0.5 * value * (1.0 + jnp.tanh(math.sqrt(2.0 / math.pi) * (value + 0.044715 * cubed)))
+
+
+def project_kernel(meta_ref, x_ref, gain_ref, wq_ref, wf_ref, send_ref, cut_ref, wire):
+    layer = 0
+    quarter = pl.multiple_of(meta_ref[4, 0] * 128, 128)
+    for k in range(3):
+        cut_ref[:, 128 * k : 128 * k + 128] = wq_ref[1, k, :, pl.ds(quarter, 128)]
+    cut_ref[:, 384:] = wf_ref[1, :, pl.ds(pl.multiple_of(meta_ref[4, 0] * 512, 512), 512)]
+    x = x_ref[:, :HD]
     gain = gain_ref[layer : layer + 1]
     mean = jnp.sum(x, axis=1, keepdims=True) * (1.0 / HD)
     centered = x - mean
@@ -155,6 +165,7 @@
     for k, part in enumerate(parts_of(mean, 3) + parts_of(square, 3)):
         stats = jnp.where(lane == request + 16 * k, part, stats)
     stats = jnp.sum(stats, axis=0, keepdims=True)
+    later = jnp.concatenate(parts_of(gain_ref[1:2], 2), axis=1)
     pieces = [
         stack_q(every_q[0:8]),
         stack_q(every_q[8:16]),
@@ -165,7 +176,7 @@
         stack_kv(every_kv[24:32]),
         stack_fc(every_fc[16:24]),
         jnp.broadcast_to(stats, (32, 128)),
-        jnp.zeros((32, 128), F32),
+        jnp.broadcast_to(later, (32, 128)),
     ]
     for k, piece in enumerate(pieces):
         wire[pl.ds(k, 32, stride=WIRE), :] = piece
@@ -189,19 +200,21 @@
     )(meta, *[near(arg) for arg in args])
 
 
-def project(layer, meta, x, gain, wq, wf, branch=None):
-    args = [x, gain, wq, wf] + ([] if branch is None else [branch])
+def project(meta, x, gain, wq, wf):
     return call(
-        functools.partial(project_kernel, layer, branch is not None),
+        project_kernel,
         "project",
-        (near_out((32 * WIRE, 128), BF16), near_out((16, 128), F32)),
+        (near_out((32 * WIRE, 128), BF16), near_out((HD, CUT), BF16)),
         [pltpu.VMEM((32 * WIRE, 128), F32)],
         meta,
-        *args,
-    )
-
-
-def finish_kernel(meta_ref, got_ref, first_ref, out_ref, wire, back):
+        x,
+        gain,
+        wq,
+        wf,
+    )
+
+
+def finish_kernel(meta_ref, got_ref, first_ref, out_ref, gain_ref, wire, back):
     rep, blk = meta_ref[4, 0], meta_ref[4, 1]
     q_row = (blk % 8) * 2
     fc_row = rep * 4 + (blk % 2) * 2
@@ -218,38 +231,32 @@
     lane = iota((32, 128), 1)
     lane_one = iota((1, 128), 1)
     columns = [take(5), take(6), take(7)]
-    half = ROT // 2
     for k, column in enumerate((0, 0, 1, 2, 2)):
         request = requests[k]
         row_offset = jnp.sum(jnp.where(lane == request, offset, 0.0), axis=1, keepdims=True)
         row_rstd = jnp.sum(jnp.where(lane_one == request, rstd, 0.0), axis=1, keepdims=True)
         value = row_rstd * jnp.sum(take(k) + row_offset * columns[column], axis=0, keepdims=True)
         if k < 3:
-            factors = first_ref[pl.ds(request, 1), :]
-            place = lane_one % HD
-            turned = place < ROT if k < 2 else (place < ROT) & (blk < 16)
-            left = lane_one < HD
-            cosine = jnp.where(left, pltpu.roll(factors, 64, 1), factors)
-            sine = jnp.where(left, pltpu.roll(factors, 32, 1), pltpu.roll(factors, 96, 1))
-            other = jnp.where(
-                place < half, pltpu.roll(value, 128 - half, 1), pltpu.roll(value, half, 1)
-            )
-            value = jnp.where(turned, value * cosine + other * sine, value)
+            turned = jnp.full((1, 128), True) if k < 2 else jnp.full((1, 128), blk) < 16
+            value = rope(value, first_ref[pl.ds(request, 1), :], turned)
         else:
-            cubed = value * value * value
-            value = (
-                0.5 * value * (1.0 + jnp.tanh(math.sqrt(2.0 / math.pi) * (value + 0.044715 * cubed)))
-            )
+            value = gelu(value)
         back[pl.ds(k, 32, stride=BACK), :] = jnp.broadcast_to(value, (32, 128))
     back[pl.ds(5, 32, stride=BACK), :] = jnp.zeros((32, 128), F32)
     out_ref[...] = back[...].astype(BF16)
+    later = take(9)
+    later = later + pltpu.roll(later, HD, 1)
+    for z in range(16):
+        gain_ref[:, 128 * z : 128 * z + 128] = jnp.where(
+            lane_one < HD, later[2 * z : 2 * z + 1], later[2 * z + 1 : 2 * z + 2]
+        )
 
 
 def finish(meta, got, first):
     return call(
         finish_kernel,
         "finish",
-        near_out((32 * BACK, 128), BF16),
+        (near_out((32 * BACK, 128), BF16), near_out((1, D), F32)),
         [pltpu.VMEM((32 * WIRE, 128), F32), pltpu.VMEM((32 * BACK, 128), F32)],
         meta,
         got,
@@ -257,20 +264,108 @@
     )
 
 
-def attend_kernel(layer, aliased, meta_ref, got_ref, cache_ref, *refs):
-    if aliased:
-        _, pages_ref, out_ref, back, kv = refs
-    else:
-        pages_ref, out_ref, back, kv = refs
+def renew_kernel(meta_ref, x_ref, branch_ref, out_ref, state_ref):
+    sums = []
+    for rep in range(4):
+        total = branch_ref[rep * 16 : rep * 16 + 4]
+        for tp in range(1, 4):
+            start = rep * 16 + tp * 4
+            total = total + branch_ref[start : start + 4]
+        sums.append(total)
+    x = (x_ref[...] + jnp.concatenate(sums, axis=0)).astype(BF16).astype(F32)
+    state_ref[...] = x
+    packed = jnp.where(iota((8, 128), 1) < HD, x[:8], pltpu.roll(x[8:], HD, 1)).astype(BF16)
+    out_ref[...] = jnp.broadcast_to(packed[None], (32, 8, 128))
+
+
+def renew(meta, x, branch):
+    return call(
+        renew_kernel,
+        "renew",
+        (near_out((32, 8, 128), BF16), near_out((16, 128), F32)),
+        [],
+        meta,
+        x,
+        branch,
+    )
+
+
+def deepen_kernel(meta_ref, got_ref, gain_ref, deep_ref, out_ref):
+    left = iota((8, 128), 1) < HD
+    tiles = []
+    for z in range(16):
+        even = got_ref[2 * z].astype(F32)
+        odd = got_ref[2 * z + 1].astype(F32)
+        top = jnp.where(left, even, pltpu.roll(odd, HD, 1))
+        bottom = jnp.where(left, pltpu.roll(even, HD, 1), odd)
+        tiles.append(jnp.concatenate([top, bottom], axis=0))
+    x = jnp.concatenate(tiles, axis=1)
+    average = jnp.sum(x, axis=1, keepdims=True) * (1.0 / D)
+    centered = x - average
+    variance = jnp.sum(centered * centered, axis=1, keepdims=True) * (1.0 / D)
+    normed = centered * lax.rsqrt(variance + EPSILON) * gain_ref[...]
+    low = iota((16, 128), 1) < HD
+    first_core = jnp.full((16, 128), meta_ref[4, 1] % 2) == 0
+    tiles = []
+    for pair in range(8):
+        one = normed[:, 256 * pair : 256 * pair + 128]
+        two = normed[:, 256 * pair + 128 : 256 * pair + 256]
+        tiles.append(
+            jnp.where(
+                first_core,
+                jnp.where(low, one, pltpu.roll(two, HD, 1)),
+                jnp.where(low, pltpu.roll(one, HD, 1), two),
+            )
+        )
+    mixed = dot32(jnp.concatenate(tiles, axis=1).astype(BF16), deep_ref[...])
+    for rep in range(4):
+        rows = mixed[4 * rep : 4 * rep + 4]
+        parts = [mixed[:, :128]] + [rows[:, 128 * k : 128 * k + 128] for k in range(1, 7)]
+        block = jnp.concatenate(parts, axis=0).astype(BF16)
+        for core in range(2):
+            out_ref[2 * rep + core] = block
+
+
+def deepen(meta, got, gain, deep):
+    return call(
+        deepen_kernel, "deepen", near_out((8, 40, 128), BF16), [], meta, got, gain, deep
+    )
+
+
+def gather_shallow(got_ref, back, kv):
     back[...] = got_ref[...].astype(F32)
     take = lambda k: back[pl.ds(k, 32, stride=BACK), :]
     new = take(2)
-    for j in range(4):
-        for part in range(2):
-            chunk = 2 * j + part
-            kv[chunk // 4, :, 128 * (chunk % 4) : 128 * (chunk % 4) + 128] = new[
-                8 * j + 4 * part : 8 * j + 4 * part + 4
-            ]
+    for chunk in range(8):
+        kv[chunk // 4, :, 128 * (chunk % 4) : 128 * (chunk % 4) + 128] = new[
+            4 * chunk : 4 * chunk + 4
+        ]
+    sides = []
+    for k in range(2):
+        tall = take(k)
+        sides.append(jnp.concatenate([tall[8 * j : 8 * j + 8] for j in range(4)], axis=1))
+    return [sides[i % 2][i // 2 : i // 2 + 1] for i in range(16)]
+
+
+def gather_deep(meta_ref, got_ref, first_ref, kv):
+    own = first_ref[pl.ds(meta_ref[4, 0] * 4, 4), :]
+    tiles = []
+    for r in range(4):
+        both = got_ref[2 * r, :24].astype(F32) + got_ref[2 * r + 1, :24].astype(F32)
+        tiles.append(rope(both[:16], first_ref[...], jnp.full((16, 128), True)))
+        kv[0, :, 128 * r : 128 * r + 128] = rope(both[16:20], own, jnp.full((4, 128), True))
+        kv[1, :, 128 * r : 128 * r + 128] = both[20:24]
+    queries = jnp.concatenate(tiles, axis=1)
+    return [queries[i : i + 1] for i in range(16)]
+
+
+def attend_kernel(layer, meta_ref, got_ref, cache_ref, *refs):
+    if layer == 0:
+        pages_ref, out_ref, back, kv = refs
+        queries = gather_shallow(got_ref, back, kv)
+    else:
+        first_ref, _, pages_ref, out_ref, kv = refs
+        queries = gather_deep(meta_ref, got_ref, first_ref, kv)
     spot = iota((PAGE, 512), 0)
     for side in range(2):
         for page in range(8):
@@ -280,17 +375,8 @@
             old = cache_ref[layer, side, page].astype(F32)
             pages_ref[layer, side, page] = jnp.where(spot == place, fresh, old).astype(BF16)
     head_of = iota((8, 512), 1) // HD == iota((8, 512), 0)
-    sides = []
-    for k in range(2):
-        tall = take(k)
-        sides.append(jnp.concatenate([tall[8 * j : 8 * j + 8] for j in range(4)], axis=1))
     wide = jnp.concatenate(
-        [
-            jnp.where(head_of, jnp.broadcast_to(sides[k][p : p + 1], (8, 512)), 0.0)
-            for p in range(8)
-            for k in range(2)
-        ],
-        axis=0,
+        [jnp.where(head_of, jnp.broadcast_to(row, (8, 512)), 0.0) for row in queries], axis=0
     ).astype(BF16)
     keys = pages_ref[layer, 0].reshape(8 * PAGE, 512)
     values = pages_ref[layer, 1].reshape(8 * PAGE, 512)
@@ -320,16 +406,18 @@
     )
 
 
-def attend(layer, meta, got, caches, pages=None):
-    args = [got, caches] + ([] if pages is None else [pages])
+def attend(layer, meta, got, caches, *more):
+    back = [pltpu.VMEM((32 * BACK, 128), F32)] if layer == 0 else []
     return call(
-        functools.partial(attend_kernel, layer, pages is not None),
+        functools.partial(attend_kernel, layer),
         "attend",
         (near_out(caches.shape, BF16), near_out((128, 128), F32)),
-        [pltpu.VMEM((32 * BACK, 128), F32), pltpu.VMEM((2, 4, 512), F32)],
+        back + [pltpu.VMEM((2, 4, 512), F32)],
         meta,
-        *args,
-        aliases={} if pages is None else {3: 0},
+        got,
+        caches,
+        *more,
+        aliases={} if layer == 0 else {4: 0},
     )
 
 
@@ -374,25 +462,34 @@
     )(near(got))
 
 
-def output_kernel(layer, copies, meta_ref, att_ref, got_ref, wo_ref, wf_ref, out_ref, back):
-    back[...] = got_ref[...].astype(F32)
+def output_kernel(layer, copies, meta_ref, att_ref, got_ref, wo_ref, wf_ref, out_ref, *scratch):
     att = att_ref[...].astype(F32)
     att = att + pltpu.roll(att, HD, 1)
     att = jnp.concatenate([att] * 4, axis=1)
     own = iota((32, 512), 1) // HD == iota((32, 512), 0) % 8
     by_head = dot_t(jnp.where(own, att, 0.0).astype(BF16), wo_ref[layer])
-    chunk = iota((32, D), 1) // 128 == iota((32, D), 0) // 2
-    mlp = []
-    for k in range(2):
-        act = back[pl.ds(3 + k, 32, stride=BACK), :]
-        act = jnp.concatenate([act] * 16, axis=1)
-        mlp.append(dot_t(jnp.where(chunk, act, 0.0).astype(BF16), wf_ref[layer]))
-    odd = iota((32, HD), 0) % 2
-    rows = []
-    for i in range(4):
-        from_mlp = jnp.sum(jnp.where(odd == i // 2, mlp[i % 2], 0.0), axis=0, keepdims=True)
-        from_att = jnp.sum(by_head[8 * i : 8 * i + 8], axis=0, keepdims=True)
-        rows.append(from_att + from_mlp)
+    rows = [jnp.sum(by_head[8 * i : 8 * i + 8], axis=0, keepdims=True) for i in range(4)]
+    if layer == 0:
+        back = scratch[0]
+        back[...] = got_ref[...].astype(F32)
+        chunk = iota((32, D), 1) // 128 == iota((32, D), 0) // 2
+        mlp = []
+        for k in range(2):
+            act = back[pl.ds(3 + k, 32, stride=BACK), :]
+            act = jnp.concatenate([act] * 16, axis=1)
+            mlp.append(dot_t(jnp.where(chunk, act, 0.0).astype(BF16), wf_ref[layer]))
+        odd = iota((32, HD), 0) % 2
+        rows = [
+            rows[i] + jnp.sum(jnp.where(odd == i // 2, mlp[i % 2], 0.0), axis=0, keepdims=True)
+            for i in range(4)
+        ]
+    else:
+        tiles = []
+        for r in range(4):
+            both = got_ref[2 * r, 24:].astype(F32) + got_ref[2 * r + 1, 24:].astype(F32)
+            tiles += [gelu(both[4 * k : 4 * k + 4]) for k in range(4)]
+        mlp = dot_t(jnp.concatenate(tiles, axis=1).astype(BF16), wf_ref[layer])
+        rows = [rows[i] + mlp[i : i + 1] for i in range(4)]
     tile = jnp.concatenate(rows, axis=0)
     tile = jnp.concatenate([tile, jnp.zeros_like(tile)], axis=1)
     for k in range(copies):
@@ -404,7 +501,7 @@
         functools.partial(output_kernel, layer, copies),
         "output",
         near_out((4 * copies, 128), F32),
-        [pltpu.VMEM((32 * BACK, 128), F32)],
+        [pltpu.VMEM((32 * BACK, 128), F32)] if layer == 0 else [],
         meta,
         att,
         got,
@@ -441,25 +538,27 @@
     w_out = w_out.transpose(0, 2, 1)
     w_fc2 = w_fc2.transpose(0, 2, 1)
 
-    state, branch, pages = first, None, None
-    for layer in range(LAYERS):
-        send, state = project(layer, meta, state, ln_gain, w_qkv, w_fc1, branch)
-        got = exchange(send.reshape(32, WIRE // 2, 2, 128), "blk").reshape(32 * WIRE, 128)
-        back = finish(meta, got, first)
-        got = exchange(back.reshape(32, BACK // 2, 2, 128), "blk").reshape(32 * BACK, 128)
-        pages, parts = attend(layer, meta, got, caches, pages)
+    def combine(parts):
         parts = exchange(parts.reshape(8, 16, 128), ("rep", "blk"), rep_core)
         parts = exchange(join(parts), "blk", zs)
-        att = lax.all_gather(settle(parts), "blk", axis_index_groups=pairs, tiled=True)
-        if layer + 1 < LAYERS:
-            out = output(layer, 16, meta, att, got, w_out, w_fc2).reshape(16, 4, 128)
-            branch = exchange(out, ("rep", "tp")).reshape(64, 128)
-        else:
-            out = output(layer, 4, meta, att, got, w_out, w_fc2).reshape(4, 4, 128)
-            branch = jnp.sum(exchange(out, "tp"), axis=0)[:, :HD]
-            own = lax.dynamic_slice(state, (rep * 4, 0), (4, HD))
-            result = (own + branch).astype(BF16)
-    return (result, pages)
+        return lax.all_gather(settle(parts), "blk", axis_index_groups=pairs, tiled=True)
+
+    send, cut = project(meta, first, ln_gain, w_qkv, w_fc1)
+    deep = lax.all_gather(cut, "blk", axis_index_groups=zs, tiled=True)
+    got = exchange(send.reshape(32, WIRE // 2, 2, 128), "blk").reshape(32 * WIRE, 128)
+    back, gain = finish(meta, got, first)
+    got = exchange(back.reshape(32, BACK // 2, 2, 128), "blk").reshape(32 * BACK, 128)
+    pages, parts = attend(0, meta, got, caches)
+    out = output(0, 16, meta, combine(parts), got, w_out, w_fc2).reshape(16, 4, 128)
+    branch = exchange(out, ("rep", "tp")).reshape(64, 128)
+
+    piece, state = renew(meta, first, branch)
+    got = exchange(deepen(meta, exchange(piece, "blk"), gain, deep), ("rep", "blk"), rep_core)
+    pages, parts = attend(1, meta, got, caches, first, pages)
+    out = output(1, 4, meta, combine(parts), got, w_out, w_fc2).reshape(4, 4, 128)
+    branch = jnp.sum(exchange(out, "tp"), axis=0)[:, :HD]
+    own = lax.dynamic_slice(state, (rep * 4, 0), (4, HD))
+    return ((own + branch).astype(BF16), pages)
 
 
 def solution(mesh):

time: 181 us -> 187 us (1.033)
  between operations: 0.75 us -> 14.1 us
  blocking collectives: 147 us -> 139 us
    all_to_all x9, blocking collectives: 140 us -> 132 us  [exchange(): lax.all_to_all(value, axis, 0, 0, tiled=True, axis_index_groups=groups)]
    unnamed x19 -> x15, local copies, waits for them, and re-layouts: 4.38 us -> 5.2 us
  transfers between devices with their start and end apart: 2 -> 3, of which waited for: 2 -> 2; matrix products, arithmetic and copies ran while one was open for 1% -> 1% of each run, Pallas kernels for 0% -> 2%
where the time goes in v5:
time: 187 us
  blocking collectives  139 us (74%)
  between operations  14.1 us (8%)
  Pallas kernels  10.4 us (6%)
  starting transfers between devices  8.26 us (4%)
  waiting for transfers between devices  6.61 us (4%)
  local copies, waits for them, and re-layouts  6.53 us (3%)
  other arithmetic  2.24 us (1%)
    all_to_all x9, blocking collectives, exchange(): lax.all_to_all(value, axis, 0, 0, tiled=True, axis_index_groups=groups)  132 us
    pallas_call x8, Pallas kernels, call(): pl.pallas_call(kernel, in_specs=specs, out_specs=jax.tree.map(lambda _: p...  9.49 us
    all_to_all x2, starting transfers between devices, exchange(): lax.all_to_all(value, axis, 0, 0, tiled=True, axis_index_groups=groups)  8.26 us
    all_gather x2, blocking collectives, combine(): lax.all_gather(settle(parts), 'blk', axis_index_groups=pairs, tiled=True)  6.95 us
    all_to_all x2, waiting for transfers between devices, exchange(): lax.all_to_all(value, axis, 0, 0, tiled=True, axis_index_groups=groups)  6.59 us
    unnamed x15, local copies, waits for them, and re-layouts  5.2 us
  transfers between devices with their start and end apart: 3, of which 2 were waited for; matrix products, arithmetic and copies ran while one was open for 1% of the time, Pallas kernels for 2%

profile of v5, /device:TPU:1, one launch (start us, length us, event | category | flops | bytes accessed | tf_op | source)
XLA Modules:
  0.0 186.7 jit_solution(12143165851607602581)
XLA Ops:
  7.2 0.8 convert_element_type.17
  8.0 0.7 convert_element_type.16
  8.8 0.6 broadcast_in_dim.27
  9.5 5.0 %all-to-all-start = ((f32[4,4,128]{2,1,0:T(4,128)}), f32[4,4,128]{2,1,0:T(4,128)S(1)}, u32[]{:S(2)}, u32[]{:S(2)}) async-start(f32[4,4,128]{2,1,0:T(4,128)} %broadcast_in_dim.27), calls=%async_computation | async-start | bytes 16384 | tf_op jit(solution)/shard_map/all_to_all | solution.py:27
  14.5 0.7 stack.20.meta_ref
  15.2 3.4 %all-to-all-done = f32[4,4,128]{2,1,0:T(4,128)S(1)} async-done(((f32[4,4,128]{2,1,0:T(4,128)}), f32[4,4,128]{2,1,0:T(4,128)S(1)}, u32[]{:S(2)}, u32[]{:S(2)}) %all-to-all-start) | async-done | bytes 8224 | tf_op jit(solution)/shard_map/all_to_all | solution.py:27
  18.6 1.0 copy-done.3
  19.7 1.0 copy-done.5
  20.7 0.7 copy-done.6
  21.4 1.6 project.1
  23.0 30.9 %all_to_all.55 = bf16[32,5,2,128]{3,2,1,0:T(2,128)(2,1)S(1)} all-to-all(bf16[32,5,2,128]{3,2,1,0:T(2,128)(2,1)S(1)} %bitcast.31), channel_id=1, replica_groups=mesh['rep'=4,'blk'=32,'tp'=4] {'blk'}, dimensions={0} | all-to-all | bytes 163840 | tf_op jit(solution)/shard_map/all_to_all | solution.py:27
  53.9 1.0 finish.1
  54.9 18.0 %all_to_all.56 = bf16[32,3,2,128]{3,2,1,0:T(2,128)(2,1)S(1)} all-to-all(bf16[32,3,2,128]{3,2,1,0:T(2,128)(2,1)S(1)} %bitcast.34), channel_id=1, replica_groups=mesh['rep'=4,'blk'=32,'tp'=4] {'blk'}, dimensions={0} | all-to-all | bytes 98304 | tf_op jit(solution)/shard_map/all_to_all | solution.py:27
  72.9 1.2 attend.2
  74.1 7.8 %all_to_all.57.got_ref = f32[8,16,128]{2,1,0:T(8,128)S(1)} all-to-all(f32[8,16,128]{2,1,0:T(8,128)S(1)} %bitcast.33), channel_id=1, replica_groups={{0,4,128,132,256,260,384,388},{8,12,136,140,264,268,392,396},{16,20,144..., dimensions={0} | all-to-all | bytes 131072 | tf_op jit(solution)/shard_map/all_to_all | solution.py:27
  82.1 14.1 %all_to_all.58.got_ref = bf16[16,16,128]{2,1,0:T(8,128)(2,1)S(1)} all-to-all(bf16[16,16,128]{2,1,0:T(8,128)(2,1)S(1)} %join.2), channel_id=1, replica_groups={{0,8,16,24,32,40,48,56,64,72,80,88,96,104,112,120},{4,12,20,28,36,44,52..., dimensions={0} | all-to-all | bytes 131072 | tf_op jit(solution)/shard_map/all_to_all | solution.py:27
  96.6 3.4 %all_gather.9.att_ref = bf16[32,128]{1,0:T(8,128)(2,1)S(1)} all-gather(bf16[16,128]{1,0:T(8,128)(2,1)S(1)} %settle.2), channel_id=1, replica_groups={{0,4},{8,12},{16,20},{24,28},{32,36},{40,44},{48,52},{56,60},{64,68},{7..., dimensions={0}, use_global_device_ids=true | all-gather | bytes 12288 | tf_op jit(solution)/shard_map/all_gather | solution.py:544
  100.0 0.9 output.2
  101.0 11.7 %all_to_all.59 = f32[16,4,128]{2,1,0:T(4,128)S(1)} all-to-all(f32[16,4,128]{2,1,0:T(4,128)S(1)} %bitcast.29), channel_id=1, replica_groups=mesh['rep'=4,'blk'=32,'tp'=4] {'rep','tp'}, dimensions={0} | all-to-all | bytes 65536 | tf_op jit(solution)/shard_map/all_to_all | solution.py:27
  112.7 0.7 renew.1
  113.4 17.9 %all_to_all.60.got_ref = bf16[32,8,128]{2,1,0:T(8,128)(2,1)S(1)} all-to-all(bf16[32,8,128]{2,1,0:T(8,128)(2,1)S(1)} %get-tuple-element.16), channel_id=1, replica_groups=mesh['rep'=4,'blk'=32,'tp'=4] {'blk'}, dimensions={0} | all-to-all | bytes 131072 | tf_op jit(solution)/shard_map/all_to_all | solution.py:27
  131.3 1.5 copy-done.2
  132.8 1.3 deepen.1
  134.0 8.9 %all_to_all.61.got_ref = bf16[8,40,128]{2,1,0:T(8,128)(2,1)S(1)} all-to-all(bf16[8,40,128]{2,1,0:T(8,128)(2,1)S(1)} %deepen.1), channel_id=1, replica_groups={{0,4,128,132,256,260,384,388},{8,12,136,140,264,268,392,396},{16,20,144..., dimensions={0} | all-to-all | bytes 163840 | tf_op jit(solution)/shard_map/all_to_all | solution.py:27
  142.9 1.3 attend.3
  144.2 8.0 %all_to_all.62.got_ref = f32[8,16,128]{2,1,0:T(8,128)S(1)} all-to-all(f32[8,16,128]{2,1,0:T(8,128)S(1)} %bitcast.32), channel_id=1, replica_groups={{0,4,128,132,256,260,384,388},{8,12,136,140,264,268,392,396},{16,20,144..., dimensions={0} | all-to-all | bytes 131072 | tf_op jit(solution)/shard_map/all_to_all | solution.py:27
  152.4 14.2 %all_to_all.63.got_ref = bf16[16,16,128]{2,1,0:T(8,128)(2,1)S(1)} all-to-all(bf16[16,16,128]{2,1,0:T(8,128)(2,1)S(1)} %join.3), channel_id=1, replica_groups={{0,8,16,24,32,40,48,56,64,72,80,88,96,104,112,120},{4,12,20,28,36,44,52..., dimensions={0} | all-to-all | bytes 131072 | tf_op jit(solution)/shard_map/all_to_all | solution.py:27
  166.9 3.5 %all_gather.11.att_ref = bf16[32,128]{1,0:T(8,128)(2,1)S(1)} all-gather(bf16[16,128]{1,0:T(8,128)(2,1)S(1)} %settle.3), channel_id=1, replica_groups={{0,4},{8,12},{16,20},{24,28},{32,36},{40,44},{48,52},{56,60},{64,68},{7..., dimensions={0}, use_global_device_ids=true | all-gather | bytes 12288 | tf_op jit(solution)/shard_map/all_gather | solution.py:544
  170.5 1.5 output.3
  171.9 3.2 %all-to-all-start.10 = ((f32[4,4,128]{2,1,0:T(4,128)}), f32[4,4,128]{2,1,0:T(4,128)S(1)}, u32[]{:S(2)}, u32[]{:S(2)}) async-start(f32[4,4,128]{2,1,0:T(4,128)} %bitcast.16), calls=%async_computation.10 | async-start | bytes 16384 | tf_op jit(solution)/shard_map/all_to_all | solution.py:27
  175.2 1.0 copy.16
  176.2 3.2 %all-to-all-done.10 = f32[4,4,128]{2,1,0:T(4,128)S(1)} async-done(((f32[4,4,128]{2,1,0:T(4,128)}), f32[4,4,128]{2,1,0:T(4,128)S(1)}, u32[]{:S(2)}, u32[]{:S(2)}) %all-to-all-start.10) | async-done | bytes 8224 | tf_op jit(solution)/shard_map/all_to_all | solution.py:27
  (24 shorter events, 1.8 us)
Async XLA Ops:
  7.2 65.7 %copy-start = (bf16[2,2,8,32,512]{4,3,2,1,0:T(8,128)(2,1)S(1)}, bf16[2,2,8,32,512]{4,3,2,1,0:T(8,128)(2,1)}, u32[]{:S(2)}) copy-start(bf16[2,2,8,32,512]{4,3,2,1,0:T(8,128)(2,1)} %cache_ref.3) | copy-start | bytes 3145732
  7.2 92.8 %copy-start.1 = (bf16[2,2048,64]{1,2,0:T(8,128)(2,1)S(1)}, bf16[2,2048,64]{1,2,0:T(8,128)(2,1)}, u32[]{:S(2)}) copy-start(bf16[2,2048,64]{1,2,0:T(8,128)(2,1)} %param.17) | copy-start | bytes 1572868
  9.5 9.2 %all-to-all-start = ((f32[4,4,128]{2,1,0:T(4,128)}), f32[4,4,128]{2,1,0:T(4,128)S(1)}, u32[]{:S(2)}, u32[]{:S(2)}) async-start(f32[4,4,128]{2,1,0:T(4,128)} %broadcast_in_dim.27), calls=%async_computation | async-start | bytes 16384 | tf_op jit(solution)/shard_map/all_to_all | solution.py:27
  14.5 116.8 %all-gather.2.cloned.1.call-start = ((), (), s32[]{:S(2)}) async-start(), calls=%async_computation.11 | async-start | bytes 1949696 | tf_op jit(solution)/shard_map/all_gather | solution.py:547
  18.6 1.0 copy-start.3
  19.7 1.0 copy-start.5
  20.7 0.7 copy-start.6
  21.4 78.7 %copy-start.4 = (bf16[2,512,64]{1,2,0:T(8,128)(2,1)S(1)}, bf16[2,512,64]{1,2,0:T(8,128)(2,1)}, u32[]{:S(2)}) copy-start(bf16[2,512,64]{1,2,0:T(8,128)(2,1)} %param.16) | copy-start | bytes 393220
  131.3 1.5 copy-start.2
  171.9 7.4 %all-to-all-start.10 = ((f32[4,4,128]{2,1,0:T(4,128)}), f32[4,4,128]{2,1,0:T(4,128)S(1)}, u32[]{:S(2)}, u32[]{:S(2)}) async-start(f32[4,4,128]{2,1,0:T(4,128)} %bitcast.16), calls=%async_computation.10 | async-start | bytes 16384 | tf_op jit(solution)/shard_map/all_to_all | solution.py:27
Sparse Core Ops, SparseCore 0:
  23.1 70.1 all-gather.1

commit v6 on v4

v6 whole, which is shorter than its diff:
```python
import functools
import math

import jax
import jax.numpy as jnp
from jax import lax
from jax.experimental import pallas as pl
from jax.experimental.pallas import tpu as pltpu
from jax.sharding import PartitionSpec as P

D = 2048
HD = 64
ROT = 32
LAYERS = 2
PAGE = 32
EPSILON = 1e-05
LOWEST = -1e30
F32 = jnp.float32
BF16 = jnp.bfloat16
INTERPRET = False
HALF = 296
FLOW = 64
JOIN = 18


def exchange(value, axis, groups=None):
    return lax.all_to_all(value, axis, 0, 0, tiled=True, axis_index_groups=groups)


def spread(value, count, axis, groups=None):
    return exchange(jnp.broadcast_to(value[None], (count,) + value.shape), axis, groups)


def rope_factors(positions):
    lane = jnp.arange(64, dtype=jnp.int32)
    steps_f = (lane % (ROT // 2)).astype(F32)
    angles = positions.astype(F32)[:, None] * (10000.0 ** (-2.0 * steps_f / ROT))[None, :]
    sine = jnp.sin(angles)
    return jnp.where(lane < 32, jnp.cos(angles), jnp.where(lane < 48, -sine, sine))


def near(value):
    return value if INTERPRET else pltpu.with_memory_space_constraint(value, pltpu.VMEM)


def near_out(shape, dtype):
    return jax.ShapeDtypeStruct(shape, dtype) if INTERPRET else pltpu.VMEM(shape, dtype)


def iota(shape, axis):
    return lax.broadcasted_iota(jnp.int32, shape, axis)


def dot32(left, right):
    return jnp.dot(left, right, preferred_element_type=F32)


def dot_t(left, right):
    return lax.dot_general(left, right, (((1,), (1,)), ((), ())), preferred_element_type=F32)


def parts_of(value, count):
    found = []
    for _ in range(count):
        part = value.astype(BF16).astype(F32)
        found.append(part)
        value = value - part
    return found


def rope(value, factors):
    lane = iota(value.shape, 1)
    left = lane < HD
    half = ROT // 2
    cosine = jnp.where(left, pltpu.roll(factors, 64, 1), factors)
    sine = jnp.where(left, pltpu.roll(factors, 32, 1), pltpu.roll(factors, 96, 1))
    other = jnp.where(
        lane % HD < half, pltpu.roll(value, 128 - half, 1), pltpu.roll(value, half, 1)
    )
    return jnp.where(lane % HD < ROT, value * cosine + other * sine, value)


def gelu(value):
    cubed = value * value * value
    return 0.5 * value * (1.0 + jnp.tanh(math.sqrt(2.0 / math.pi) * (value + 0.044715 * cubed)))


def column_of(row, first, period, shape):
    mine = iota(shape, 1) == first + iota(shape, 0) % period
    return jnp.sum(jnp.where(mine, row, 0.0), axis=1, keepdims=True)


def project_kernel(layer, with_branch, meta_ref, x_ref, gain_ref, wq_ref, wf_ref, *refs):
    if with_branch:
        branch_ref, out_ref, state_ref = refs
        sums = []
        for rep in range(4):
            total = branch_ref[rep * 16 : rep * 16 + 4]
            for tp in range(1, 4):
                start = rep * 16 + tp * 4
                total = total + branch_ref[start : start + 4]
            sums.append(total)
        state_ref[...] = (x_ref[...] + jnp.concatenate(sums, axis=0)).astype(BF16).astype(F32)
    else:
        out_ref, state_ref = refs
        state_ref[...] = x_ref[...]
    own = state_ref[pl.ds(meta_ref[4, 0] * 4, 4), :]
    x = jnp.concatenate([state_ref[...], own], axis=0)[:, :HD]
    gain = gain_ref[layer : layer + 1]
    mean = jnp.sum(x, axis=1, keepdims=True) * (1.0 / HD)
    centered = x - mean
    square = jnp.sum(centered * centered, axis=1, keepdims=True)
    rows = jnp.concatenate([centered * gain, jnp.broadcast_to(gain, (4, HD))], axis=0)
    high, low = parts_of(rows, 2)
    high, low = high.astype(BF16), low.astype(BF16)
    for k in range(3):
        every = dot32(high, wq_ref[layer, k]) + dot32(low, wq_ref[layer, k])
        for j in range(4):
            tile = every[:, 128 * j : 128 * j + 128]
            if k == 0:
                out_ref[24 * j : 24 * j + 24] = tile
            else:
                start = 96 + 8 * (4 * (k - 1) + j)
                out_ref[start : start + 8] = tile[16:]
    every = dot32(high[16:], wf_ref[layer]) + dot32(low[16:], wf_ref[layer])
    for j in range(16):
        out_ref[160 + 8 * j : 168 + 8 * j] = every[:, 128 * j : 128 * j + 128]
    lane = iota((16, 128), 1)
    request = iota((16, 128), 0)
    stats = jnp.where(
        lane == request, mean[:16], jnp.where(lane == request + 16, square[:16], 0.0)
    )
    out_ref[288:296] = jnp.broadcast_to(jnp.sum(stats, axis=0, keepdims=True), (8, 128))


def call(kernel, name, outs, scratch, meta, *args, aliases=None):
    specs = [pl.BlockSpec(memory_space=pltpu.SMEM)]
    specs += [pl.BlockSpec(memory_space=pltpu.VMEM) for _ in args]
    place = pl.BlockSpec(memory_space=pltpu.VMEM)
    return pl.pallas_call(
        kernel,
        in_specs=specs,
        out_specs=jax.tree.map(lambda _: place, outs, is_leaf=lambda x: hasattr(x, "shape")),
        out_shape=outs,
        scratch_shapes=scratch,
        input_output_aliases=aliases or {},
        compiler_params=pltpu.CompilerParams(vmem_limit_bytes=24 * 2**20),
        name=name,
        interpret=INTERPRET,
    )(meta, *[near(arg) for arg in args])


def project(layer, meta, x, gain, wq, wf, *branch):
    return call(
        functools.partial(project_kernel, layer, len(branch) > 0),
        "project",
        (near_out((HALF, 128), F32), near_out((16, 128), F32)),
        [],
        meta,
        x,
        gain,
        wq,
        wf,
        *branch,
    )


def pool_kernel(meta_ref, got_ref, out_ref):
    core = meta_ref[4, 1] % 2
    first = meta_ref[4, 0] * 4
    means = [got_ref[s, 288:289] for s in range(2)]
    center = 0.5 * (means[0] + means[1])
    moves = [mean - center for mean in means]
    square = pltpu.roll(means[0] + means[1], 112, 1) + 64.0 * (
        moves[0] * moves[0] + moves[1] * moves[1]
    )
    shift_all = [column_of(move, 0, 16, (16, 128)) for move in moves]
    upper = iota((8, 1), 0) < 4
    shift_own = [jnp.where(upper, column_of(move, first, 4, (8, 128)), 0.0) for move in moves]

    def block(start):
        total = 0.0
        for s in range(2):
            part = got_ref[s, pl.ds(pl.multiple_of(start, 8), 8), :]
            total = total + part + shift_own[s] * part[4:5]
        return total

    common = []
    columns = []
    for j in range(2):
        start = 48 * core + 24 * j
        total, column = 0.0, 0.0
        for s in range(2):
            part = got_ref[s, pl.ds(pl.multiple_of(start, 8), 24), :]
            total = total + part[:16] + shift_all[s] * part[20:21]
            column = column + part[20:21]
        common.append(total)
        columns.append(column)
    for base in (96, 128):
        one = block(base + 16 * core)
        two = block(base + 16 * core + 8)
        common.append(jnp.where(upper, one, pltpu.roll(two, 4, 0)))
        columns += [one[4:5], two[4:5]]
    lane = iota((16, 128), 1)
    request = iota((16, 128), 0)
    stats = jnp.zeros((16, 128), F32)
    both = parts_of(column_of(center, 0, 16, (16, 128)), 3)
    both += parts_of(column_of(square, 0, 16, (16, 128)), 3)
    for k, part in enumerate(both):
        stats = jnp.where(lane == request + 16 * k, part, stats)
    columns.append(jnp.sum(stats, axis=0, keepdims=True))
    tail = jnp.zeros((8, 128), F32)
    for k, column in enumerate(columns):
        tail = jnp.where(iota((8, 128), 0) == k, column, tail)
    common.append(tail)
    shared = jnp.concatenate(common, axis=0)
    for m in range(8):
        whole = jnp.concatenate([shared, block(160 + 64 * core + 8 * m)], axis=0).astype(BF16)
        out_ref[2 * m] = whole
        out_ref[2 * m + 1] = whole


def pool(meta, got):
    return call(pool_kernel, "pool", near_out((16, FLOW, 128), BF16), [], meta, got)


def finish_kernel(meta_ref, got_ref, first_ref, out_ref, act_ref, own_scratch):
    first = meta_ref[4, 0] * 4
    tails = [got_ref[z, 48:].astype(F32) for z in range(16)]
    stats = jnp.concatenate([tail[6:7] for tail in tails], axis=0)
    stats = stats + pltpu.roll(stats, 112, 1) + pltpu.roll(stats, 96, 1)
    average = jnp.sum(stats, axis=0, keepdims=True) * (1.0 / 16)
    offset = stats - average
    spread_sum = 128.0 * jnp.sum(offset * offset, axis=0, keepdims=True)
    square_sum = pltpu.roll(jnp.sum(stats, axis=0, keepdims=True), 80, 1)
    rstd = lax.rsqrt((square_sum + spread_sum) * (1.0 / D) + EPSILON)
    upper = iota((8, 128), 0) < 4
    sums = [0.0] * 5
    for z in range(16):
        tail = tails[z]
        move = offset[z : z + 1]
        every = column_of(move, 0, 16, (16, 128))
        mine = column_of(move, first, 4, (8, 128))
        for j in range(2):
            part = got_ref[z, 16 * j : 16 * j + 16].astype(F32)
            sums[j] = sums[j] + part + every * tail[j : j + 1]
            part = got_ref[z, 32 + 8 * j : 40 + 8 * j].astype(F32)
            column = jnp.where(upper, tail[2 + 2 * j : 3 + 2 * j], tail[3 + 2 * j : 4 + 2 * j])
            sums[2 + j] = sums[2 + j] + part + mine * column
        sums[4] = sums[4] + tail[8:] + mine * tail[12:13]
    every = column_of(rstd, 0, 16, (16, 128))
    mine = column_of(rstd, first, 4, (8, 128))
    own_scratch[:4] = first_ref[pl.ds(first, 4), :]
    own_scratch[4:] = first_ref[pl.ds(first, 4), :]
    queries = [rope(every * sums[j], first_ref[...]) for j in range(2)]
    keys = rope(mine * sums[2], own_scratch[...])
    out_ref[...] = jnp.concatenate(queries + [keys, mine * sums[3]], axis=0).astype(BF16)
    act_ref[...] = gelu(mine * sums[4])


def finish(meta, got, first):
    return call(
        finish_kernel,
        "finish",
        (near_out((48, 128), BF16), near_out((8, 128), F32)),
        [pltpu.VMEM((8, 128), F32)],
        meta,
        got,
        first,
    )


def attend_kernel(layer, meta_ref, got_ref, cache_ref, *refs):
    pages_ref, out_ref, kv = refs[-3:]
    tiles = []
    for tile in range(4):
        start = 48 * (tile // 2)
        rows = start + 16 * (tile % 2)
        tiles.append(got_ref[rows : rows + 16].astype(F32))
        new = got_ref[start + 32 : start + 48].astype(F32)
        for side in range(2):
            rows = 8 * side + 4 * (tile % 2)
            kv[side, :, 128 * tile : 128 * tile + 128] = new[rows : rows + 4]
    queries = jnp.concatenate(tiles, axis=1)
    queries = [queries[i : i + 1] for i in range(16)]
    spot = iota((PAGE, 512), 0)
    for side in range(2):
        for page in range(8):
            home = jnp.clip(meta_ref[0, page] - meta_ref[4, 0] * 4, 0, 3)
            place = jnp.where(meta_ref[3, page] == 1, meta_ref[2, page], -1)
            fresh = kv[side, pl.ds(home, 1), :]
            old = cache_ref[layer, side, page].astype(F32)
            pages_ref[layer, side, page] = jnp.where(spot == place, fresh, old).astype(BF16)
    head_of = iota((8, 512), 1) // HD == iota((8, 512), 0)
    wide = jnp.concatenate(
        [jnp.where(head_of, jnp.broadcast_to(row, (8, 512)), 0.0) for row in queries], axis=0
    ).astype(BF16)
    keys = pages_ref[layer, 0].reshape(8 * PAGE, 512)
    values = pages_ref[layer, 1].reshape(8 * PAGE, 512)
    scores = dot_t(wide, keys) * HD ** (-0.5)
    page_of = iota((1, 256), 1) // PAGE
    owner = jnp.zeros((1, 256), jnp.int32)
    limit = jnp.zeros((1, 256), jnp.int32)
    for page in range(8):
        length = jnp.where(meta_ref[1, page] == 1, meta_ref[2, page] + meta_ref[3, page], 0)
        owner = jnp.where(page_of == page, meta_ref[0, page], owner)
        limit = jnp.where(page_of == page, length, limit)
    owner = jnp.where(iota((1, 256), 1) % PAGE < limit, owner, -1)
    allowed = iota((128, 256), 0) // 8 == owner
    scores = jnp.where(allowed, scores, LOWEST)
    high = jnp.max(scores, axis=1, keepdims=True)
    weights = jnp.where(allowed, jnp.exp(scores - high), 0.0)
    total = jnp.sum(weights, axis=1, keepdims=True)
    mixed = dot32(weights.astype(BF16), values)
    head = iota((128, 128), 0) % 8
    lane = iota((128, 128), 1)
    picked = mixed[:, :128]
    for k in range(1, 4):
        picked = jnp.where(head // 2 == k, mixed[:, 128 * k : 128 * k + 128], picked)
    picked = jnp.where(head % 2 == 1, pltpu.roll(picked, HD, 1), picked)
    out_ref[...] = jnp.where(
        lane < HD, picked, jnp.where(lane == HD, total, jnp.where(lane == HD + 1, high, 0.0))
    )


def attend(layer, meta, got, caches, *pages):
    return call(
        functools.partial(attend_kernel, layer),
        "attend",
        (near_out(caches.shape, BF16), near_out((128, 128), F32)),
        [pltpu.VMEM((2, 4, 512), F32)],
        meta,
        got,
        caches,
        *pages,
        aliases={3: 0} if pages else {},
    )


def join_kernel(meta_ref, got_ref, act_ref, out_ref, wire):
    got = got_ref[...]
    high = got[:, :, HD + 1 : HD + 2]
    top = jnp.max(high, axis=0)
    total = jnp.sum(got * jnp.exp(high - top[None]), axis=0)
    lane = iota((16, 128), 1)
    out = jnp.where(lane < HD, total, 0.0)
    extra = parts_of(total[:, HD : HD + 1], 3) + parts_of(top, 3)
    for k, part in enumerate(extra):
        out = jnp.where(lane == HD + k, part, out)
    even = jnp.full((2, 128), (meta_ref[4, 1] // 2) % 2) == 0
    act = jnp.where(even, act_ref[0:2], act_ref[2:4])
    for z in range(16):
        wire[JOIN * z : JOIN * z + 16] = out
        wire[JOIN * z + 16 : JOIN * z + 18] = act
    out_ref[...] = wire[...].astype(BF16)


def join(meta, got, act):
    return call(
        join_kernel,
        "join",
        near_out((16 * JOIN, 128), BF16),
        [pltpu.VMEM((16 * JOIN, 128), F32)],
        meta,
        got,
        act,
    )


def settle_kernel(meta_ref, got_ref, out_ref, wire, back):
    wire[...] = got_ref[...].astype(F32)
    parts = [wire[JOIN * z : JOIN * z + 16] for z in range(16)]
    take = lambda part, k: part[:, HD + k : HD + k + 1]
    highs = [take(part, 3) + take(part, 4) + take(part, 5) for part in parts]
    top = functools.reduce(jnp.maximum, highs)
    total, mixed = 0.0, 0.0
    for part, high in zip(parts, highs):
        factor = jnp.exp(high - top)
        total = total + (take(part, 0) + take(part, 1) + take(part, 2)) * factor
        mixed = mixed + part * factor
    back[:16] = jnp.where(iota((16, 128), 1) < HD, mixed / total, 0.0)
    for k in range(2):
        back[pl.ds(16 + k, 16, stride=2), :] = wire[pl.ds(16 + k, 16, stride=JOIN), :]
    out_ref[...] = back[...].astype(BF16)


def settle(meta, got):
    return call(
        settle_kernel,
        "settle",
        near_out((48, 128), BF16),
        [pltpu.VMEM((16 * JOIN, 128), F32), pltpu.VMEM((48, 128), F32)],
        meta,
        got,
    )


def output_kernel(layer, copies, meta_ref, got_ref, wo_ref, wf_ref, out_ref):
    att = jnp.concatenate([got_ref[:16], got_ref[48:64]], axis=0).astype(F32)
    att = att + pltpu.roll(att, HD, 1)
    att = jnp.concatenate([att] * 4, axis=1)
    own = iota((32, 512), 1) // HD == iota((32, 512), 0) % 8
    by_head = dot_t(jnp.where(own, att, 0.0).astype(BF16), wo_ref[layer])
    tiles = []
    for core in range(2):
        act = got_ref[48 * core + 16 : 48 * core + 48].astype(F32)
        tiles += [act[4 * m : 4 * m + 4] for m in range(8)]
    mlp = dot_t(jnp.concatenate(tiles, axis=1).astype(BF16), wf_ref[layer])
    rows = [
        jnp.sum(by_head[8 * i : 8 * i + 8], axis=0, keepdims=True) + mlp[i : i + 1]
        for i in range(4)
    ]
    tile = jnp.concatenate(rows, axis=0)
    tile = jnp.concatenate([tile, jnp.zeros_like(tile)], axis=1)
    for k in range(copies):
        out_ref[4 * k : 4 * k + 4] = tile


def output(layer, copies, meta, got, w_out, w_fc2):
    return call(
        functools.partial(output_kernel, layer, copies),
        "output",
        near_out((4 * copies, 128), F32),
        [],
        meta,
        got,
        w_out,
        w_fc2,
    )


def per_device(
    hidden,
    ln_gain,
    w_qkv,
    w_fc1,
    w_out,
    w_fc2,
    caches,
    page_owner,
    page_used,
    page_fill,
    page_tail,
    positions,
):
    rep = lax.axis_index("rep")
    blk = lax.axis_index("blk")
    zs = [[2 * z + c for z in range(16)] for c in range(2)]
    pairs = [[2 * z, 2 * z + 1] for z in range(16)]
    rep_core = [[r * 32 + 2 * z + c for r in range(4) for c in range(2)] for z in range(16)]

    first = jnp.concatenate([hidden.astype(F32), rope_factors(positions)], axis=1)
    first = spread(first, 4, "rep").reshape(16, 128)
    place = jnp.where(jnp.arange(8) == 0, rep, blk).astype(jnp.int32)
    meta = jnp.stack([page_owner, page_used, page_fill, page_tail, place])
    w_qkv = w_qkv.transpose(0, 2, 1, 3)
    w_out = w_out.transpose(0, 2, 1)
    w_fc2 = w_fc2.transpose(0, 2, 1)

    state, branch, pages = first, (), ()
    for layer in range(LAYERS):
        parts, state = project(layer, meta, state, ln_gain, w_qkv, w_fc1, *branch)
        parts = lax.all_gather(parts, "blk", axis_index_groups=pairs)
        got = exchange(pool(meta, parts), "blk", zs)
        packed, act = finish(meta, got, first)
        got = lax.all_gather(packed, "blk", axis_index_groups=pairs, tiled=True)
        fresh, parts = attend(layer, meta, got, caches, *pages)
        pages = (fresh,)
        parts = exchange(parts.reshape(8, 16, 128), ("rep", "blk"), rep_core)
        got = exchange(join(meta, parts, act).reshape(16, JOIN // 2, 2, 128), "blk", zs)
        got = settle(meta, got.reshape(16 * JOIN, 128))
        got = lax.all_gather(got, "blk", axis_index_groups=pairs, tiled=True)
        if layer + 1 < LAYERS:
            out = output(layer, 16, meta, got, w_out, w_fc2).reshape(16, 4, 128)
            branch = (exchange(out, ("rep", "tp")).reshape(64, 128),)
    out = output(layer, 4, meta, got, w_out, w_fc2).reshape(4, 4, 128)
    total = jnp.sum(exchange(out, "tp"), axis=0)[:, :HD]
    own = lax.dynamic_slice(state, (rep * 4, 0), (4, HD))
    return ((own + total).astype(BF16), fresh)


def solution(mesh):
    in_specs = (
        P("rep", "blk"),
        P(None, "blk"),
        P(None, "blk", None, "tp"),
        P(None, "blk", "tp"),
        P(None, "tp", "blk"),
        P(None, "tp", "blk"),
        P(None, None, ("rep", "blk"), None, "tp"),
        P(("rep", "blk")),
        P(("rep", "blk")),
        P(("rep", "blk")),
        P(("rep", "blk")),
        P("rep"),
    )
    out_specs = (P("rep", "blk"), P(None, None, ("rep", "blk"), None, "tp"))
    return jax.shard_map(
        per_device, mesh=mesh, in_specs=in_specs, out_specs=out_specs, check_vma=False
    )
```

time: 181 us -> 171 us (0.945)
  blocking collectives: 147 us -> 134 us
  Pallas kernels: 9.89 us -> 13.3 us
    all_to_all x9 -> x7, blocking collectives: 140 us -> 102 us  [exchange(): lax.all_to_all(value, axis, 0, 0, tiled=True, axis_index_groups=groups)]
    all_gather x2 -> x6, blocking collectives: 7.04 us -> 32.2 us  [the longest x2 13.3 us: per_device(): got = lax.all_gather(packed, 'blk', axis_index_groups=pairs, tiled=True)]
    pallas_call x8 -> x14, Pallas kernels: 8.94 us -> 13.3 us  [call(): pl.pallas_call(kernel, in_specs=specs, out_specs=jax.tree.map(lambda _: p...]
    unnamed x19 -> x29, local copies, waits for them, and re-layouts: 4.38 us -> 5.71 us
where the time goes in v6:
time: 171 us; the launch traced here: 170 us
  blocking collectives  134 us (78%)
  Pallas kernels  13.3 us (8%)
  starting transfers between devices  8.24 us (5%)
  waiting for transfers between devices  6.59 us (4%)
  local copies, waits for them, and re-layouts  6.34 us (4%)
    all_to_all x7, blocking collectives, exchange(): lax.all_to_all(value, axis, 0, 0, tiled=True, axis_index_groups=groups)  102 us
    pallas_call x14, Pallas kernels, call(): pl.pallas_call(kernel, in_specs=specs, out_specs=jax.tree.map(lambda _: p...  13.3 us
    all_gather x2, blocking collectives, per_device(): got = lax.all_gather(packed, 'blk', axis_index_groups=pairs, tiled=True)  13.3 us
    all_gather x2, blocking collectives, per_device(): parts = lax.all_gather(parts, 'blk', axis_index_groups=pairs)  11.5 us
    all_to_all x2, starting transfers between devices, exchange(): lax.all_to_all(value, axis, 0, 0, tiled=True, axis_index_groups=groups)  8.24 us
    all_gather x2, blocking collectives, per_device(): got = lax.all_gather(got, 'blk', axis_index_groups=pairs, tiled=True)  7.41 us
    all_to_all x2, waiting for transfers between devices, exchange(): lax.all_to_all(value, axis, 0, 0, tiled=True, axis_index_groups=groups)  6.59 us
    unnamed x29, local copies, waits for them, and re-layouts  5.71 us
  transfers between devices with their start and end apart: 2, of which 2 were waited for; matrix products, arithmetic and copies ran while one was open for 1% of the time, Pallas kernels for 0%

profile of v6, /device:TPU:1, one launch (start us, length us, event | category | flops | bytes accessed | tf_op | source)
XLA Modules:
  0.0 170.2 jit_solution(16804354583833204378)
XLA Ops:
  2.8 5.0 %all-to-all-start = ((f32[4,4,128]{2,1,0:T(4,128)}), f32[4,4,128]{2,1,0:T(4,128)S(1)}, u32[]{:S(2)}, u32[]{:S(2)}) async-start(f32[4,4,128]{2,1,0:T(4,128)} %broadcast_in_dim.27), calls=%async_computation | async-start | bytes 16384 | tf_op jit(solution)/shard_map/all_to_all | solution.py:27
  8.5 3.4 %all-to-all-done = f32[4,4,128]{2,1,0:T(4,128)S(1)} async-done(((f32[4,4,128]{2,1,0:T(4,128)}), f32[4,4,128]{2,1,0:T(4,128)S(1)}, u32[]{:S(2)}, u32[]{:S(2)}) %all-to-all-start) | async-done | bytes 8224 | tf_op jit(solution)/shard_map/all_to_all | solution.py:27
  12.6 1.0 copy-done.1
  13.7 1.0 copy-done.4
  14.7 0.9 project.2
  15.6 8.0 %all-gather = f32[592,128]{1,0:T(8,128)S(1)} all-gather(f32[296,128]{1,0:T(8,128)S(1)} %get-tuple-element.15), channel_id=2, replica_groups={{0,4},{8,12},{16,20},{24,28},{32,36},{40,44},{48,52},{56,60},{64,68},{7..., dimensions={0}, use_global_device_ids=true | all-gather | bytes 454656 | tf_op jit(solution)/shard_map/all_gather | solution.py:463
  24.4 24.6 %all_to_all.45.got_ref = bf16[16,64,128]{2,1,0:T(8,128)(2,1)S(1)} all-to-all(bf16[16,64,128]{2,1,0:T(8,128)(2,1)S(1)} %pool.2), channel_id=1, replica_groups={{0,8,16,24,32,40,48,56,64,72,80,88,96,104,112,120},{4,12,20,28,36,44,52..., dimensions={0} | all-to-all | bytes 524288 | tf_op jit(solution)/shard_map/all_to_all | solution.py:27
  49.0 0.9 finish.2
  50.0 6.6 %all_gather.26.got_ref = bf16[96,128]{1,0:T(8,128)(2,1)S(1)} all-gather(bf16[48,128]{1,0:T(8,128)(2,1)S(1)} %get-tuple-element.16), channel_id=1, replica_groups={{0,4},{8,12},{16,20},{24,28},{32,36},{40,44},{48,52},{56,60},{64,68},{7..., dimensions={0}, use_global_device_ids=true | all-gather | bytes 36864 | tf_op jit(solution)/shard_map/all_gather | solution.py:466
  56.6 1.2 attend.2
  57.8 7.7 %all_to_all.46.got_ref = f32[8,16,128]{2,1,0:T(8,128)S(1)} all-to-all(f32[8,16,128]{2,1,0:T(8,128)S(1)} %bitcast.37), channel_id=1, replica_groups={{0,4,128,132,256,260,384,388},{8,12,136,140,264,268,392,396},{16,20,144..., dimensions={0} | all-to-all | bytes 131072 | tf_op jit(solution)/shard_map/all_to_all | solution.py:27
  65.5 0.8 join.2
  66.3 17.3 %all_to_all.47 = bf16[16,9,2,128]{3,2,1,0:T(2,128)(2,1)S(1)} all-to-all(bf16[16,9,2,128]{3,2,1,0:T(2,128)(2,1)S(1)} %bitcast.27), channel_id=1, replica_groups={{0,8,16,24,32,40,48,56,64,72,80,88,96,104,112,120},{4,12,20,28,36,44,52..., dimensions={0} | all-to-all | bytes 147456 | tf_op jit(solution)/shard_map/all_to_all | solution.py:27
  83.6 0.9 settle.2
  84.5 3.7 %all_gather.27.got_ref = bf16[96,128]{1,0:T(8,128)(2,1)S(1)} all-gather(bf16[48,128]{1,0:T(8,128)(2,1)S(1)} %settle.2), channel_id=1, replica_groups={{0,4},{8,12},{16,20},{24,28},{32,36},{40,44},{48,52},{56,60},{64,68},{7..., dimensions={0}, use_global_device_ids=true | all-gather | bytes 36864 | tf_op jit(solution)/shard_map/all_gather | solution.py:472
  88.3 0.9 output.2
  89.1 11.0 %all_to_all.48 = f32[16,4,128]{2,1,0:T(4,128)S(1)} all-to-all(f32[16,4,128]{2,1,0:T(4,128)S(1)} %bitcast.35), channel_id=1, replica_groups=mesh['rep'=4,'blk'=32,'tp'=4] {'rep','tp'}, dimensions={0} | all-to-all | bytes 65536 | tf_op jit(solution)/shard_map/all_to_all | solution.py:27
  100.1 0.9 project.3
  101.0 3.4 %all-gather.1 = f32[592,128]{1,0:T(8,128)S(1)} all-gather(f32[296,128]{1,0:T(8,128)S(1)} %get-tuple-element.20), channel_id=3, replica_groups={{0,4},{8,12},{16,20},{24,28},{32,36},{40,44},{48,52},{56,60},{64,68},{7..., dimensions={0}, use_global_device_ids=true | all-gather | bytes 454656 | tf_op jit(solution)/shard_map/all_gather | solution.py:463
  105.2 16.6 %all_to_all.49.got_ref = bf16[16,64,128]{2,1,0:T(8,128)(2,1)S(1)} all-to-all(bf16[16,64,128]{2,1,0:T(8,128)(2,1)S(1)} %pool.3), channel_id=1, replica_groups={{0,8,16,24,32,40,48,56,64,72,80,88,96,104,112,120},{4,12,20,28,36,44,52..., dimensions={0} | all-to-all | bytes 524288 | tf_op jit(solution)/shard_map/all_to_all | solution.py:27
  121.9 0.9 finish.3
  122.8 6.6 %all_gather.30.got_ref = bf16[96,128]{1,0:T(8,128)(2,1)S(1)} all-gather(bf16[48,128]{1,0:T(8,128)(2,1)S(1)} %get-tuple-element.21), channel_id=1, replica_groups={{0,4},{8,12},{16,20},{24,28},{32,36},{40,44},{48,52},{56,60},{64,68},{7..., dimensions={0}, use_global_device_ids=true | all-gather | bytes 36864 | tf_op jit(solution)/shard_map/all_gather | solution.py:466
  129.4 1.2 attend.3
  130.7 7.6 %all_to_all.50.got_ref = f32[8,16,128]{2,1,0:T(8,128)S(1)} all-to-all(f32[8,16,128]{2,1,0:T(8,128)S(1)} %bitcast.36), channel_id=1, replica_groups={{0,4,128,132,256,260,384,388},{8,12,136,140,264,268,392,396},{16,20,144..., dimensions={0} | all-to-all | bytes 131072 | tf_op jit(solution)/shard_map/all_to_all | solution.py:27
  138.2 0.8 join.3
  139.0 17.2 %all_to_all.51 = bf16[16,9,2,128]{3,2,1,0:T(2,128)(2,1)S(1)} all-to-all(bf16[16,9,2,128]{3,2,1,0:T(2,128)(2,1)S(1)} %bitcast.28), channel_id=1, replica_groups={{0,8,16,24,32,40,48,56,64,72,80,88,96,104,112,120},{4,12,20,28,36,44,52..., dimensions={0} | all-to-all | bytes 147456 | tf_op jit(solution)/shard_map/all_to_all | solution.py:27
  156.2 0.9 settle.3
  157.1 3.7 %all_gather.31.got_ref = bf16[96,128]{1,0:T(8,128)(2,1)S(1)} all-gather(bf16[48,128]{1,0:T(8,128)(2,1)S(1)} %settle.3), channel_id=1, replica_groups={{0,4},{8,12},{16,20},{24,28},{32,36},{40,44},{48,52},{56,60},{64,68},{7..., dimensions={0}, use_global_device_ids=true | all-gather | bytes 36864 | tf_op jit(solution)/shard_map/all_gather | solution.py:472
  160.8 1.5 output.3
  162.2 3.2 %all-to-all-start.8 = ((f32[4,4,128]{2,1,0:T(4,128)}), f32[4,4,128]{2,1,0:T(4,128)S(1)}, u32[]{:S(2)}, u32[]{:S(2)}) async-start(f32[4,4,128]{2,1,0:T(4,128)} %bitcast.18), calls=%async_computation.8 | async-start | bytes 16384 | tf_op jit(solution)/shard_map/all_to_all | solution.py:27
  165.5 1.0 copy.16
  166.5 3.2 %all-to-all-done.8 = f32[4,4,128]{2,1,0:T(4,128)S(1)} async-done(((f32[4,4,128]{2,1,0:T(4,128)}), f32[4,4,128]{2,1,0:T(4,128)S(1)}, u32[]{:S(2)}, u32[]{:S(2)}) %all-to-all-start.8) | async-done | bytes 8224 | tf_op jit(solution)/shard_map/all_to_all | solution.py:27
  (39 shorter events, 5.7 us)
Async XLA Ops:
  0.6 0.7 copy-start.13
  1.3 0.7 copy-start.8
  2.8 9.2 %all-to-all-start = ((f32[4,4,128]{2,1,0:T(4,128)}), f32[4,4,128]{2,1,0:T(4,128)S(1)}, u32[]{:S(2)}, u32[]{:S(2)}) async-start(f32[4,4,128]{2,1,0:T(4,128)} %broadcast_in_dim.27), calls=%async_computation | async-start | bytes 16384 | tf_op jit(solution)/shard_map/all_to_all | solution.py:27
  7.8 0.7 copy-start.12
  7.8 0.7 copy-start.9
  7.8 0.7 copy-start.10
  7.8 0.7 copy-start.11
  12.0 0.7 copy-start.7
  12.6 1.0 copy-start.1
  13.7 1.0 copy-start.4
  15.6 41.0 %copy-start = (bf16[2,2,8,32,512]{4,3,2,1,0:T(8,128)(2,1)S(1)}, bf16[2,2,8,32,512]{4,3,2,1,0:T(8,128)(2,1)}, u32[]{:S(2)}) copy-start(bf16[2,2,8,32,512]{4,3,2,1,0:T(8,128)(2,1)} %cache_ref.3) | copy-start | bytes 3145732
  56.6 31.6 %copy-start.6 = (bf16[2,512,64]{1,2,0:T(8,128)(2,1)S(1)}, bf16[2,512,64]{1,2,0:T(8,128)(2,1)}, u32[]{:S(2)}) copy-start(bf16[2,512,64]{1,2,0:T(8,128)(2,1)} %param.16) | copy-start | bytes 393220
  56.6 43.5 %copy-start.5 = (bf16[2,64,3,512]{3,1,2,0:T(8,128)(2,1)S(1)}, bf16[2,64,3,512]{3,1,2,0:T(8,128)(2,1)}, u32[]{:S(2)}) copy-start(bf16[2,64,3,512]{3,1,2,0:T(8,128)(2,1)} %param.14) | copy-start | bytes 1179652
  57.8 30.4 %copy-start.3 = (bf16[2,2048,64]{1,2,0:T(8,128)(2,1)S(1)}, bf16[2,2048,64]{1,2,0:T(8,128)(2,1)}, u32[]{:S(2)}) copy-start(bf16[2,2048,64]{1,2,0:T(8,128)(2,1)} %param.17) | copy-start | bytes 1572868
  66.3 33.8 %copy-start.2 = (bf16[2,64,2048]{2,1,0:T(8,128)(2,1)S(1)}, bf16[2,64,2048]{2,1,0:T(8,128)(2,1)}, u32[]{:S(2)}) copy-start(bf16[2,64,2048]{2,1,0:T(8,128)(2,1)} %wf_ref.3) | copy-start | bytes 1572868
  162.2 7.4 %all-to-all-start.8 = ((f32[4,4,128]{2,1,0:T(4,128)}), f32[4,4,128]{2,1,0:T(4,128)S(1)}, u32[]{:S(2)}, u32[]{:S(2)}) async-start(f32[4,4,128]{2,1,0:T(4,128)} %bitcast.18), calls=%async_computation.8 | async-start | bytes 16384 | tf_op jit(solution)/shard_map/all_to_all | solution.py:27

commit v7 on v6

--- a/solution.py
+++ b/solution.py
@@ -18,17 +18,13 @@
 F32 = jnp.float32
 BF16 = jnp.bfloat16
 INTERPRET = False
-HALF = 296
-FLOW = 64
+HALF = 232
+FLOW = 34
 JOIN = 18
 
 
 def exchange(value, axis, groups=None):
     return lax.all_to_all(value, axis, 0, 0, tiled=True, axis_index_groups=groups)
-
-
-def spread(value, count, axis, groups=None):
-    return exchange(jnp.broadcast_to(value[None], (count,) + value.shape), axis, groups)
 
 
 def rope_factors(positions):
@@ -90,22 +86,15 @@
     return jnp.sum(jnp.where(mine, row, 0.0), axis=1, keepdims=True)
 
 
-def project_kernel(layer, with_branch, meta_ref, x_ref, gain_ref, wq_ref, wf_ref, *refs):
-    if with_branch:
-        branch_ref, out_ref, state_ref = refs
-        sums = []
-        for rep in range(4):
-            total = branch_ref[rep * 16 : rep * 16 + 4]
-            for tp in range(1, 4):
-                start = rep * 16 + tp * 4
-                total = total + branch_ref[start : start + 4]
-            sums.append(total)
-        state_ref[...] = (x_ref[...] + jnp.concatenate(sums, axis=0)).astype(BF16).astype(F32)
+def project_kernel(layer, meta_ref, x_ref, gain_ref, wq_ref, wf_ref, *refs):
+    out_ref, state_ref = refs[-2:]
+    if layer == 0:
+        x = x_ref[...].astype(F32)
     else:
-        out_ref, state_ref = refs
-        state_ref[...] = x_ref[...]
-    own = state_ref[pl.ds(meta_ref[4, 0] * 4, 4), :]
-    x = jnp.concatenate([state_ref[...], own], axis=0)[:, :HD]
+        branch_ref = refs[0]
+        x = x_ref[...] + branch_ref[0:4] + branch_ref[4:8] + branch_ref[8:12] + branch_ref[12:16]
+        x = x.astype(BF16).astype(F32)[:, :HD]
+    state_ref[...] = jnp.concatenate([x, jnp.zeros_like(x)], axis=1)
     gain = gain_ref[layer : layer + 1]
     mean = jnp.sum(x, axis=1, keepdims=True) * (1.0 / HD)
     centered = x - mean
@@ -116,21 +105,15 @@
     for k in range(3):
         every = dot32(high, wq_ref[layer, k]) + dot32(low, wq_ref[layer, k])
         for j in range(4):
-            tile = every[:, 128 * j : 128 * j + 128]
-            if k == 0:
-                out_ref[24 * j : 24 * j + 24] = tile
-            else:
-                start = 96 + 8 * (4 * (k - 1) + j)
-                out_ref[start : start + 8] = tile[16:]
-    every = dot32(high[16:], wf_ref[layer]) + dot32(low[16:], wf_ref[layer])
+            start = 8 * (4 * k + j)
+            out_ref[start : start + 8] = every[:, 128 * j : 128 * j + 128]
+    every = dot32(high, wf_ref[layer]) + dot32(low, wf_ref[layer])
     for j in range(16):
-        out_ref[160 + 8 * j : 168 + 8 * j] = every[:, 128 * j : 128 * j + 128]
-    lane = iota((16, 128), 1)
-    request = iota((16, 128), 0)
-    stats = jnp.where(
-        lane == request, mean[:16], jnp.where(lane == request + 16, square[:16], 0.0)
-    )
-    out_ref[288:296] = jnp.broadcast_to(jnp.sum(stats, axis=0, keepdims=True), (8, 128))
+        out_ref[96 + 8 * j : 104 + 8 * j] = every[:, 128 * j : 128 * j + 128]
+    lane = iota((4, 128), 1)
+    request = iota((4, 128), 0)
+    stats = jnp.where(lane == request, mean, jnp.where(lane == request + 16, square, 0.0))
+    out_ref[224:232] = jnp.broadcast_to(jnp.sum(stats, axis=0, keepdims=True), (8, 128))
 
 
 def call(kernel, name, outs, scratch, meta, *args, aliases=None):
@@ -152,9 +135,9 @@
 
 def project(layer, meta, x, gain, wq, wf, *branch):
     return call(
-        functools.partial(project_kernel, layer, len(branch) > 0),
+        functools.partial(project_kernel, layer),
         "project",
-        (near_out((HALF, 128), F32), near_out((16, 128), F32)),
+        (near_out((HALF, 128), F32), near_out((4, 128), F32)),
         [],
         meta,
         x,
@@ -165,69 +148,68 @@
     )
 
 
-def pool_kernel(meta_ref, got_ref, out_ref):
+def pool_kernel(meta_ref, got_ref, out_ref, wire):
     core = meta_ref[4, 1] % 2
-    first = meta_ref[4, 0] * 4
-    means = [got_ref[s, 288:289] for s in range(2)]
+    means = [got_ref[s, 224:225] for s in range(2)]
     center = 0.5 * (means[0] + means[1])
     moves = [mean - center for mean in means]
     square = pltpu.roll(means[0] + means[1], 112, 1) + 64.0 * (
         moves[0] * moves[0] + moves[1] * moves[1]
     )
-    shift_all = [column_of(move, 0, 16, (16, 128)) for move in moves]
     upper = iota((8, 1), 0) < 4
-    shift_own = [jnp.where(upper, column_of(move, first, 4, (8, 128)), 0.0) for move in moves]
+    shift = [jnp.where(upper, column_of(move, 0, 4, (8, 128)), 0.0) for move in moves]
 
     def block(start):
         total = 0.0
         for s in range(2):
             part = got_ref[s, pl.ds(pl.multiple_of(start, 8), 8), :]
-            total = total + part + shift_own[s] * part[4:5]
+            total = total + part + shift[s] * part[4:5]
         return total
 
     common = []
     columns = []
-    for j in range(2):
-        start = 48 * core + 24 * j
-        total, column = 0.0, 0.0
-        for s in range(2):
-            part = got_ref[s, pl.ds(pl.multiple_of(start, 8), 24), :]
-            total = total + part[:16] + shift_all[s] * part[20:21]
-            column = column + part[20:21]
-        common.append(total)
-        columns.append(column)
-    for base in (96, 128):
+    for base in (0, 32, 64):
         one = block(base + 16 * core)
         two = block(base + 16 * core + 8)
         common.append(jnp.where(upper, one, pltpu.roll(two, 4, 0)))
         columns += [one[4:5], two[4:5]]
-    lane = iota((16, 128), 1)
-    request = iota((16, 128), 0)
-    stats = jnp.zeros((16, 128), F32)
-    both = parts_of(column_of(center, 0, 16, (16, 128)), 3)
-    both += parts_of(column_of(square, 0, 16, (16, 128)), 3)
+    lane = iota((4, 128), 1)
+    request = iota((4, 128), 0)
+    stats = jnp.zeros((4, 128), F32)
+    both = parts_of(column_of(center, 0, 4, (4, 128)), 3)
+    both += parts_of(column_of(square, 0, 4, (4, 128)), 3)
     for k, part in enumerate(both):
         stats = jnp.where(lane == request + 16 * k, part, stats)
     columns.append(jnp.sum(stats, axis=0, keepdims=True))
+    row = iota((8, 128), 0)
     tail = jnp.zeros((8, 128), F32)
     for k, column in enumerate(columns):
-        tail = jnp.where(iota((8, 128), 0) == k, column, tail)
-    common.append(tail)
+        tail = jnp.where(row == k, column, tail)
     shared = jnp.concatenate(common, axis=0)
     for m in range(8):
-        whole = jnp.concatenate([shared, block(160 + 64 * core + 8 * m)], axis=0).astype(BF16)
-        out_ref[2 * m] = whole
-        out_ref[2 * m + 1] = whole
+        last = block(96 + 64 * core + 8 * m)
+        whole = jnp.concatenate([shared, jnp.where(row == 7, last[4:5], tail)], axis=0)
+        for k in range(2):
+            start = FLOW * (2 * m + k)
+            wire[start : start + 32] = whole
+            wire[start + 32 : start + 34] = last[2 * k : 2 * k + 2]
+    out_ref[...] = wire[...].astype(BF16)
 
 
 def pool(meta, got):
-    return call(pool_kernel, "pool", near_out((16, FLOW, 128), BF16), [], meta, got)
-
-
-def finish_kernel(meta_ref, got_ref, first_ref, out_ref, act_ref, own_scratch):
-    first = meta_ref[4, 0] * 4
-    tails = [got_ref[z, 48:].astype(F32) for z in range(16)]
-    stats = jnp.concatenate([tail[6:7] for tail in tails], axis=0)
+    return call(
+        pool_kernel,
+        "pool",
+        near_out((16 * FLOW, 128), BF16),
+        [pltpu.VMEM((16 * FLOW, 128), F32)],
+        meta,
+        got,
+    )
+
+
+def finish_kernel(meta_ref, got_ref, factor_ref, out_ref, act_ref, wire):
+    wire[...] = got_ref[...].astype(F32)
+    stats = wire[pl.ds(30, 16, stride=FLOW), :]
     stats = stats + pltpu.roll(stats, 112, 1) + pltpu.roll(stats, 96, 1)
     average = jnp.sum(stats, axis=0, keepdims=True) * (1.0 / 16)
     offset = stats - average
@@ -235,38 +217,37 @@
     square_sum = pltpu.roll(jnp.sum(stats, axis=0, keepdims=True), 80, 1)
     rstd = lax.rsqrt((square_sum + spread_sum) * (1.0 / D) + EPSILON)
     upper = iota((8, 128), 0) < 4
-    sums = [0.0] * 5
+    pair = 2 * ((meta_ref[4, 1] // 2) % 2)
+    sums = [0.0] * 4
     for z in range(16):
-        tail = tails[z]
+        base = FLOW * z
         move = offset[z : z + 1]
-        every = column_of(move, 0, 16, (16, 128))
-        mine = column_of(move, first, 4, (8, 128))
-        for j in range(2):
-            part = got_ref[z, 16 * j : 16 * j + 16].astype(F32)
-            sums[j] = sums[j] + part + every * tail[j : j + 1]
-            part = got_ref[z, 32 + 8 * j : 40 + 8 * j].astype(F32)
-            column = jnp.where(upper, tail[2 + 2 * j : 3 + 2 * j], tail[3 + 2 * j : 4 + 2 * j])
-            sums[2 + j] = sums[2 + j] + part + mine * column
-        sums[4] = sums[4] + tail[8:] + mine * tail[12:13]
-    every = column_of(rstd, 0, 16, (16, 128))
-    mine = column_of(rstd, first, 4, (8, 128))
-    own_scratch[:4] = first_ref[pl.ds(first, 4), :]
-    own_scratch[4:] = first_ref[pl.ds(first, 4), :]
-    queries = [rope(every * sums[j], first_ref[...]) for j in range(2)]
-    keys = rope(mine * sums[2], own_scratch[...])
-    out_ref[...] = jnp.concatenate(queries + [keys, mine * sums[3]], axis=0).astype(BF16)
-    act_ref[...] = gelu(mine * sums[4])
-
-
-def finish(meta, got, first):
+        mine = column_of(move, 0, 4, (8, 128))
+        tail = wire[base + 24 : base + 32]
+        for k in range(3):
+            part = wire[base + 8 * k : base + 8 * k + 8]
+            column = jnp.where(upper, tail[2 * k : 2 * k + 1], tail[2 * k + 1 : 2 * k + 2])
+            sums[k] = sums[k] + part + mine * column
+        part = wire[base + 32 : base + 34]
+        sums[3] = sums[3] + part + column_of(move, pair, 2, (2, 128)) * tail[7:8]
+    mine = column_of(rstd, 0, 4, (8, 128))
+    factors = jnp.concatenate([factor_ref[...], factor_ref[...]], axis=0)
+    packed = [rope(mine * sums[k], factors) for k in range(2)] + [mine * sums[2]]
+    packed = jnp.concatenate(packed, axis=0).astype(BF16)
+    for k in range(8):
+        out_ref[k] = packed
+    act_ref[...] = gelu(column_of(rstd, pair, 2, (2, 128)) * sums[3])
+
+
+def finish(meta, got, factors):
     return call(
         finish_kernel,
         "finish",
-        (near_out((48, 128), BF16), near_out((8, 128), F32)),
-        [pltpu.VMEM((8, 128), F32)],
-        meta,
-        got,
-        first,
+        (near_out((8, 24, 128), BF16), near_out((2, 128), F32)),
+        [pltpu.VMEM((16 * FLOW, 128), F32)],
+        meta,
+        got,
+        factors,
     )
 
 
@@ -274,13 +255,13 @@
     pages_ref, out_ref, kv = refs[-3:]
     tiles = []
     for tile in range(4):
-        start = 48 * (tile // 2)
-        rows = start + 16 * (tile % 2)
-        tiles.append(got_ref[rows : rows + 16].astype(F32))
-        new = got_ref[start + 32 : start + 48].astype(F32)
+        core, rows = tile // 2, 4 * (tile % 2)
+        parts = [got_ref[2 * r + core, :8].astype(F32)[rows : rows + 4] for r in range(4)]
+        tiles.append(jnp.concatenate(parts, axis=0))
+        new = got_ref[2 * meta_ref[4, 0] + core].astype(F32)
         for side in range(2):
-            rows = 8 * side + 4 * (tile % 2)
-            kv[side, :, 128 * tile : 128 * tile + 128] = new[rows : rows + 4]
+            start = 8 + 8 * side + rows
+            kv[side, :, 128 * tile : 128 * tile + 128] = new[start : start + 4]
     queries = jnp.concatenate(tiles, axis=1)
     queries = [queries[i : i + 1] for i in range(16)]
     spot = iota((PAGE, 512), 0)
@@ -347,8 +328,7 @@
     extra = parts_of(total[:, HD : HD + 1], 3) + parts_of(top, 3)
     for k, part in enumerate(extra):
         out = jnp.where(lane == HD + k, part, out)
-    even = jnp.full((2, 128), (meta_ref[4, 1] // 2) % 2) == 0
-    act = jnp.where(even, act_ref[0:2], act_ref[2:4])
+    act = act_ref[...]
     for z in range(16):
         wire[JOIN * z : JOIN * z + 16] = out
         wire[JOIN * z + 16 : JOIN * z + 18] = act
@@ -395,7 +375,7 @@
     )
 
 
-def output_kernel(layer, copies, meta_ref, got_ref, wo_ref, wf_ref, out_ref):
+def output_kernel(layer, meta_ref, got_ref, wo_ref, wf_ref, out_ref):
     att = jnp.concatenate([got_ref[:16], got_ref[48:64]], axis=0).astype(F32)
     att = att + pltpu.roll(att, HD, 1)
     att = jnp.concatenate([att] * 4, axis=1)
@@ -412,15 +392,15 @@
     ]
     tile = jnp.concatenate(rows, axis=0)
     tile = jnp.concatenate([tile, jnp.zeros_like(tile)], axis=1)
-    for k in range(copies):
+    for k in range(4):
         out_ref[4 * k : 4 * k + 4] = tile
 
 
-def output(layer, copies, meta, got, w_out, w_fc2):
-    return call(
-        functools.partial(output_kernel, layer, copies),
+def output(layer, meta, got, w_out, w_fc2):
+    return call(
+        functools.partial(output_kernel, layer),
         "output",
-        near_out((4 * copies, 128), F32),
+        near_out((16, 128), F32),
         [],
         meta,
         got,
@@ -449,34 +429,32 @@
     pairs = [[2 * z, 2 * z + 1] for z in range(16)]
     rep_core = [[r * 32 + 2 * z + c for r in range(4) for c in range(2)] for z in range(16)]
 
-    first = jnp.concatenate([hidden.astype(F32), rope_factors(positions)], axis=1)
-    first = spread(first, 4, "rep").reshape(16, 128)
+    factors = rope_factors(positions)
+    factors = jnp.concatenate([factors, factors], axis=1)
     place = jnp.where(jnp.arange(8) == 0, rep, blk).astype(jnp.int32)
     meta = jnp.stack([page_owner, page_used, page_fill, page_tail, place])
     w_qkv = w_qkv.transpose(0, 2, 1, 3)
     w_out = w_out.transpose(0, 2, 1)
     w_fc2 = w_fc2.transpose(0, 2, 1)
 
-    state, branch, pages = first, (), ()
+    state, branch, pages = hidden, (), ()
     for layer in range(LAYERS):
         parts, state = project(layer, meta, state, ln_gain, w_qkv, w_fc1, *branch)
         parts = lax.all_gather(parts, "blk", axis_index_groups=pairs)
-        got = exchange(pool(meta, parts), "blk", zs)
-        packed, act = finish(meta, got, first)
-        got = lax.all_gather(packed, "blk", axis_index_groups=pairs, tiled=True)
+        got = exchange(pool(meta, parts).reshape(16, FLOW // 2, 2, 128), "blk", zs)
+        packed, act = finish(meta, got.reshape(16 * FLOW, 128), factors)
+        got = exchange(packed, ("rep", "blk"), rep_core)
         fresh, parts = attend(layer, meta, got, caches, *pages)
         pages = (fresh,)
         parts = exchange(parts.reshape(8, 16, 128), ("rep", "blk"), rep_core)
         got = exchange(join(meta, parts, act).reshape(16, JOIN // 2, 2, 128), "blk", zs)
         got = settle(meta, got.reshape(16 * JOIN, 128))
         got = lax.all_gather(got, "blk", axis_index_groups=pairs, tiled=True)
-        if layer + 1 < LAYERS:
-            out = output(layer, 16, meta, got, w_out, w_fc2).reshape(16, 4, 128)
-            branch = (exchange(out, ("rep", "tp")).reshape(64, 128),)
-    out = output(layer, 4, meta, got, w_out, w_fc2).reshape(4, 4, 128)
-    total = jnp.sum(exchange(out, "tp"), axis=0)[:, :HD]
-    own = lax.dynamic_slice(state, (rep * 4, 0), (4, HD))
-    return ((own + total).astype(BF16), fresh)
+        out = output(layer, meta, got, w_out, w_fc2).reshape(4, 4, 128)
+        out = exchange(out, "tp")
+        branch = (out.reshape(16, 128),)
+    result = (state[:, :HD] + jnp.sum(out, axis=0)[:, :HD]).astype(BF16)
+    return (result, fresh)
 
 
 def solution(mesh):

time: 171 us -> 161 us (0.942)
  blocking collectives: 134 us -> 112 us
  waiting for transfers between devices: 6.59 us -> 15.1 us
  starting transfers between devices: 8.24 us -> 12.9 us
  local copies, waits for them, and re-layouts: 6.34 us -> 4.41 us
    all_gather x2 -> x0, blocking collectives: 13.3 us -> none  [per_device(): got = lax.all_gather(packed, 'blk', axis_index_groups=pairs, tiled=True)]
    all_to_all x7 -> x8, blocking collectives: 102 us -> 92.9 us  [exchange(): lax.all_to_all(value, axis, 0, 0, tiled=True, axis_index_groups=groups)]
    all_to_all x2, waiting for transfers between devices: 6.59 us -> 15.1 us  [exchange(): lax.all_to_all(value, axis, 0, 0, tiled=True, axis_index_groups=groups)]
    all_to_all x2, starting transfers between devices: 8.24 us -> 12.9 us  [exchange(): lax.all_to_all(value, axis, 0, 0, tiled=True, axis_index_groups=groups)]
where the time goes in v7:
time: 161 us; the launch traced here: 160 us
  blocking collectives  112 us (70%)
  waiting for transfers between devices  15.1 us (9%)
  Pallas kernels  14 us (9%)
  starting transfers between devices  12.9 us (8%)
  local copies, waits for them, and re-layouts  4.41 us (3%)
    all_to_all x8, blocking collectives, exchange(): lax.all_to_all(value, axis, 0, 0, tiled=True, axis_index_groups=groups)  92.9 us
    all_to_all x2, waiting for transfers between devices, exchange(): lax.all_to_all(value, axis, 0, 0, tiled=True, axis_index_groups=groups)  15.1 us
    pallas_call x14, Pallas kernels, call(): pl.pallas_call(kernel, in_specs=specs, out_specs=jax.tree.map(lambda _: p...  14 us
    all_to_all x2, starting transfers between devices, exchange(): lax.all_to_all(value, axis, 0, 0, tiled=True, axis_index_groups=groups)  12.9 us
    all_gather x2, blocking collectives, per_device(): parts = lax.all_gather(parts, 'blk', axis_index_groups=pairs)  11.9 us
    all_gather x2, blocking collectives, per_device(): got = lax.all_gather(got, 'blk', axis_index_groups=pairs, tiled=True)  7.41 us
    unnamed x29, local copies, waits for them, and re-layouts  4.39 us
  transfers between devices with their start and end apart: 2, of which 2 were waited for; matrix products, arithmetic and copies ran while one was open for 1% of the time, Pallas kernels for 0%

profile of v7, /device:TPU:1, one launch (start us, length us, event | category | flops | bytes accessed | tf_op | source)
XLA Modules:
  0.0 160.2 jit_solution(13159195112926903902)
XLA Ops:
  2.1 1.0 copy-done.1
  3.1 1.0 copy-done.4
  4.1 0.9 project.2
  5.0 8.5 %all-gather = f32[464,128]{1,0:T(8,128)S(1)} all-gather(f32[232,128]{1,0:T(8,128)S(1)} %get-tuple-element.15), channel_id=2, replica_groups={{0,4},{8,12},{16,20},{24,28},{32,36},{40,44},{48,52},{56,60},{64,68},{7..., dimensions={0}, use_global_device_ids=true | all-gather | bytes 356352 | tf_op jit(solution)/shard_map/all_gather | solution.py:443
  13.5 1.4 pool.2
  14.9 9.7 %all-to-all-start = ((bf16[16,17,2,128]{3,2,1,0:T(2,128)(2,1)}), bf16[16,17,2,128]{3,2,1,0:T(2,128)(2,1)S(1)}, u32[]{:S(2)}, u32[]{:S(2)}) async-start(bf16[16,17,2,128]{3,2,1,0:T(2,128)(2,1)} %bitcast.6), calls=%async_computation | async-start | bytes 278528 | tf_op jit(solution)/shard_map/all_to_all | solution.py:27
  24.9 12.0 %all-to-all-done = bf16[16,17,2,128]{3,2,1,0:T(2,128)(2,1)S(1)} async-done(((bf16[16,17,2,128]{3,2,1,0:T(2,128)(2,1)}), bf16[16,17,2,128]{3,2,1,0:T(2,128)(2,1)S(1)}, u32[]{:S(2)}, u32[]{:S(2)}) %all-to-all-start) | async-done | bytes 139296 | tf_op jit(solution)/shard_map/all_to_all | solution.py:27
  36.9 0.9 finish.2
  37.8 12.6 %all_to_all.50.got_ref = bf16[8,24,128]{2,1,0:T(8,128)(2,1)S(1)} all-to-all(bf16[8,24,128]{2,1,0:T(8,128)(2,1)S(1)} %get-tuple-element.16), channel_id=1, replica_groups={{0,4,128,132,256,260,384,388},{8,12,136,140,264,268,392,396},{16,20,144..., dimensions={0} | all-to-all | bytes 98304 | tf_op jit(solution)/shard_map/all_to_all | solution.py:27
  50.4 1.2 attend.2
  51.6 8.1 %all_to_all.51.got_ref = f32[8,16,128]{2,1,0:T(8,128)S(1)} all-to-all(f32[8,16,128]{2,1,0:T(8,128)S(1)} %bitcast.38), channel_id=1, replica_groups={{0,4,128,132,256,260,384,388},{8,12,136,140,264,268,392,396},{16,20,144..., dimensions={0} | all-to-all | bytes 131072 | tf_op jit(solution)/shard_map/all_to_all | solution.py:27
  59.7 0.8 join.2
  60.6 15.4 %all_to_all.52 = bf16[16,9,2,128]{3,2,1,0:T(2,128)(2,1)S(1)} all-to-all(bf16[16,9,2,128]{3,2,1,0:T(2,128)(2,1)S(1)} %bitcast.33), channel_id=1, replica_groups={{0,8,16,24,32,40,48,56,64,72,80,88,96,104,112,120},{4,12,20,28,36,44,52..., dimensions={0} | all-to-all | bytes 147456 | tf_op jit(solution)/shard_map/all_to_all | solution.py:27
  75.9 0.9 settle.2
  76.8 3.7 %all_gather.20.got_ref = bf16[96,128]{1,0:T(8,128)(2,1)S(1)} all-gather(bf16[48,128]{1,0:T(8,128)(2,1)S(1)} %settle.2), channel_id=1, replica_groups={{0,4},{8,12},{16,20},{24,28},{32,36},{40,44},{48,52},{56,60},{64,68},{7..., dimensions={0}, use_global_device_ids=true | all-gather | bytes 36864 | tf_op jit(solution)/shard_map/all_gather | solution.py:452
  80.6 0.8 output.2
  81.4 8.0 %all_to_all.53 = f32[4,4,128]{2,1,0:T(4,128)S(1)} all-to-all(f32[4,4,128]{2,1,0:T(4,128)S(1)} %bitcast.40), channel_id=1, replica_groups=mesh['rep'=4,'blk'=32,'tp'=4] {'tp'}, dimensions={0} | all-to-all | bytes 16384 | tf_op jit(solution)/shard_map/all_to_all | solution.py:27
  89.4 0.9 project.3
  90.3 3.4 %all-gather.1 = f32[464,128]{1,0:T(8,128)S(1)} all-gather(f32[232,128]{1,0:T(8,128)S(1)} %get-tuple-element.20), channel_id=3, replica_groups={{0,4},{8,12},{16,20},{24,28},{32,36},{40,44},{48,52},{56,60},{64,68},{7..., dimensions={0}, use_global_device_ids=true | all-gather | bytes 356352 | tf_op jit(solution)/shard_map/all_gather | solution.py:443
  94.5 14.8 %all_to_all.54 = bf16[16,17,2,128]{3,2,1,0:T(2,128)(2,1)S(1)} all-to-all(bf16[16,17,2,128]{3,2,1,0:T(2,128)(2,1)S(1)} %bitcast.30), channel_id=1, replica_groups={{0,8,16,24,32,40,48,56,64,72,80,88,96,104,112,120},{4,12,20,28,36,44,52..., dimensions={0} | all-to-all | bytes 278528 | tf_op jit(solution)/shard_map/all_to_all | solution.py:27
  109.3 0.9 finish.3
  110.2 10.7 %all_to_all.55.got_ref = bf16[8,24,128]{2,1,0:T(8,128)(2,1)S(1)} all-to-all(bf16[8,24,128]{2,1,0:T(8,128)(2,1)S(1)} %get-tuple-element.21), channel_id=1, replica_groups={{0,4,128,132,256,260,384,388},{8,12,136,140,264,268,392,396},{16,20,144..., dimensions={0} | all-to-all | bytes 98304 | tf_op jit(solution)/shard_map/all_to_all | solution.py:27
  121.0 1.2 attend.3
  122.2 8.0 %all_to_all.56.got_ref = f32[8,16,128]{2,1,0:T(8,128)S(1)} all-to-all(f32[8,16,128]{2,1,0:T(8,128)S(1)} %bitcast.37), channel_id=1, replica_groups={{0,4,128,132,256,260,384,388},{8,12,136,140,264,268,392,396},{16,20,144..., dimensions={0} | all-to-all | bytes 131072 | tf_op jit(solution)/shard_map/all_to_all | solution.py:27
  130.2 0.8 join.3
  131.0 15.3 %all_to_all.57 = bf16[16,9,2,128]{3,2,1,0:T(2,128)(2,1)S(1)} all-to-all(bf16[16,9,2,128]{3,2,1,0:T(2,128)(2,1)S(1)} %bitcast.34), channel_id=1, replica_groups={{0,8,16,24,32,40,48,56,64,72,80,88,96,104,112,120},{4,12,20,28,36,44,52..., dimensions={0} | all-to-all | bytes 147456 | tf_op jit(solution)/shard_map/all_to_all | solution.py:27
  146.2 0.9 settle.3
  147.1 3.7 %all_gather.23.got_ref = bf16[96,128]{1,0:T(8,128)(2,1)S(1)} all-gather(bf16[48,128]{1,0:T(8,128)(2,1)S(1)} %settle.3), channel_id=1, replica_groups={{0,4},{8,12},{16,20},{24,28},{32,36},{40,44},{48,52},{56,60},{64,68},{7..., dimensions={0}, use_global_device_ids=true | all-gather | bytes 36864 | tf_op jit(solution)/shard_map/all_gather | solution.py:452
  150.8 1.5 output.3
  152.3 3.2 %all-to-all-start.9 = ((f32[4,4,128]{2,1,0:T(4,128)}), f32[4,4,128]{2,1,0:T(4,128)S(1)}, u32[]{:S(2)}, u32[]{:S(2)}) async-start(f32[4,4,128]{2,1,0:T(4,128)} %bitcast.21), calls=%async_computation.9 | async-start | bytes 16384 | tf_op jit(solution)/shard_map/all_to_all | solution.py:27
  155.5 1.0 copy.16
  156.5 3.2 %all-to-all-done.9 = f32[4,4,128]{2,1,0:T(4,128)S(1)} async-done(((f32[4,4,128]{2,1,0:T(4,128)}), f32[4,4,128]{2,1,0:T(4,128)S(1)}, u32[]{:S(2)}, u32[]{:S(2)}) %all-to-all-start.9) | async-done | bytes 8224 | tf_op jit(solution)/shard_map/all_to_all | solution.py:27
  (36 shorter events, 3.0 us)
Async XLA Ops:
  0.6 0.7 copy-start.12
  0.7 0.7 copy-start.9
  0.7 0.7 copy-start.10
  0.7 0.7 copy-start.11
  1.4 0.7 copy-start.8
  1.4 0.7 copy-start.7
  2.1 1.0 copy-start.1
  3.1 1.0 copy-start.4
  4.1 46.3 %copy-start = (bf16[2,2,8,32,512]{4,3,2,1,0:T(8,128)(2,1)S(1)}, bf16[2,2,8,32,512]{4,3,2,1,0:T(8,128)(2,1)}, u32[]{:S(2)}) copy-start(bf16[2,2,8,32,512]{4,3,2,1,0:T(8,128)(2,1)} %cache_ref.3) | copy-start | bytes 3145732
  14.9 9.7 %copy-start.13 = (s32[4]{0:T(128)S(1)}, s32[4]{0:T(128)}, u32[]{:S(2)}) copy-start(s32[4]{0:T(128)} %param.23) | copy-start | bytes 52
  14.9 21.9 %all-to-all-start = ((bf16[16,17,2,128]{3,2,1,0:T(2,128)(2,1)}), bf16[16,17,2,128]{3,2,1,0:T(2,128)(2,1)S(1)}, u32[]{:S(2)}, u32[]{:S(2)}) async-start(bf16[16,17,2,128]{3,2,1,0:T(2,128)(2,1)} %bitcast.6), calls=%async_computation | async-start | bytes 278528 | tf_op jit(solution)/shard_map/all_to_all | solution.py:27
  50.4 30.1 %copy-start.6 = (bf16[2,512,64]{1,2,0:T(8,128)(2,1)S(1)}, bf16[2,512,64]{1,2,0:T(8,128)(2,1)}, u32[]{:S(2)}) copy-start(bf16[2,512,64]{1,2,0:T(8,128)(2,1)} %param.16) | copy-start | bytes 393220
  50.4 39.0 %copy-start.5 = (bf16[2,64,3,512]{3,1,2,0:T(8,128)(2,1)S(1)}, bf16[2,64,3,512]{3,1,2,0:T(8,128)(2,1)}, u32[]{:S(2)}) copy-start(bf16[2,64,3,512]{3,1,2,0:T(8,128)(2,1)} %param.14) | copy-start | bytes 1179652
  51.6 28.9 %copy-start.3 = (bf16[2,2048,64]{1,2,0:T(8,128)(2,1)S(1)}, bf16[2,2048,64]{1,2,0:T(8,128)(2,1)}, u32[]{:S(2)}) copy-start(bf16[2,2048,64]{1,2,0:T(8,128)(2,1)} %param.17) | copy-start | bytes 1572868
  60.5 28.9 %copy-start.2 = (bf16[2,64,2048]{2,1,0:T(8,128)(2,1)S(1)}, bf16[2,64,2048]{2,1,0:T(8,128)(2,1)}, u32[]{:S(2)}) copy-start(bf16[2,64,2048]{2,1,0:T(8,128)(2,1)} %wf_ref.3) | copy-start | bytes 1572868
  152.3 7.4 %all-to-all-start.9 = ((f32[4,4,128]{2,1,0:T(4,128)}), f32[4,4,128]{2,1,0:T(4,128)S(1)}, u32[]{:S(2)}, u32[]{:S(2)}) async-start(f32[4,4,128]{2,1,0:T(4,128)} %bitcast.21), calls=%async_computation.9 | async-start | bytes 16384 | tf_op jit(solution)/shard_map/all_to_all | solution.py:27

commit v8 on v7

--- a/solution.py
+++ b/solution.py
@@ -39,6 +39,10 @@
     return value if INTERPRET else pltpu.with_memory_space_constraint(value, pltpu.VMEM)
 
 
+def away(value):
+    return value if INTERPRET else pltpu.with_memory_space_constraint(value, pltpu.HBM)
+
+
 def near_out(shape, dtype):
     return jax.ShapeDtypeStruct(shape, dtype) if INTERPRET else pltpu.VMEM(shape, dtype)
 
@@ -86,12 +90,23 @@
     return jnp.sum(jnp.where(mine, row, 0.0), axis=1, keepdims=True)
 
 
-def project_kernel(layer, meta_ref, x_ref, gain_ref, wq_ref, wf_ref, *refs):
-    out_ref, state_ref = refs[-2:]
+def project_kernel(layer, x_ref, gain_ref, wq_ref, wf_ref, *refs):
     if layer == 0:
-        x = x_ref[...].astype(F32)
+        out_ref, state_ref, q_held, f_held, x_held, gain_held, sems = refs
+        copies = [
+            pltpu.make_async_copy(x_ref, x_held, sems.at[0]),
+            pltpu.make_async_copy(gain_ref, gain_held, sems.at[1]),
+            pltpu.make_async_copy(wq_ref.at[0], q_held, sems.at[2]),
+            pltpu.make_async_copy(wf_ref.at[0], f_held, sems.at[3]),
+        ]
+        for copy in copies:
+            copy.start()
+        copies[0].wait()
+        copies[1].wait()
+        x = x_held[...].astype(F32)
+        gain_ref = gain_held
     else:
-        branch_ref = refs[0]
+        branch_ref, out_ref, state_ref = refs
         x = x_ref[...] + branch_ref[0:4] + branch_ref[4:8] + branch_ref[8:12] + branch_ref[12:16]
         x = x.astype(BF16).astype(F32)[:, :HD]
     state_ref[...] = jnp.concatenate([x, jnp.zeros_like(x)], axis=1)
@@ -102,12 +117,18 @@
     rows = jnp.concatenate([centered * gain, jnp.broadcast_to(gain, (4, HD))], axis=0)
     high, low = parts_of(rows, 2)
     high, low = high.astype(BF16), low.astype(BF16)
+    if layer == 0:
+        copies[2].wait()
     for k in range(3):
-        every = dot32(high, wq_ref[layer, k]) + dot32(low, wq_ref[layer, k])
+        weights = q_held[k] if layer == 0 else wq_ref[layer, k]
+        every = dot32(high, weights) + dot32(low, weights)
         for j in range(4):
             start = 8 * (4 * k + j)
             out_ref[start : start + 8] = every[:, 128 * j : 128 * j + 128]
-    every = dot32(high, wf_ref[layer]) + dot32(low, wf_ref[layer])
+    if layer == 0:
+        copies[3].wait()
+    weights = f_held[...] if layer == 0 else wf_ref[layer]
+    every = dot32(high, weights) + dot32(low, weights)
     for j in range(16):
         out_ref[96 + 8 * j : 104 + 8 * j] = every[:, 128 * j : 128 * j + 128]
     lane = iota((4, 128), 1)
@@ -116,40 +137,50 @@
     out_ref[224:232] = jnp.broadcast_to(jnp.sum(stats, axis=0, keepdims=True), (8, 128))
 
 
-def call(kernel, name, outs, scratch, meta, *args, aliases=None):
-    specs = [pl.BlockSpec(memory_space=pltpu.SMEM)]
-    specs += [pl.BlockSpec(memory_space=pltpu.VMEM) for _ in args]
-    place = pl.BlockSpec(memory_space=pltpu.VMEM)
+def call(kernel, name, outs, scratch, tables, *args, far=(), far_outs=(), aliases=None):
+    near_spec = pl.BlockSpec(memory_space=pltpu.VMEM)
+    far_spec = pl.BlockSpec(memory_space=pl.ANY)
+    specs = [pl.BlockSpec(memory_space=pltpu.SMEM) for _ in tables]
+    specs += [far_spec if k in far else near_spec for k in range(len(args))]
+    args = [away(arg) if k in far else near(arg) for k, arg in enumerate(args)]
     return pl.pallas_call(
         kernel,
         in_specs=specs,
-        out_specs=jax.tree.map(lambda _: place, outs, is_leaf=lambda x: hasattr(x, "shape")),
-        out_shape=outs,
+        out_specs=tuple(far_spec if k in far_outs else near_spec for k in range(len(outs))),
+        out_shape=tuple(outs),
         scratch_shapes=scratch,
         input_output_aliases=aliases or {},
         compiler_params=pltpu.CompilerParams(vmem_limit_bytes=24 * 2**20),
         name=name,
         interpret=INTERPRET,
-    )(meta, *[near(arg) for arg in args])
-
-
-def project(layer, meta, x, gain, wq, wf, *branch):
+    )(*tables, *args)
+
+
+def project(layer, x, gain, wq, wf, *branch):
+    scratch = [
+        pltpu.VMEM(wq.shape[1:], BF16),
+        pltpu.VMEM(wf.shape[1:], BF16),
+        pltpu.VMEM(x.shape, x.dtype),
+        pltpu.VMEM(gain.shape, F32),
+        pltpu.SemaphoreType.DMA((4,)),
+    ]
     return call(
         functools.partial(project_kernel, layer),
         "project",
         (near_out((HALF, 128), F32), near_out((4, 128), F32)),
-        [],
-        meta,
+        scratch if layer == 0 else [],
+        (),
         x,
         gain,
         wq,
         wf,
         *branch,
-    )
-
-
-def pool_kernel(meta_ref, got_ref, out_ref, wire):
-    core = meta_ref[4, 1] % 2
+        far=(0, 1, 2, 3) if layer == 0 else (),
+    )
+
+
+def pool_kernel(got_ref, out_ref, wire):
+    core = lax.axis_index("blk") % 2
     means = [got_ref[s, 224:225] for s in range(2)]
     center = 0.5 * (means[0] + means[1])
     moves = [mean - center for mean in means]
@@ -196,18 +227,18 @@
     out_ref[...] = wire[...].astype(BF16)
 
 
-def pool(meta, got):
+def pool(got):
     return call(
         pool_kernel,
         "pool",
-        near_out((16 * FLOW, 128), BF16),
+        (near_out((16 * FLOW, 128), BF16),),
         [pltpu.VMEM((16 * FLOW, 128), F32)],
-        meta,
+        (),
         got,
-    )
-
-
-def finish_kernel(meta_ref, got_ref, factor_ref, out_ref, act_ref, wire):
+    )[0]
+
+
+def finish_kernel(got_ref, factor_ref, out_ref, act_ref, wire):
     wire[...] = got_ref[...].astype(F32)
     stats = wire[pl.ds(30, 16, stride=FLOW), :]
     stats = stats + pltpu.roll(stats, 112, 1) + pltpu.roll(stats, 96, 1)
@@ -217,7 +248,7 @@
     square_sum = pltpu.roll(jnp.sum(stats, axis=0, keepdims=True), 80, 1)
     rstd = lax.rsqrt((square_sum + spread_sum) * (1.0 / D) + EPSILON)
     upper = iota((8, 128), 0) < 4
-    pair = 2 * ((meta_ref[4, 1] // 2) % 2)
+    pair = 2 * ((lax.axis_index("blk") // 2) % 2)
     sums = [0.0] * 4
     for z in range(16):
         base = FLOW * z
@@ -239,26 +270,27 @@
     act_ref[...] = gelu(column_of(rstd, pair, 2, (2, 128)) * sums[3])
 
 
-def finish(meta, got, factors):
+def finish(got, factors):
     return call(
         finish_kernel,
         "finish",
         (near_out((8, 24, 128), BF16), near_out((2, 128), F32)),
         [pltpu.VMEM((16 * FLOW, 128), F32)],
-        meta,
+        (),
         got,
         factors,
     )
 
 
 def attend_kernel(layer, meta_ref, got_ref, cache_ref, *refs):
-    pages_ref, out_ref, kv = refs[-3:]
+    held, out_ref, kv = refs
+    rep = lax.axis_index("rep")
     tiles = []
     for tile in range(4):
         core, rows = tile // 2, 4 * (tile % 2)
         parts = [got_ref[2 * r + core, :8].astype(F32)[rows : rows + 4] for r in range(4)]
         tiles.append(jnp.concatenate(parts, axis=0))
-        new = got_ref[2 * meta_ref[4, 0] + core].astype(F32)
+        new = got_ref[2 * rep + core].astype(F32)
         for side in range(2):
             start = 8 + 8 * side + rows
             kv[side, :, 128 * tile : 128 * tile + 128] = new[start : start + 4]
@@ -267,17 +299,17 @@
     spot = iota((PAGE, 512), 0)
     for side in range(2):
         for page in range(8):
-            home = jnp.clip(meta_ref[0, page] - meta_ref[4, 0] * 4, 0, 3)
+            home = jnp.clip(meta_ref[0, page] - rep * 4, 0, 3)
             place = jnp.where(meta_ref[3, page] == 1, meta_ref[2, page], -1)
             fresh = kv[side, pl.ds(home, 1), :]
             old = cache_ref[layer, side, page].astype(F32)
-            pages_ref[layer, side, page] = jnp.where(spot == place, fresh, old).astype(BF16)
+            held[side, page] = jnp.where(spot == place, fresh, old).astype(BF16)
     head_of = iota((8, 512), 1) // HD == iota((8, 512), 0)
     wide = jnp.concatenate(
         [jnp.where(head_of, jnp.broadcast_to(row, (8, 512)), 0.0) for row in queries], axis=0
     ).astype(BF16)
-    keys = pages_ref[layer, 0].reshape(8 * PAGE, 512)
-    values = pages_ref[layer, 1].reshape(8 * PAGE, 512)
+    keys = held[0].reshape(8 * PAGE, 512)
+    values = held[1].reshape(8 * PAGE, 512)
     scores = dot_t(wide, keys) * HD ** (-0.5)
     page_of = iota((1, 256), 1) // PAGE
     owner = jnp.zeros((1, 256), jnp.int32)
@@ -304,21 +336,19 @@
     )
 
 
-def attend(layer, meta, got, caches, *pages):
+def attend(layer, meta, got, caches):
     return call(
         functools.partial(attend_kernel, layer),
         "attend",
-        (near_out(caches.shape, BF16), near_out((128, 128), F32)),
+        (near_out(caches.shape[1:], BF16), near_out((128, 128), F32)),
         [pltpu.VMEM((2, 4, 512), F32)],
-        meta,
+        (meta,),
         got,
         caches,
-        *pages,
-        aliases={3: 0} if pages else {},
-    )
-
-
-def join_kernel(meta_ref, got_ref, act_ref, out_ref, wire):
+    )
+
+
+def join_kernel(got_ref, act_ref, out_ref, wire):
     got = got_ref[...]
     high = got[:, :, HD + 1 : HD + 2]
     top = jnp.max(high, axis=0)
@@ -335,19 +365,22 @@
     out_ref[...] = wire[...].astype(BF16)
 
 
-def join(meta, got, act):
+def join(got, act):
     return call(
         join_kernel,
         "join",
-        near_out((16 * JOIN, 128), BF16),
+        (near_out((16 * JOIN, 128), BF16),),
         [pltpu.VMEM((16 * JOIN, 128), F32)],
-        meta,
+        (),
         got,
         act,
-    )
-
-
-def settle_kernel(meta_ref, got_ref, out_ref, wire, back):
+    )[0]
+
+
+def settle_kernel(layer, got_ref, held_ref, *refs):
+    pages_ref, out_ref, wire, back, sem = refs[-5:]
+    send = pltpu.make_async_copy(held_ref, pages_ref.at[layer], sem)
+    send.start()
     wire[...] = got_ref[...].astype(F32)
     parts = [wire[JOIN * z : JOIN * z + 16] for z in range(16)]
     take = lambda part, k: part[:, HD + k : HD + k + 1]
@@ -362,20 +395,30 @@
     for k in range(2):
         back[pl.ds(16 + k, 16, stride=2), :] = wire[pl.ds(16 + k, 16, stride=JOIN), :]
     out_ref[...] = back[...].astype(BF16)
-
-
-def settle(meta, got):
-    return call(
-        settle_kernel,
+    send.wait()
+
+
+def settle(layer, got, held, *pages):
+    return call(
+        functools.partial(settle_kernel, layer),
         "settle",
-        near_out((48, 128), BF16),
-        [pltpu.VMEM((16 * JOIN, 128), F32), pltpu.VMEM((48, 128), F32)],
-        meta,
+        (jax.ShapeDtypeStruct((LAYERS,) + held.shape, BF16), near_out((48, 128), BF16)),
+        [
+            pltpu.VMEM((16 * JOIN, 128), F32),
+            pltpu.VMEM((48, 128), F32),
+            pltpu.SemaphoreType.DMA,
+        ],
+        (),
         got,
-    )
-
-
-def output_kernel(layer, meta_ref, got_ref, wo_ref, wf_ref, out_ref):
+        held,
+        *pages,
+        far=(2,),
+        far_outs=(0,),
+        aliases={2: 0} if pages else {},
+    )
+
+
+def output_kernel(layer, got_ref, wo_ref, wf_ref, out_ref):
     att = jnp.concatenate([got_ref[:16], got_ref[48:64]], axis=0).astype(F32)
     att = att + pltpu.roll(att, HD, 1)
     att = jnp.concatenate([att] * 4, axis=1)
@@ -396,17 +439,17 @@
         out_ref[4 * k : 4 * k + 4] = tile
 
 
-def output(layer, meta, got, w_out, w_fc2):
+def output(layer, got, w_out, w_fc2):
     return call(
         functools.partial(output_kernel, layer),
         "output",
-        near_out((16, 128), F32),
+        (near_out((16, 128), F32),),
         [],
-        meta,
+        (),
         got,
         w_out,
         w_fc2,
-    )
+    )[0]
 
 
 def per_device(
@@ -423,34 +466,31 @@
     page_tail,
     positions,
 ):
-    rep = lax.axis_index("rep")
-    blk = lax.axis_index("blk")
     zs = [[2 * z + c for z in range(16)] for c in range(2)]
     pairs = [[2 * z, 2 * z + 1] for z in range(16)]
     rep_core = [[r * 32 + 2 * z + c for r in range(4) for c in range(2)] for z in range(16)]
 
     factors = rope_factors(positions)
     factors = jnp.concatenate([factors, factors], axis=1)
-    place = jnp.where(jnp.arange(8) == 0, rep, blk).astype(jnp.int32)
-    meta = jnp.stack([page_owner, page_used, page_fill, page_tail, place])
+    meta = jnp.stack([page_owner, page_used, page_fill, page_tail])
     w_qkv = w_qkv.transpose(0, 2, 1, 3)
     w_out = w_out.transpose(0, 2, 1)
     w_fc2 = w_fc2.transpose(0, 2, 1)
 
     state, branch, pages = hidden, (), ()
     for layer in range(LAYERS):
-        parts, state = project(layer, meta, state, ln_gain, w_qkv, w_fc1, *branch)
+        parts, state = project(layer, state, ln_gain, w_qkv, w_fc1, *branch)
         parts = lax.all_gather(parts, "blk", axis_index_groups=pairs)
-        got = exchange(pool(meta, parts).reshape(16, FLOW // 2, 2, 128), "blk", zs)
-        packed, act = finish(meta, got.reshape(16 * FLOW, 128), factors)
+        got = exchange(pool(parts).reshape(16, FLOW // 2, 2, 128), "blk", zs)
+        packed, act = finish(got.reshape(16 * FLOW, 128), factors)
         got = exchange(packed, ("rep", "blk"), rep_core)
-        fresh, parts = attend(layer, meta, got, caches, *pages)
+        held, parts = attend(layer, meta, got, caches)
+        parts = exchange(parts.reshape(8, 16, 128), ("rep", "blk"), rep_core)
+        got = exchange(join(parts, act).reshape(16, JOIN // 2, 2, 128), "blk", zs)
+        fresh, got = settle(layer, got.reshape(16 * JOIN, 128), held, *pages)
         pages = (fresh,)
-        parts = exchange(parts.reshape(8, 16, 128), ("rep", "blk"), rep_core)
-        got = exchange(join(meta, parts, act).reshape(16, JOIN // 2, 2, 128), "blk", zs)
-        got = settle(meta, got.reshape(16 * JOIN, 128))
         got = lax.all_gather(got, "blk", axis_index_groups=pairs, tiled=True)
-        out = output(layer, meta, got, w_out, w_fc2).reshape(4, 4, 128)
+        out = output(layer, got, w_out, w_fc2).reshape(4, 4, 128)
         out = exchange(out, "tp")
         branch = (out.reshape(16, 128),)
     result = (state[:, :HD] + jnp.sum(out, axis=0)[:, :HD]).astype(BF16)

time: 161 us -> 153 us (0.950)
  blocking collectives: 112 us -> 106 us
  Pallas kernels: 14 us -> 8.91 us
  starting transfers between devices: 12.9 us -> 17.9 us
  local copies, waits for them, and re-layouts: 4.41 us -> 1.37 us
    all_to_all x8, blocking collectives: 92.9 us -> 86.7 us  [exchange(): lax.all_to_all(value, axis, 0, 0, tiled=True, axis_index_groups=groups)]
    pallas_call x14, Pallas kernels: 14 us -> 8.91 us  [call(): pl.pallas_call(kernel, in_specs=specs, out_specs=tuple((far_spec if k in...]
    all_to_all x2, starting transfers between devices: 12.9 us -> 17.9 us  [exchange(): lax.all_to_all(value, axis, 0, 0, tiled=True, axis_index_groups=groups)]
    unnamed x29 -> x22, local copies, waits for them, and re-layouts: 4.39 us -> 1.37 us
  transfers between devices with their start and end apart: 2 -> 2, of which waited for: 2 -> 2; matrix products, arithmetic and copies ran while one was open for 1% -> 0% of each run, Pallas kernels for 0% -> 0%
where the time goes in v8:
time: 153 us; the launch traced here: 152 us
  blocking collectives  106 us (69%)
  starting transfers between devices  17.9 us (12%)
  waiting for transfers between devices  16.1 us (11%)
  Pallas kernels  8.91 us (6%)
    all_to_all x8, blocking collectives, exchange(): lax.all_to_all(value, axis, 0, 0, tiled=True, axis_index_groups=groups)  86.7 us
    all_to_all x2, starting transfers between devices, exchange(): lax.all_to_all(value, axis, 0, 0, tiled=True, axis_index_groups=groups)  17.9 us
    all_to_all x2, waiting for transfers between devices, exchange(): lax.all_to_all(value, axis, 0, 0, tiled=True, axis_index_groups=groups)  16.1 us
    all_gather x2, blocking collectives, per_device(): parts = lax.all_gather(parts, 'blk', axis_index_groups=pairs)  11.9 us
    pallas_call x14, Pallas kernels, call(): pl.pallas_call(kernel, in_specs=specs, out_specs=tuple((far_spec if k in...  8.91 us
    all_gather x2, blocking collectives, per_device(): got = lax.all_gather(got, 'blk', axis_index_groups=pairs, tiled=True)  7.54 us
  transfers between devices with their start and end apart: 2, of which 2 were waited for; matrix products, arithmetic and copies ran while one was open for 0% of the time, Pallas kernels for 0%

profile of v8, /device:TPU:1, one launch (start us, length us, event | category | flops | bytes accessed | tf_op | source)
XLA Modules:
  0.0 151.9 jit_solution(874909516956573134)
XLA Ops:
  0.6 1.5 project.2
  2.1 8.5 %all-gather = f32[464,128]{1,0:T(8,128)S(1)} all-gather(f32[232,128]{1,0:T(8,128)S(1)} %get-tuple-element.19), channel_id=2, replica_groups={{0,4},{8,12},{16,20},{24,28},{32,36},{40,44},{48,52},{56,60},{64,68},{7..., dimensions={0}, use_global_device_ids=true | all-gather | bytes 356352 | tf_op jit(solution)/shard_map/all_gather | solution.py:483
  10.6 0.8 pool.2
  11.4 9.7 %all-to-all-start = ((bf16[16,17,2,128]{3,2,1,0:T(2,128)(2,1)}), bf16[16,17,2,128]{3,2,1,0:T(2,128)(2,1)S(1)}, u32[]{:S(2)}, u32[]{:S(2)}) async-start(bf16[16,17,2,128]{3,2,1,0:T(2,128)(2,1)} %bitcast.6), calls=%async_computation | async-start | bytes 278528 | tf_op jit(solution)/shard_map/all_to_all | solution.py:27
  21.4 12.0 %all-to-all-done = bf16[16,17,2,128]{3,2,1,0:T(2,128)(2,1)S(1)} async-done(((bf16[16,17,2,128]{3,2,1,0:T(2,128)(2,1)}), bf16[16,17,2,128]{3,2,1,0:T(2,128)(2,1)S(1)}, u32[]{:S(2)}, u32[]{:S(2)}) %all-to-all-start) | async-done | bytes 139296 | tf_op jit(solution)/shard_map/all_to_all | solution.py:27
  33.4 0.9 finish.2
  34.3 8.2 %all-to-all-start.1 = ((bf16[8,24,128]{2,1,0:T(8,128)(2,1)}), bf16[8,24,128]{2,1,0:T(8,128)(2,1)S(1)}, u32[]{:S(2)}, u32[]{:S(2)}) async-start(bf16[8,24,128]{2,1,0:T(8,128)(2,1)} %get-tuple-element.20), calls=%async_computation.1 | async-start | bytes 98304 | tf_op jit(solution)/shard_map/all_to_all | solution.py:27
  42.5 0.6 copy-done.6
  43.2 4.1 %all-to-all-done.1.got_ref = bf16[8,24,128]{2,1,0:T(8,128)(2,1)S(1)} async-done(((bf16[8,24,128]{2,1,0:T(8,128)(2,1)}), bf16[8,24,128]{2,1,0:T(8,128)(2,1)S(1)}, u32[]{:S(2)}, u32[]{:S(2)}) %all-to-all-start.1) | async-done | bytes 49184 | tf_op jit(solution)/shard_map/all_to_all | solution.py:27
  47.3 1.2 attend.2
  48.5 8.1 %all_to_all.50.got_ref = f32[8,16,128]{2,1,0:T(8,128)S(1)} all-to-all(f32[8,16,128]{2,1,0:T(8,128)S(1)} %bitcast.38), channel_id=1, replica_groups={{0,4,128,132,256,260,384,388},{8,12,136,140,264,268,392,396},{16,20,144..., dimensions={0} | all-to-all | bytes 131072 | tf_op jit(solution)/shard_map/all_to_all | solution.py:27
  56.6 0.2 join.2
  56.8 15.3 %all_to_all.51 = bf16[16,9,2,128]{3,2,1,0:T(2,128)(2,1)S(1)} all-to-all(bf16[16,9,2,128]{3,2,1,0:T(2,128)(2,1)S(1)} %bitcast.35), channel_id=1, replica_groups={{0,8,16,24,32,40,48,56,64,72,80,88,96,104,112,120},{4,12,20,28,36,44,52..., dimensions={0} | all-to-all | bytes 147456 | tf_op jit(solution)/shard_map/all_to_all | solution.py:27
  72.0 0.8 settle.2
  72.9 3.8 %all_gather.20.got_ref = bf16[96,128]{1,0:T(8,128)(2,1)S(1)} all-gather(bf16[48,128]{1,0:T(8,128)(2,1)S(1)} %get-tuple-element.24), channel_id=1, replica_groups={{0,4},{8,12},{16,20},{24,28},{32,36},{40,44},{48,52},{56,60},{64,68},{7..., dimensions={0}, use_global_device_ids=true | all-gather | bytes 36864 | tf_op jit(solution)/shard_map/all_gather | solution.py:492
  76.7 0.3 output.2
  77.0 8.0 %all_to_all.52 = f32[4,4,128]{2,1,0:T(4,128)S(1)} all-to-all(f32[4,4,128]{2,1,0:T(4,128)S(1)} %bitcast.40), channel_id=1, replica_groups=mesh['rep'=4,'blk'=32,'tp'=4] {'tp'}, dimensions={0} | all-to-all | bytes 16384 | tf_op jit(solution)/shard_map/all_to_all | solution.py:27
  85.0 0.7 copy-done.5
  85.6 0.3 project.3
  85.9 3.4 %all-gather.1 = f32[464,128]{1,0:T(8,128)S(1)} all-gather(f32[232,128]{1,0:T(8,128)S(1)} %get-tuple-element.26), channel_id=3, replica_groups={{0,4},{8,12},{16,20},{24,28},{32,36},{40,44},{48,52},{56,60},{64,68},{7..., dimensions={0}, use_global_device_ids=true | all-gather | bytes 356352 | tf_op jit(solution)/shard_map/all_gather | solution.py:483
  89.3 0.2 pool.3
  89.5 14.8 %all_to_all.53 = bf16[16,17,2,128]{3,2,1,0:T(2,128)(2,1)S(1)} all-to-all(bf16[16,17,2,128]{3,2,1,0:T(2,128)(2,1)S(1)} %bitcast.30), channel_id=1, replica_groups={{0,8,16,24,32,40,48,56,64,72,80,88,96,104,112,120},{4,12,20,28,36,44,52..., dimensions={0} | all-to-all | bytes 278528 | tf_op jit(solution)/shard_map/all_to_all | solution.py:27
  104.4 0.3 finish.3
  104.7 10.7 %all_to_all.54.got_ref = bf16[8,24,128]{2,1,0:T(8,128)(2,1)S(1)} all-to-all(bf16[8,24,128]{2,1,0:T(8,128)(2,1)S(1)} %get-tuple-element.27), channel_id=1, replica_groups={{0,4,128,132,256,260,384,388},{8,12,136,140,264,268,392,396},{16,20,144..., dimensions={0} | all-to-all | bytes 98304 | tf_op jit(solution)/shard_map/all_to_all | solution.py:27
  115.4 1.2 attend.3
  116.6 8.0 %all_to_all.55.got_ref = f32[8,16,128]{2,1,0:T(8,128)S(1)} all-to-all(f32[8,16,128]{2,1,0:T(8,128)S(1)} %bitcast.37), channel_id=1, replica_groups={{0,4,128,132,256,260,384,388},{8,12,136,140,264,268,392,396},{16,20,144..., dimensions={0} | all-to-all | bytes 131072 | tf_op jit(solution)/shard_map/all_to_all | solution.py:27
  124.8 15.3 %all_to_all.56 = bf16[16,9,2,128]{3,2,1,0:T(2,128)(2,1)S(1)} all-to-all(bf16[16,9,2,128]{3,2,1,0:T(2,128)(2,1)S(1)} %bitcast.36), channel_id=1, replica_groups={{0,8,16,24,32,40,48,56,64,72,80,88,96,104,112,120},{4,12,20,28,36,44,52..., dimensions={0} | all-to-all | bytes 147456 | tf_op jit(solution)/shard_map/all_to_all | solution.py:27
  140.0 0.8 settle.3
  140.9 3.7 %all_gather.23.got_ref = bf16[96,128]{1,0:T(8,128)(2,1)S(1)} all-gather(bf16[48,128]{1,0:T(8,128)(2,1)S(1)} %get-tuple-element.32), channel_id=1, replica_groups={{0,4},{8,12},{16,20},{24,28},{32,36},{40,44},{48,52},{56,60},{64,68},{7..., dimensions={0}, use_global_device_ids=true | all-gather | bytes 36864 | tf_op jit(solution)/shard_map/all_gather | solution.py:492
  144.6 0.3 output.3
  144.8 6.5 %all_to_all.57 = f32[4,4,128]{2,1,0:T(4,128)S(1)} all-to-all(f32[4,4,128]{2,1,0:T(4,128)S(1)} %bitcast.41), channel_id=1, replica_groups=mesh['rep'=4,'blk'=32,'tp'=4] {'tp'}, dimensions={0} | all-to-all | bytes 16384 | tf_op jit(solution)/shard_map/all_to_all | solution.py:27
  151.3 0.6 add_convert_fusion
  (28 shorter events, 0.5 us)
Async XLA Ops:
  0.6 46.6 %copy-start = (bf16[2,2,8,32,512]{4,3,2,1,0:T(8,128)(2,1)S(1)}, bf16[2,2,8,32,512]{4,3,2,1,0:T(8,128)(2,1)}, u32[]{:S(2)}) copy-start(bf16[2,2,8,32,512]{4,3,2,1,0:T(8,128)(2,1)} %cache_ref.3) | copy-start | bytes 3145732
  11.4 9.7 %copy-start.10 = (s32[4]{0:T(128)S(1)}, s32[4]{0:T(128)}, u32[]{:S(2)}) copy-start(s32[4]{0:T(128)} %param.23) | copy-start | bytes 52
  11.4 21.9 %all-to-all-start = ((bf16[16,17,2,128]{3,2,1,0:T(2,128)(2,1)}), bf16[16,17,2,128]{3,2,1,0:T(2,128)(2,1)S(1)}, u32[]{:S(2)}, u32[]{:S(2)}) async-start(bf16[16,17,2,128]{3,2,1,0:T(2,128)(2,1)} %bitcast.6), calls=%async_computation | async-start | bytes 278528 | tf_op jit(solution)/shard_map/all_to_all | solution.py:27
  34.3 8.2 %copy-start.9 = (s32[8]{0:T(128)S(1)}, s32[8]{0:T(128)}, u32[]{:S(2)}) copy-start(s32[8]{0:T(128)} %param.19) | copy-start | bytes 100
  34.3 13.0 %all-to-all-start.1 = ((bf16[8,24,128]{2,1,0:T(8,128)(2,1)}), bf16[8,24,128]{2,1,0:T(8,128)(2,1)S(1)}, u32[]{:S(2)}, u32[]{:S(2)}) async-start(bf16[8,24,128]{2,1,0:T(8,128)(2,1)} %get-tuple-element.20), calls=%async_computation.1 | async-start | bytes 98304 | tf_op jit(solution)/shard_map/all_to_all | solution.py:27
  42.5 0.7 copy-start.6
  42.5 0.7 copy-start.7
  42.5 0.7 copy-start.8
  48.5 28.2 %copy-start.2 = (bf16[2,2048,64]{1,2,0:T(8,128)(2,1)S(1)}, bf16[2,2048,64]{1,2,0:T(8,128)(2,1)}, u32[]{:S(2)}) copy-start(bf16[2,2048,64]{1,2,0:T(8,128)(2,1)} %param.17) | copy-start | bytes 1572868
  72.0 4.7 %copy-start.4 = (bf16[2,512,64]{1,2,0:T(8,128)(2,1)S(1)}, bf16[2,512,64]{1,2,0:T(8,128)(2,1)}, u32[]{:S(2)}) copy-start(bf16[2,512,64]{1,2,0:T(8,128)(2,1)} %param.16) | copy-start | bytes 393220
  72.0 12.9 %copy-start.3 = (bf16[2,64,3,512]{3,1,2,0:T(8,128)(2,1)S(1)}, bf16[2,64,3,512]{3,1,2,0:T(8,128)(2,1)}, u32[]{:S(2)}) copy-start(bf16[2,64,3,512]{3,1,2,0:T(8,128)(2,1)} %param.14) | copy-start | bytes 1179652
  72.9 12.1 %copy-start.1 = (bf16[2,64,2048]{2,1,0:T(8,128)(2,1)S(1)}, bf16[2,64,2048]{2,1,0:T(8,128)(2,1)}, u32[]{:S(2)}) copy-start(bf16[2,64,2048]{2,1,0:T(8,128)(2,1)} %wf_ref.3) | copy-start | bytes 1572868
  84.9 0.7 copy-start.5

commit v9 on v8

--- a/solution.py
+++ b/solution.py
@@ -3,6 +3,7 @@
 
 import jax
 import jax.numpy as jnp
+import numpy as np
 from jax import lax
 from jax.experimental import pallas as pl
 from jax.experimental.pallas import tpu as pltpu
@@ -17,6 +18,9 @@
 LOWEST = -1e30
 F32 = jnp.float32
 BF16 = jnp.bfloat16
+INVERSE = [float(np.float32(10000.0 ** (-2.0 * k / ROT))) for k in range(ROT // 2)]
+TWO_PI_MIDDLE = float(np.floor((2.0 * math.pi - 6.28125) * 2.0**21) / 2.0**21)
+TWO_PI_LAST = 2.0 * math.pi - 6.28125 - TWO_PI_MIDDLE
 INTERPRET = False
 HALF = 232
 FLOW = 34
@@ -28,9 +32,15 @@
 
 
 def rope_factors(positions):
-    lane = jnp.arange(64, dtype=jnp.int32)
-    steps_f = (lane % (ROT // 2)).astype(F32)
-    angles = positions.astype(F32)[:, None] * (10000.0 ** (-2.0 * steps_f / ROT))[None, :]
+    lane = iota((positions.shape[0], 128), 1) % HD
+    inverse = jnp.zeros(lane.shape, F32)
+    for k in range(ROT // 2):
+        inverse = jnp.where(lane % (ROT // 2) == k, INVERSE[k], inverse)
+    angles = positions * inverse
+    turns = jnp.floor(angles * (1.0 / (2.0 * math.pi)) + 0.5)
+    angles = angles - turns * 6.28125
+    angles = angles - turns * TWO_PI_MIDDLE
+    angles = angles - turns * TWO_PI_LAST
     sine = jnp.sin(angles)
     return jnp.where(lane < 32, jnp.cos(angles), jnp.where(lane < 48, -sine, sine))
 
@@ -92,12 +102,14 @@
 
 def project_kernel(layer, x_ref, gain_ref, wq_ref, wf_ref, *refs):
     if layer == 0:
-        out_ref, state_ref, q_held, f_held, x_held, gain_held, sems = refs
+        pos_ref, out_ref, state_ref, gain_held, factor_ref, q_held, f_held = refs[:7]
+        x_held, pos_held, sems = refs[7:]
         copies = [
             pltpu.make_async_copy(x_ref, x_held, sems.at[0]),
             pltpu.make_async_copy(gain_ref, gain_held, sems.at[1]),
             pltpu.make_async_copy(wq_ref.at[0], q_held, sems.at[2]),
             pltpu.make_async_copy(wf_ref.at[0], f_held, sems.at[3]),
+            pltpu.make_async_copy(pos_ref, pos_held, sems.at[4]),
         ]
         for copy in copies:
             copy.start()
@@ -105,6 +117,11 @@
         copies[1].wait()
         x = x_held[...].astype(F32)
         gain_ref = gain_held
+        copies[4].wait()
+        places = jnp.broadcast_to(pos_held[...].astype(F32), (4, 4))
+        mine = iota((4, 4), 0) == iota((4, 4), 1)
+        places = jnp.sum(jnp.where(mine, places, 0.0), axis=1, keepdims=True)
+        factor_ref[...] = rope_factors(places)
     else:
         branch_ref, out_ref, state_ref = refs
         x = x_ref[...] + branch_ref[0:4] + branch_ref[4:8] + branch_ref[8:12] + branch_ref[12:16]
@@ -156,26 +173,30 @@
     )(*tables, *args)
 
 
-def project(layer, x, gain, wq, wf, *branch):
-    scratch = [
-        pltpu.VMEM(wq.shape[1:], BF16),
-        pltpu.VMEM(wf.shape[1:], BF16),
-        pltpu.VMEM(x.shape, x.dtype),
-        pltpu.VMEM(gain.shape, F32),
-        pltpu.SemaphoreType.DMA((4,)),
-    ]
+def project(layer, x, gain, wq, wf, *more):
+    outs = [near_out((HALF, 128), F32), near_out((4, 128), F32)]
+    scratch = []
+    if layer == 0:
+        outs += [near_out(gain.shape, F32), near_out((4, 128), F32)]
+        scratch = [
+            pltpu.VMEM(wq.shape[1:], BF16),
+            pltpu.VMEM(wf.shape[1:], BF16),
+            pltpu.VMEM(x.shape, x.dtype),
+            pltpu.VMEM((1, 4), jnp.int32),
+            pltpu.SemaphoreType.DMA((5,)),
+        ]
     return call(
         functools.partial(project_kernel, layer),
         "project",
-        (near_out((HALF, 128), F32), near_out((4, 128), F32)),
-        scratch if layer == 0 else [],
+        outs,
+        scratch,
         (),
         x,
         gain,
         wq,
         wf,
-        *branch,
-        far=(0, 1, 2, 3) if layer == 0 else (),
+        *more,
+        far=(0, 1, 2, 3, 4) if layer == 0 else (),
     )
 
 
@@ -282,8 +303,8 @@
     )
 
 
-def attend_kernel(layer, meta_ref, got_ref, cache_ref, *refs):
-    held, out_ref, kv = refs
+def attend_kernel(layer, owner_ref, used_ref, fill_ref, tail_ref, got_ref, cache_ref, *refs):
+    pages_ref, held, out_ref, kv, sem = refs[-5:]
     rep = lax.axis_index("rep")
     tiles = []
     for tile in range(4):
@@ -297,13 +318,16 @@
     queries = jnp.concatenate(tiles, axis=1)
     queries = [queries[i : i + 1] for i in range(16)]
     spot = iota((PAGE, 512), 0)
+    send = pltpu.make_async_copy(held.at[0], pages_ref.at[layer, 0], sem)
     for side in range(2):
         for page in range(8):
-            home = jnp.clip(meta_ref[0, page] - rep * 4, 0, 3)
-            place = jnp.where(meta_ref[3, page] == 1, meta_ref[2, page], -1)
+            home = jnp.clip(owner_ref[page] - rep * 4, 0, 3)
+            place = jnp.where(tail_ref[page] == 1, fill_ref[page], -1)
             fresh = kv[side, pl.ds(home, 1), :]
             old = cache_ref[layer, side, page].astype(F32)
             held[side, page] = jnp.where(spot == place, fresh, old).astype(BF16)
+        if side == 0:
+            send.start()
     head_of = iota((8, 512), 1) // HD == iota((8, 512), 0)
     wide = jnp.concatenate(
         [jnp.where(head_of, jnp.broadcast_to(row, (8, 512)), 0.0) for row in queries], axis=0
@@ -315,8 +339,8 @@
     owner = jnp.zeros((1, 256), jnp.int32)
     limit = jnp.zeros((1, 256), jnp.int32)
     for page in range(8):
-        length = jnp.where(meta_ref[1, page] == 1, meta_ref[2, page] + meta_ref[3, page], 0)
-        owner = jnp.where(page_of == page, meta_ref[0, page], owner)
+        length = jnp.where(used_ref[page] == 1, fill_ref[page] + tail_ref[page], 0)
+        owner = jnp.where(page_of == page, owner_ref[page], owner)
         limit = jnp.where(page_of == page, length, limit)
     owner = jnp.where(iota((1, 256), 1) % PAGE < limit, owner, -1)
     allowed = iota((128, 256), 0) // 8 == owner
@@ -334,17 +358,26 @@
     out_ref[...] = jnp.where(
         lane < HD, picked, jnp.where(lane == HD, total, jnp.where(lane == HD + 1, high, 0.0))
     )
-
-
-def attend(layer, meta, got, caches):
+    send.wait()
+
+
+def attend(layer, tables, got, caches, *pages):
     return call(
         functools.partial(attend_kernel, layer),
         "attend",
-        (near_out(caches.shape[1:], BF16), near_out((128, 128), F32)),
-        [pltpu.VMEM((2, 4, 512), F32)],
-        (meta,),
+        (
+            jax.ShapeDtypeStruct(caches.shape, BF16),
+            near_out(caches.shape[1:], BF16),
+            near_out((128, 128), F32),
+        ),
+        [pltpu.VMEM((2, 4, 512), F32), pltpu.SemaphoreType.DMA],
+        tables,
         got,
         caches,
+        *pages,
+        far=(2,),
+        far_outs=(0,),
+        aliases={6: 0} if pages else {},
     )
 
 
@@ -379,7 +412,7 @@
 
 def settle_kernel(layer, got_ref, held_ref, *refs):
     pages_ref, out_ref, wire, back, sem = refs[-5:]
-    send = pltpu.make_async_copy(held_ref, pages_ref.at[layer], sem)
+    send = pltpu.make_async_copy(held_ref.at[1], pages_ref.at[layer, 1], sem)
     send.start()
     wire[...] = got_ref[...].astype(F32)
     parts = [wire[JOIN * z : JOIN * z + 16] for z in range(16)]
@@ -398,7 +431,7 @@
     send.wait()
 
 
-def settle(layer, got, held, *pages):
+def settle(layer, got, held, pages):
     return call(
         functools.partial(settle_kernel, layer),
         "settle",
@@ -411,10 +444,10 @@
         (),
         got,
         held,
-        *pages,
+        pages,
         far=(2,),
         far_outs=(0,),
-        aliases={2: 0} if pages else {},
+        aliases={2: 0},
     )
 
 
@@ -470,29 +503,30 @@
     pairs = [[2 * z, 2 * z + 1] for z in range(16)]
     rep_core = [[r * 32 + 2 * z + c for r in range(4) for c in range(2)] for z in range(16)]
 
-    factors = rope_factors(positions)
-    factors = jnp.concatenate([factors, factors], axis=1)
-    meta = jnp.stack([page_owner, page_used, page_fill, page_tail])
+    tables = (page_owner, page_used, page_fill, page_tail)
+    more = (positions.reshape(1, 4),)
     w_qkv = w_qkv.transpose(0, 2, 1, 3)
     w_out = w_out.transpose(0, 2, 1)
     w_fc2 = w_fc2.transpose(0, 2, 1)
 
-    state, branch, pages = hidden, (), ()
+    state, gain, pages = hidden, ln_gain, ()
     for layer in range(LAYERS):
-        parts, state = project(layer, state, ln_gain, w_qkv, w_fc1, *branch)
+        parts, state, *kept = project(layer, state, gain, w_qkv, w_fc1, *more)
+        if layer == 0:
+            gain, factors = kept
         parts = lax.all_gather(parts, "blk", axis_index_groups=pairs)
         got = exchange(pool(parts).reshape(16, FLOW // 2, 2, 128), "blk", zs)
         packed, act = finish(got.reshape(16 * FLOW, 128), factors)
         got = exchange(packed, ("rep", "blk"), rep_core)
-        held, parts = attend(layer, meta, got, caches)
+        fresh, held, parts = attend(layer, tables, got, caches, *pages)
         parts = exchange(parts.reshape(8, 16, 128), ("rep", "blk"), rep_core)
         got = exchange(join(parts, act).reshape(16, JOIN // 2, 2, 128), "blk", zs)
-        fresh, got = settle(layer, got.reshape(16 * JOIN, 128), held, *pages)
+        fresh, got = settle(layer, got.reshape(16 * JOIN, 128), held, fresh)
         pages = (fresh,)
         got = lax.all_gather(got, "blk", axis_index_groups=pairs, tiled=True)
         out = output(layer, got, w_out, w_fc2).reshape(4, 4, 128)
         out = exchange(out, "tp")
-        branch = (out.reshape(16, 128),)
+        more = (out.reshape(16, 128),)
     result = (state[:, :HD] + jnp.sum(out, axis=0)[:, :HD]).astype(BF16)
     return (result, fresh)
 

time: 153 us -> 150 us (0.980)
  blocking collectives: 106 us -> 140 us
  starting transfers between devices: 17.9 us -> 0 us
  waiting for transfers between devices: 16.1 us -> 0 us
    all_to_all x8 -> x10, blocking collectives: 86.7 us -> 121 us  [exchange(): lax.all_to_all(value, axis, 0, 0, tiled=True, axis_index_groups=groups)]
    all_to_all x2 -> x0, starting transfers between devices: 17.9 us -> none  [exchange(): lax.all_to_all(value, axis, 0, 0, tiled=True, axis_index_groups=groups)]
    all_to_all x2 -> x0, waiting for transfers between devices: 16.1 us -> none  [exchange(): lax.all_to_all(value, axis, 0, 0, tiled=True, axis_index_groups=groups)]
  transfers between devices with their start and end apart: 2 -> 0, of which waited for: 2 -> 0; matrix products, arithmetic and copies ran while one was open for 0% -> 0% of each run, Pallas kernels for 0% -> 0%
where the time goes in v9:
time: 150 us
  blocking collectives  140 us (93%)
  Pallas kernels  7.87 us (5%)
    all_to_all x10, blocking collectives, exchange(): lax.all_to_all(value, axis, 0, 0, tiled=True, axis_index_groups=groups)  121 us
    all_gather x2, blocking collectives, per_device(): parts = lax.all_gather(parts, 'blk', axis_index_groups=pairs)  11.9 us
    pallas_call x14, Pallas kernels, call(): pl.pallas_call(kernel, in_specs=specs, out_specs=tuple((far_spec if k in...  7.87 us
    all_gather x2, blocking collectives, per_device(): got = lax.all_gather(got, 'blk', axis_index_groups=pairs, tiled=True)  7.54 us

profile of v9, /device:TPU:1, one launch (start us, length us, event | category | flops | bytes accessed | tf_op | source)
XLA Modules:
  0.0 149.6 jit_solution(2303317210968757001)
XLA Ops:
  0.6 1.5 %project.2 = (f32[232,128]{1,0:T(8,128)S(1)}, f32[4,128]{1,0:T(4,128)S(1)}, f32[2,64]{1,0:T(2,128)S(1)}, f32[4,128]{1,0:T(4,128)S(1)}) custom-call(bf16[4,64]{1,0:T(4,128)(2,1)} %x_ref.1, f32[2,64]{1,0:T(2,128)} %gain_ref.1, bf16[2,3,64,512]{3,2,1,0:T(8,128)(2,1)} %bitcast.21, bf16[2,64,2048]{2,1,0:T(8,128)(2,1)} %wf_ref.3, s32[1,4]{1,0:T(1,128)} %bitcast.40), custom_call_target="tpu_custom_call" | custom-call | tf_op jit(solution)/shard_map/project/pallas_call | solution.py:163
  2.2 8.5 %all-gather = f32[464,128]{1,0:T(8,128)S(1)} all-gather(f32[232,128]{1,0:T(8,128)S(1)} %get-tuple-element.24), channel_id=2, replica_groups={{0,4},{8,12},{16,20},{24,28},{32,36},{40,44},{48,52},{56,60},{64,68},{7..., dimensions={0}, use_global_device_ids=true | all-gather | bytes 356352 | tf_op jit(solution)/shard_map/all_gather | solution.py:517
  10.7 0.2 pool.2
  10.9 21.6 %all_to_all.50 = bf16[16,17,2,128]{3,2,1,0:T(2,128)(2,1)S(1)} all-to-all(bf16[16,17,2,128]{3,2,1,0:T(2,128)(2,1)S(1)} %bitcast.27), channel_id=1, replica_groups={{0,8,16,24,32,40,48,56,64,72,80,88,96,104,112,120},{4,12,20,28,36,44,52..., dimensions={0} | all-to-all | bytes 278528 | tf_op jit(solution)/shard_map/all_to_all | solution.py:31
  32.4 0.3 finish.2
  32.7 0.0 copy-start.5
  32.8 0.0 copy-start.6
  32.8 12.8 %all_to_all.51.got_ref = bf16[8,24,128]{2,1,0:T(8,128)(2,1)S(1)} all-to-all(bf16[8,24,128]{2,1,0:T(8,128)(2,1)S(1)} %get-tuple-element.26), channel_id=1, replica_groups={{0,4,128,132,256,260,384,388},{8,12,136,140,264,268,392,396},{16,20,144..., dimensions={0} | all-to-all | bytes 98304 | tf_op jit(solution)/shard_map/all_to_all | solution.py:31
  45.6 1.4 attend.2
  47.0 8.0 %all_to_all.52.got_ref = f32[8,16,128]{2,1,0:T(8,128)S(1)} all-to-all(f32[8,16,128]{2,1,0:T(8,128)S(1)} %bitcast.36), channel_id=1, replica_groups={{0,4,128,132,256,260,384,388},{8,12,136,140,264,268,392,396},{16,20,144..., dimensions={0} | all-to-all | bytes 131072 | tf_op jit(solution)/shard_map/all_to_all | solution.py:31
  54.9 0.2 join.2
  55.1 15.3 %all_to_all.53 = bf16[16,9,2,128]{3,2,1,0:T(2,128)(2,1)S(1)} all-to-all(bf16[16,9,2,128]{3,2,1,0:T(2,128)(2,1)S(1)} %bitcast.33), channel_id=1, replica_groups={{0,8,16,24,32,40,48,56,64,72,80,88,96,104,112,120},{4,12,20,28,36,44,52..., dimensions={0} | all-to-all | bytes 147456 | tf_op jit(solution)/shard_map/all_to_all | solution.py:31
  70.4 0.7 settle.2
  71.1 0.0 copy-start.1
  71.1 3.8 %all_gather.20.got_ref = bf16[96,128]{1,0:T(8,128)(2,1)S(1)} all-gather(bf16[48,128]{1,0:T(8,128)(2,1)S(1)} %get-tuple-element.31), channel_id=1, replica_groups={{0,4},{8,12},{16,20},{24,28},{32,36},{40,44},{48,52},{56,60},{64,68},{7..., dimensions={0}, use_global_device_ids=true | all-gather | bytes 36864 | tf_op jit(solution)/shard_map/all_gather | solution.py:526
  75.0 0.2 output.2
  75.2 8.0 %all_to_all.54 = f32[4,4,128]{2,1,0:T(4,128)S(1)} all-to-all(f32[4,4,128]{2,1,0:T(4,128)S(1)} %bitcast.38), channel_id=1, replica_groups=mesh['rep'=4,'blk'=32,'tp'=4] {'tp'}, dimensions={0} | all-to-all | bytes 16384 | tf_op jit(solution)/shard_map/all_to_all | solution.py:31
  83.2 0.3 project.3
  83.5 3.4 %all-gather.1 = f32[464,128]{1,0:T(8,128)S(1)} all-gather(f32[232,128]{1,0:T(8,128)S(1)} %get-tuple-element.33), channel_id=3, replica_groups={{0,4},{8,12},{16,20},{24,28},{32,36},{40,44},{48,52},{56,60},{64,68},{7..., dimensions={0}, use_global_device_ids=true | all-gather | bytes 356352 | tf_op jit(solution)/shard_map/all_gather | solution.py:517
  86.9 0.2 pool.3
  87.1 14.8 %all_to_all.55 = bf16[16,17,2,128]{3,2,1,0:T(2,128)(2,1)S(1)} all-to-all(bf16[16,17,2,128]{3,2,1,0:T(2,128)(2,1)S(1)} %bitcast.28), channel_id=1, replica_groups={{0,8,16,24,32,40,48,56,64,72,80,88,96,104,112,120},{4,12,20,28,36,44,52..., dimensions={0} | all-to-all | bytes 278528 | tf_op jit(solution)/shard_map/all_to_all | solution.py:31
  102.0 0.3 finish.3
  102.3 10.7 %all_to_all.56.got_ref = bf16[8,24,128]{2,1,0:T(8,128)(2,1)S(1)} all-to-all(bf16[8,24,128]{2,1,0:T(8,128)(2,1)S(1)} %get-tuple-element.34), channel_id=1, replica_groups={{0,4,128,132,256,260,384,388},{8,12,136,140,264,268,392,396},{16,20,144..., dimensions={0} | all-to-all | bytes 98304 | tf_op jit(solution)/shard_map/all_to_all | solution.py:31
  113.0 1.4 attend.3
  114.4 8.0 %all_to_all.57.got_ref = f32[8,16,128]{2,1,0:T(8,128)S(1)} all-to-all(f32[8,16,128]{2,1,0:T(8,128)S(1)} %bitcast.35), channel_id=1, replica_groups={{0,4,128,132,256,260,384,388},{8,12,136,140,264,268,392,396},{16,20,144..., dimensions={0} | all-to-all | bytes 131072 | tf_op jit(solution)/shard_map/all_to_all | solution.py:31
  122.4 0.2 join.3
  122.6 15.3 %all_to_all.58 = bf16[16,9,2,128]{3,2,1,0:T(2,128)(2,1)S(1)} all-to-all(bf16[16,9,2,128]{3,2,1,0:T(2,128)(2,1)S(1)} %bitcast.34), channel_id=1, replica_groups={{0,8,16,24,32,40,48,56,64,72,80,88,96,104,112,120},{4,12,20,28,36,44,52..., dimensions={0} | all-to-all | bytes 147456 | tf_op jit(solution)/shard_map/all_to_all | solution.py:31
  137.8 0.7 settle.3
  138.5 3.7 %all_gather.23.got_ref = bf16[96,128]{1,0:T(8,128)(2,1)S(1)} all-gather(bf16[48,128]{1,0:T(8,128)(2,1)S(1)} %get-tuple-element.40), channel_id=1, replica_groups={{0,4},{8,12},{16,20},{24,28},{32,36},{40,44},{48,52},{56,60},{64,68},{7..., dimensions={0}, use_global_device_ids=true | all-gather | bytes 36864 | tf_op jit(solution)/shard_map/all_gather | solution.py:526
  142.2 0.2 output.3
  142.5 6.5 %all_to_all.59 = f32[4,4,128]{2,1,0:T(4,128)S(1)} all-to-all(f32[4,4,128]{2,1,0:T(4,128)S(1)} %bitcast.39), channel_id=1, replica_groups=mesh['rep'=4,'blk'=32,'tp'=4] {'tp'}, dimensions={0} | all-to-all | bytes 16384 | tf_op jit(solution)/shard_map/all_to_all | solution.py:31
  149.0 0.6 add_convert_fusion
  (16 shorter events, 0.0 us)
Async XLA Ops:
  0.6 44.9 %copy-start = (bf16[2,2,8,32,512]{4,3,2,1,0:T(8,128)(2,1)S(1)}, bf16[2,2,8,32,512]{4,3,2,1,0:T(8,128)(2,1)}, u32[]{:S(2)}) copy-start(bf16[2,2,8,32,512]{4,3,2,1,0:T(8,128)(2,1)} %cache_ref.3) | copy-start | bytes 3145732
  32.7 12.8 %copy-start.5 = (s32[8]{0:T(128)S(1)}, s32[8]{0:T(128)}, u32[]{:S(2)}) copy-start(s32[8]{0:T(128)} %owner_ref.3) | copy-start | bytes 100
  32.8 12.8 %copy-start.6 = (s32[8]{0:T(128)S(1)}, s32[8]{0:T(128)}, u32[]{:S(2)}) copy-start(s32[8]{0:T(128)} %used_ref.3) | copy-start | bytes 100
  32.8 12.8 %copy-start.7 = (s32[8]{0:T(128)S(1)}, s32[8]{0:T(128)}, u32[]{:S(2)}) copy-start(s32[8]{0:T(128)} %fill_ref.3) | copy-start | bytes 100
  32.8 12.8 %copy-start.8 = (s32[8]{0:T(128)S(1)}, s32[8]{0:T(128)}, u32[]{:S(2)}) copy-start(s32[8]{0:T(128)} %tail_ref.3) | copy-start | bytes 100
  70.4 4.6 %copy-start.2 = (bf16[2,2048,64]{1,2,0:T(8,128)(2,1)S(1)}, bf16[2,2048,64]{1,2,0:T(8,128)(2,1)}, u32[]{:S(2)}) copy-start(bf16[2,2048,64]{1,2,0:T(8,128)(2,1)} %param.17) | copy-start | bytes 1572868
  70.4 4.6 %copy-start.4 = (bf16[2,512,64]{1,2,0:T(8,128)(2,1)S(1)}, bf16[2,512,64]{1,2,0:T(8,128)(2,1)}, u32[]{:S(2)}) copy-start(bf16[2,512,64]{1,2,0:T(8,128)(2,1)} %param.16) | copy-start | bytes 393220
  70.4 12.8 %copy-start.3 = (bf16[2,64,3,512]{3,1,2,0:T(8,128)(2,1)S(1)}, bf16[2,64,3,512]{3,1,2,0:T(8,128)(2,1)}, u32[]{:S(2)}) copy-start(bf16[2,64,3,512]{3,1,2,0:T(8,128)(2,1)} %param.14) | copy-start | bytes 1179652
  71.1 12.1 %copy-start.1 = (bf16[2,64,2048]{2,1,0:T(8,128)(2,1)S(1)}, bf16[2,64,2048]{2,1,0:T(8,128)(2,1)}, u32[]{:S(2)}) copy-start(bf16[2,64,2048]{2,1,0:T(8,128)(2,1)} %wf_ref.3) | copy-start | bytes 1572868

commit v10 on v9

--- a/solution.py
+++ b/solution.py
@@ -23,8 +23,8 @@
 TWO_PI_LAST = 2.0 * math.pi - 6.28125 - TWO_PI_MIDDLE
 INTERPRET = False
 HALF = 232
-FLOW = 34
-JOIN = 18
+FLOW = 16
+JOIN = 20
 
 
 def exchange(value, axis, groups=None):
@@ -200,7 +200,7 @@
     )
 
 
-def pool_kernel(got_ref, out_ref, wire):
+def pool_kernel(got_ref, out_ref):
     core = lax.axis_index("blk") % 2
     means = [got_ref[s, 224:225] for s in range(2)]
     center = 0.5 * (means[0] + means[1])
@@ -218,13 +218,13 @@
             total = total + part + shift[s] * part[4:5]
         return total
 
-    common = []
+    merged = []
     columns = []
     for base in (0, 32, 64):
         one = block(base + 16 * core)
         two = block(base + 16 * core + 8)
-        common.append(jnp.where(upper, one, pltpu.roll(two, 4, 0)))
-        columns += [one[4:5], two[4:5]]
+        merged.append(jnp.where(upper, one, pltpu.roll(two, 4, 0)))
+        columns.append((one[4:5], two[4:5]))
     lane = iota((4, 128), 1)
     request = iota((4, 128), 0)
     stats = jnp.zeros((4, 128), F32)
@@ -232,20 +232,26 @@
     both += parts_of(column_of(square, 0, 4, (4, 128)), 3)
     for k, part in enumerate(both):
         stats = jnp.where(lane == request + 16 * k, part, stats)
-    columns.append(jnp.sum(stats, axis=0, keepdims=True))
+    stats = jnp.sum(stats, axis=0, keepdims=True)
     row = iota((8, 128), 0)
-    tail = jnp.zeros((8, 128), F32)
-    for k, column in enumerate(columns):
-        tail = jnp.where(row == k, column, tail)
-    shared = jnp.concatenate(common, axis=0)
+    base = jnp.where(row == 0, columns[0][0], jnp.where(row == 1, columns[0][1], stats))
     for m in range(8):
         last = block(96 + 64 * core + 8 * m)
-        whole = jnp.concatenate([shared, jnp.where(row == 7, last[4:5], tail)], axis=0)
         for k in range(2):
-            start = FLOW * (2 * m + k)
-            wire[start : start + 32] = whole
-            wire[start + 32 : start + 34] = last[2 * k : 2 * k + 2]
-    out_ref[...] = wire[...].astype(BF16)
+            z = 2 * m + k
+            side, slot = 1 + z // 8, z % 8
+            rows = (
+                merged[side][slot : slot + 1],
+                columns[side][slot // 4],
+                last[4:5],
+                last[2 * k : 2 * k + 1],
+                last[2 * k + 1 : 2 * k + 2],
+            )
+            tail = base
+            for j, value in enumerate(rows):
+                tail = jnp.where(row == 3 + j, value, tail)
+            whole = jnp.concatenate([merged[0], tail], axis=0)
+            out_ref[FLOW * z : FLOW * z + FLOW] = whole.astype(BF16)
 
 
 def pool(got):
@@ -253,15 +259,15 @@
         pool_kernel,
         "pool",
         (near_out((16 * FLOW, 128), BF16),),
-        [pltpu.VMEM((16 * FLOW, 128), F32)],
+        [],
         (),
         got,
     )[0]
 
 
-def finish_kernel(got_ref, factor_ref, out_ref, act_ref, wire):
-    wire[...] = got_ref[...].astype(F32)
-    stats = wire[pl.ds(30, 16, stride=FLOW), :]
+def finish_kernel(got_ref, factor_ref, out_ref, held_ref, extra_ref):
+    blocks = [got_ref[FLOW * z : FLOW * z + FLOW].astype(F32) for z in range(16)]
+    stats = jnp.concatenate([block[10:11] for block in blocks], axis=0)
     stats = stats + pltpu.roll(stats, 112, 1) + pltpu.roll(stats, 96, 1)
     average = jnp.sum(stats, axis=0, keepdims=True) * (1.0 / 16)
     offset = stats - average
@@ -269,87 +275,75 @@
     square_sum = pltpu.roll(jnp.sum(stats, axis=0, keepdims=True), 80, 1)
     rstd = lax.rsqrt((square_sum + spread_sum) * (1.0 / D) + EPSILON)
     upper = iota((8, 128), 0) < 4
-    pair = 2 * ((lax.axis_index("blk") // 2) % 2)
-    sums = [0.0] * 4
-    for z in range(16):
-        base = FLOW * z
+    here = lax.axis_index("blk") // 2
+    pair, single = 2 * (here % 2), here % 4
+    query, entry, inner = 0.0, 0.0, 0.0
+    for z, block in enumerate(blocks):
         move = offset[z : z + 1]
-        mine = column_of(move, 0, 4, (8, 128))
-        tail = wire[base + 24 : base + 32]
-        for k in range(3):
-            part = wire[base + 8 * k : base + 8 * k + 8]
-            column = jnp.where(upper, tail[2 * k : 2 * k + 1], tail[2 * k + 1 : 2 * k + 2])
-            sums[k] = sums[k] + part + mine * column
-        part = wire[base + 32 : base + 34]
-        sums[3] = sums[3] + part + column_of(move, pair, 2, (2, 128)) * tail[7:8]
-    mine = column_of(rstd, 0, 4, (8, 128))
-    factors = jnp.concatenate([factor_ref[...], factor_ref[...]], axis=0)
-    packed = [rope(mine * sums[k], factors) for k in range(2)] + [mine * sums[2]]
-    packed = jnp.concatenate(packed, axis=0).astype(BF16)
+        column = jnp.where(upper, block[8:9], block[9:10])
+        query = query + block[:8] + column_of(move, 0, 4, (8, 128)) * column
+        entry = entry + block[11:12] + column_of(move, single, 1, (1, 128)) * block[12:13]
+        inner = inner + block[14:16] + column_of(move, pair, 2, (2, 128)) * block[13:14]
+    query = column_of(rstd, 0, 4, (8, 128)) * query
+    query = rope(query, jnp.concatenate([factor_ref[...], factor_ref[...]], axis=0)).astype(BF16)
     for k in range(8):
-        out_ref[k] = packed
-    act_ref[...] = gelu(column_of(rstd, pair, 2, (2, 128)) * sums[3])
+        out_ref[k] = query
+    held_ref[...] = query.astype(F32)
+    entry = column_of(rstd, single, 1, (1, 128)) * entry
+    turned = rope(entry, factor_ref[pl.ds(single, 1), :])
+    extra_ref[0:2] = gelu(column_of(rstd, pair, 2, (2, 128)) * inner)
+    extra_ref[2:3] = jnp.where(jnp.full((1, 128), here) < 8, turned, entry)
+    extra_ref[3:4] = jnp.zeros((1, 128), F32)
 
 
 def finish(got, factors):
     return call(
         finish_kernel,
         "finish",
-        (near_out((8, 24, 128), BF16), near_out((2, 128), F32)),
-        [pltpu.VMEM((16 * FLOW, 128), F32)],
+        (near_out((8, 8, 128), BF16), near_out((8, 128), F32), near_out((4, 128), F32)),
+        [],
         (),
         got,
         factors,
     )
 
 
-def attend_kernel(layer, owner_ref, used_ref, fill_ref, tail_ref, got_ref, cache_ref, *refs):
-    pages_ref, held, out_ref, kv, sem = refs[-5:]
-    rep = lax.axis_index("rep")
+def attend_kernel(layer, owner_ref, used_ref, fill_ref, got_ref, cache_ref, out_ref):
     tiles = []
     for tile in range(4):
         core, rows = tile // 2, 4 * (tile % 2)
-        parts = [got_ref[2 * r + core, :8].astype(F32)[rows : rows + 4] for r in range(4)]
+        parts = [got_ref[2 * r + core].astype(F32)[rows : rows + 4] for r in range(4)]
         tiles.append(jnp.concatenate(parts, axis=0))
-        new = got_ref[2 * rep + core].astype(F32)
-        for side in range(2):
-            start = 8 + 8 * side + rows
-            kv[side, :, 128 * tile : 128 * tile + 128] = new[start : start + 4]
     queries = jnp.concatenate(tiles, axis=1)
-    queries = [queries[i : i + 1] for i in range(16)]
-    spot = iota((PAGE, 512), 0)
-    send = pltpu.make_async_copy(held.at[0], pages_ref.at[layer, 0], sem)
-    for side in range(2):
-        for page in range(8):
-            home = jnp.clip(owner_ref[page] - rep * 4, 0, 3)
-            place = jnp.where(tail_ref[page] == 1, fill_ref[page], -1)
-            fresh = kv[side, pl.ds(home, 1), :]
-            old = cache_ref[layer, side, page].astype(F32)
-            held[side, page] = jnp.where(spot == place, fresh, old).astype(BF16)
-        if side == 0:
-            send.start()
-    head_of = iota((8, 512), 1) // HD == iota((8, 512), 0)
-    wide = jnp.concatenate(
-        [jnp.where(head_of, jnp.broadcast_to(row, (8, 512)), 0.0) for row in queries], axis=0
-    ).astype(BF16)
-    keys = held[0].reshape(8 * PAGE, 512)
-    values = held[1].reshape(8 * PAGE, 512)
+    place = iota((8, 512), 0)
+    wide = []
+    for rep in range(4):
+        for core in range(2):
+            for i in (0, 2):
+                row = 4 * rep + i
+                both = jnp.where(place < 4, queries[row : row + 1], queries[row + 1 : row + 2])
+                mine = iota((8, 512), 1) // HD == 4 * core + place % 4
+                wide.append(jnp.where(mine, both, 0.0))
+    wide = jnp.concatenate(wide, axis=0).astype(BF16)
+    keys = cache_ref[layer, 0].reshape(8 * PAGE, 512)
+    values = cache_ref[layer, 1].reshape(8 * PAGE, 512)
     scores = dot_t(wide, keys) * HD ** (-0.5)
     page_of = iota((1, 256), 1) // PAGE
     owner = jnp.zeros((1, 256), jnp.int32)
     limit = jnp.zeros((1, 256), jnp.int32)
     for page in range(8):
-        length = jnp.where(used_ref[page] == 1, fill_ref[page] + tail_ref[page], 0)
+        length = jnp.where(used_ref[page] == 1, fill_ref[page], 0)
         owner = jnp.where(page_of == page, owner_ref[page], owner)
         limit = jnp.where(page_of == page, length, limit)
     owner = jnp.where(iota((1, 256), 1) % PAGE < limit, owner, -1)
-    allowed = iota((128, 256), 0) // 8 == owner
+    pair = iota((128, 256), 0)
+    allowed = 4 * (pair // 32) + pair % 16 // 4 == owner
     scores = jnp.where(allowed, scores, LOWEST)
     high = jnp.max(scores, axis=1, keepdims=True)
     weights = jnp.where(allowed, jnp.exp(scores - high), 0.0)
     total = jnp.sum(weights, axis=1, keepdims=True)
     mixed = dot32(weights.astype(BF16), values)
-    head = iota((128, 128), 0) % 8
+    head = iota((128, 128), 0) // 16 % 2 * 4 + iota((128, 128), 0) % 4
     lane = iota((128, 128), 1)
     picked = mixed[:, :128]
     for k in range(1, 4):
@@ -358,27 +352,18 @@
     out_ref[...] = jnp.where(
         lane < HD, picked, jnp.where(lane == HD, total, jnp.where(lane == HD + 1, high, 0.0))
     )
-    send.wait()
-
-
-def attend(layer, tables, got, caches, *pages):
+
+
+def attend(layer, tables, got, caches):
     return call(
         functools.partial(attend_kernel, layer),
         "attend",
-        (
-            jax.ShapeDtypeStruct(caches.shape, BF16),
-            near_out(caches.shape[1:], BF16),
-            near_out((128, 128), F32),
-        ),
-        [pltpu.VMEM((2, 4, 512), F32), pltpu.SemaphoreType.DMA],
+        (near_out((128, 128), F32),),
+        [],
         tables,
         got,
         caches,
-        *pages,
-        far=(2,),
-        far_outs=(0,),
-        aliases={6: 0} if pages else {},
-    )
+    )[0]
 
 
 def join_kernel(got_ref, act_ref, out_ref, wire):
@@ -394,7 +379,7 @@
     act = act_ref[...]
     for z in range(16):
         wire[JOIN * z : JOIN * z + 16] = out
-        wire[JOIN * z + 16 : JOIN * z + 18] = act
+        wire[JOIN * z + 16 : JOIN * z + 20] = act
     out_ref[...] = wire[...].astype(BF16)
 
 
@@ -410,16 +395,25 @@
     )[0]
 
 
-def settle_kernel(layer, got_ref, held_ref, *refs):
-    pages_ref, out_ref, wire, back, sem = refs[-5:]
-    send = pltpu.make_async_copy(held_ref.at[1], pages_ref.at[layer, 1], sem)
-    send.start()
+def settle_kernel(got_ref, query_ref, out_ref, wire, back, score, fresh):
     wire[...] = got_ref[...].astype(F32)
+    entries = wire[pl.ds(18, 16, stride=JOIN), :]
+    product = query_ref[...] * entries[:8]
+    left = iota((8, 128), 1) < HD
+    for half in range(2):
+        summed = jnp.sum(jnp.where(left == (half == 0), product, 0.0), axis=1, keepdims=True)
+        summed = jnp.broadcast_to(summed * HD ** (-0.5), (8, 128))
+        value = entries[8:] if half == 0 else pltpu.roll(entries[8:], HD, 1)
+        for j in range(2):
+            score[pl.ds(2 * j + half, 4, stride=4), :] = summed[4 * j : 4 * j + 4]
+            fresh[pl.ds(2 * j + half, 4, stride=4), :] = value[4 * j : 4 * j + 4]
     parts = [wire[JOIN * z : JOIN * z + 16] for z in range(16)]
     take = lambda part, k: part[:, HD + k : HD + k + 1]
     highs = [take(part, 3) + take(part, 4) + take(part, 5) for part in parts]
-    top = functools.reduce(jnp.maximum, highs)
-    total, mixed = 0.0, 0.0
+    own = score[:, 0:1]
+    top = functools.reduce(jnp.maximum, highs, own)
+    total = jnp.exp(own - top)
+    mixed = fresh[...] * total
     for part, high in zip(parts, highs):
         factor = jnp.exp(high - top)
         total = total + (take(part, 0) + take(part, 1) + take(part, 2)) * factor
@@ -427,43 +421,85 @@
     back[:16] = jnp.where(iota((16, 128), 1) < HD, mixed / total, 0.0)
     for k in range(2):
         back[pl.ds(16 + k, 16, stride=2), :] = wire[pl.ds(16 + k, 16, stride=JOIN), :]
+    back[48:] = entries
     out_ref[...] = back[...].astype(BF16)
-    send.wait()
-
-
-def settle(layer, got, held, pages):
-    return call(
-        functools.partial(settle_kernel, layer),
+
+
+def settle(got, query):
+    return call(
+        settle_kernel,
         "settle",
-        (jax.ShapeDtypeStruct((LAYERS,) + held.shape, BF16), near_out((48, 128), BF16)),
+        (near_out((64, 128), BF16),),
         [
             pltpu.VMEM((16 * JOIN, 128), F32),
-            pltpu.VMEM((48, 128), F32),
-            pltpu.SemaphoreType.DMA,
+            pltpu.VMEM((64, 128), F32),
+            pltpu.VMEM((16, 128), F32),
+            pltpu.VMEM((16, 128), F32),
         ],
         (),
         got,
-        held,
-        pages,
-        far=(2,),
+        query,
+    )[0]
+
+
+def renew_kernel(owner_ref, fill_ref, tail_ref, one_ref, two_ref, cache_ref, pages_ref, held, kv, sems):
+    rep = lax.axis_index("rep")
+    spot = iota((PAGE, 512), 0)
+    sends = []
+    for layer, got_ref in enumerate((one_ref, two_ref)):
+        for tile in range(4):
+            start = 64 * (tile // 2) + 48
+            new = got_ref[start : start + 16].astype(F32)
+            for side in range(2):
+                rows = 8 * side + 4 * (tile % 2)
+                kv[side, :, 128 * tile : 128 * tile + 128] = new[rows : rows + 4]
+        for side in range(2):
+            for page in range(8):
+                home = jnp.clip(owner_ref[page] - rep * 4, 0, 3)
+                place = jnp.where(tail_ref[page] == 1, fill_ref[page], -1)
+                fresh = kv[side, pl.ds(home, 1), :]
+                old = cache_ref[layer, side, page].astype(F32)
+                held[layer, side, page] = jnp.where(spot == place, fresh, old).astype(BF16)
+        sends.append(
+            pltpu.make_async_copy(held.at[layer], pages_ref.at[layer], sems.at[layer])
+        )
+        sends[-1].start()
+    for send in sends:
+        send.wait()
+
+
+def renew(tables, one, two, caches):
+    return call(
+        renew_kernel,
+        "renew",
+        (jax.ShapeDtypeStruct(caches.shape, BF16),),
+        [
+            pltpu.VMEM(caches.shape, BF16),
+            pltpu.VMEM((2, 4, 512), F32),
+            pltpu.SemaphoreType.DMA((2,)),
+        ],
+        tables,
+        one,
+        two,
+        caches,
         far_outs=(0,),
-        aliases={2: 0},
-    )
+    )[0]
 
 
 def output_kernel(layer, got_ref, wo_ref, wf_ref, out_ref):
-    att = jnp.concatenate([got_ref[:16], got_ref[48:64]], axis=0).astype(F32)
+    att = jnp.concatenate([got_ref[:16], got_ref[64:80]], axis=0).astype(F32)
     att = att + pltpu.roll(att, HD, 1)
     att = jnp.concatenate([att] * 4, axis=1)
-    own = iota((32, 512), 1) // HD == iota((32, 512), 0) % 8
+    own = iota((32, 512), 1) // HD == iota((32, 512), 0) // 16 * 4 + iota((32, 512), 0) % 4
     by_head = dot_t(jnp.where(own, att, 0.0).astype(BF16), wo_ref[layer])
     tiles = []
     for core in range(2):
-        act = got_ref[48 * core + 16 : 48 * core + 48].astype(F32)
+        act = got_ref[64 * core + 16 : 64 * core + 48].astype(F32)
         tiles += [act[4 * m : 4 * m + 4] for m in range(8)]
     mlp = dot_t(jnp.concatenate(tiles, axis=1).astype(BF16), wf_ref[layer])
     rows = [
-        jnp.sum(by_head[8 * i : 8 * i + 8], axis=0, keepdims=True) + mlp[i : i + 1]
+        jnp.sum(by_head[4 * i : 4 * i + 4] + by_head[16 + 4 * i : 20 + 4 * i], axis=0, keepdims=True)
+        + mlp[i : i + 1]
         for i in range(4)
     ]
     tile = jnp.concatenate(rows, axis=0)
@@ -503,32 +539,31 @@
     pairs = [[2 * z, 2 * z + 1] for z in range(16)]
     rep_core = [[r * 32 + 2 * z + c for r in range(4) for c in range(2)] for z in range(16)]
 
-    tables = (page_owner, page_used, page_fill, page_tail)
     more = (positions.reshape(1, 4),)
     w_qkv = w_qkv.transpose(0, 2, 1, 3)
     w_out = w_out.transpose(0, 2, 1)
     w_fc2 = w_fc2.transpose(0, 2, 1)
 
-    state, gain, pages = hidden, ln_gain, ()
+    state, gain, joined = hidden, ln_gain, []
     for layer in range(LAYERS):
         parts, state, *kept = project(layer, state, gain, w_qkv, w_fc1, *more)
         if layer == 0:
             gain, factors = kept
         parts = lax.all_gather(parts, "blk", axis_index_groups=pairs)
         got = exchange(pool(parts).reshape(16, FLOW // 2, 2, 128), "blk", zs)
-        packed, act = finish(got.reshape(16 * FLOW, 128), factors)
+        packed, query, extra = finish(got.reshape(16 * FLOW, 128), factors)
         got = exchange(packed, ("rep", "blk"), rep_core)
-        fresh, held, parts = attend(layer, tables, got, caches, *pages)
+        parts = attend(layer, (page_owner, page_used, page_fill), got, caches)
         parts = exchange(parts.reshape(8, 16, 128), ("rep", "blk"), rep_core)
-        got = exchange(join(parts, act).reshape(16, JOIN // 2, 2, 128), "blk", zs)
-        fresh, got = settle(layer, got.reshape(16 * JOIN, 128), held, fresh)
-        pages = (fresh,)
+        got = exchange(join(parts, extra).reshape(16, JOIN // 2, 2, 128), "blk", zs)
+        got = settle(got.reshape(16 * JOIN, 128), query)
         got = lax.all_gather(got, "blk", axis_index_groups=pairs, tiled=True)
+        joined.append(got)
         out = output(layer, got, w_out, w_fc2).reshape(4, 4, 128)
         out = exchange(out, "tp")
         more = (out.reshape(16, 128),)
     result = (state[:, :HD] + jnp.sum(out, axis=0)[:, :HD]).astype(BF16)
-    return (result, fresh)
+    return (result, renew((page_owner, page_fill, page_tail), *joined, caches))
 
 
 def solution(mesh):

time: 150 us -> 145 us (0.967)
  blocking collectives: 140 us -> 128 us
  starting transfers between devices: 0 us -> 3.35 us
  waiting for transfers between devices: 0 us -> 2.46 us
    all_to_all x10 -> x9, blocking collectives: 121 us -> 108 us  [exchange(): lax.all_to_all(value, axis, 0, 0, tiled=True, axis_index_groups=groups)]
    all_to_all x0 -> x1, starting transfers between devices: none -> 3.35 us  [exchange(): lax.all_to_all(value, axis, 0, 0, tiled=True, axis_index_groups=groups)]
    all_to_all x0 -> x1, waiting for transfers between devices: none -> 2.46 us  [exchange(): lax.all_to_all(value, axis, 0, 0, tiled=True, axis_index_groups=groups)]
    pallas_call x14 -> x15, Pallas kernels: 7.87 us -> 9.18 us  [call(): pl.pallas_call(kernel, in_specs=specs, out_specs=tuple((far_spec if k in...]
  transfers between devices with their start and end apart: 0 -> 1, of which waited for: 0 -> 1; matrix products, arithmetic and copies ran while one was open for 0% -> 0% of each run, Pallas kernels for 0% -> 1%
where the time goes in v10:
time: 145 us; the launch traced here: 144 us
  blocking collectives  128 us (88%)
  Pallas kernels  9.18 us (6%)
  starting transfers between devices  3.35 us (2%)
  waiting for transfers between devices  2.46 us (2%)
    all_to_all x9, blocking collectives, exchange(): lax.all_to_all(value, axis, 0, 0, tiled=True, axis_index_groups=groups)  108 us
    all_gather x2, blocking collectives, per_device(): parts = lax.all_gather(parts, 'blk', axis_index_groups=pairs)  11.9 us
    pallas_call x15, Pallas kernels, call(): pl.pallas_call(kernel, in_specs=specs, out_specs=tuple((far_spec if k in...  9.18 us
    all_gather x2, blocking collectives, per_device(): got = lax.all_gather(got, 'blk', axis_index_groups=pairs, tiled=True)  7.8 us
    all_to_all x1, starting transfers between devices, exchange(): lax.all_to_all(value, axis, 0, 0, tiled=True, axis_index_groups=groups)  3.35 us
  transfers between devices with their start and end apart: 1, of which 1 were waited for; matrix products, arithmetic and copies ran while one was open for 0% of the time, Pallas kernels for 1%

profile of v10, /device:TPU:1, one launch (start us, length us, event | category | flops | bytes accessed | tf_op | source)
XLA Modules:
  0.0 144.3 jit_solution(5534178957719620554)
XLA Ops:
  0.6 1.5 %project.2 = (f32[232,128]{1,0:T(8,128)S(1)}, f32[4,128]{1,0:T(4,128)S(1)}, f32[2,64]{1,0:T(2,128)S(1)}, f32[4,128]{1,0:T(4,128)S(1)}) custom-call(bf16[4,64]{1,0:T(4,128)(2,1)} %x_ref.1, f32[2,64]{1,0:T(2,128)} %gain_ref.1, bf16[2,3,64,512]{3,2,1,0:T(8,128)(2,1)} %bitcast.21, bf16[2,64,2048]{2,1,0:T(8,128)(2,1)} %wf_ref.3, s32[1,4]{1,0:T(1,128)} %bitcast.39), custom_call_target="tpu_custom_call" | custom-call | tf_op jit(solution)/shard_map/project/pallas_call | solution.py:163
  2.2 8.5 %all-gather = f32[464,128]{1,0:T(8,128)S(1)} all-gather(f32[232,128]{1,0:T(8,128)S(1)} %get-tuple-element.16), channel_id=2, replica_groups={{0,4},{8,12},{16,20},{24,28},{32,36},{40,44},{48,52},{56,60},{64,68},{7..., dimensions={0}, use_global_device_ids=true | all-gather | bytes 356352 | tf_op jit(solution)/shard_map/all_gather | solution.py:552
  10.7 0.2 pool.2
  10.9 21.0 %all_to_all.50 = bf16[16,8,2,128]{3,2,1,0:T(2,128)(2,1)S(1)} all-to-all(bf16[16,8,2,128]{3,2,1,0:T(2,128)(2,1)S(1)} %bitcast.31), channel_id=1, replica_groups={{0,8,16,24,32,40,48,56,64,72,80,88,96,104,112,120},{4,12,20,28,36,44,52..., dimensions={0} | all-to-all | bytes 131072 | tf_op jit(solution)/shard_map/all_to_all | solution.py:31
  31.9 0.3 finish.2
  32.2 0.0 copy-start.6
  32.2 11.0 %all_to_all.51.got_ref = bf16[8,8,128]{2,1,0:T(8,128)(2,1)S(1)} all-to-all(bf16[8,8,128]{2,1,0:T(8,128)(2,1)S(1)} %get-tuple-element.18), channel_id=1, replica_groups={{0,4,128,132,256,260,384,388},{8,12,136,140,264,268,392,396},{16,20,144..., dimensions={0} | all-to-all | bytes 32768 | tf_op jit(solution)/shard_map/all_to_all | solution.py:31
  43.3 1.1 attend.2
  44.5 8.1 %all_to_all.52.got_ref = f32[8,16,128]{2,1,0:T(8,128)S(1)} all-to-all(f32[8,16,128]{2,1,0:T(8,128)S(1)} %bitcast.32), channel_id=1, replica_groups={{0,4,128,132,256,260,384,388},{8,12,136,140,264,268,392,396},{16,20,144..., dimensions={0} | all-to-all | bytes 131072 | tf_op jit(solution)/shard_map/all_to_all | solution.py:31
  52.5 0.2 join.2
  52.7 14.4 %all_to_all.53 = bf16[16,10,2,128]{3,2,1,0:T(2,128)(2,1)S(1)} all-to-all(bf16[16,10,2,128]{3,2,1,0:T(2,128)(2,1)S(1)} %bitcast.29), channel_id=1, replica_groups={{0,8,16,24,32,40,48,56,64,72,80,88,96,104,112,120},{4,12,20,28,36,44,52..., dimensions={0} | all-to-all | bytes 163840 | tf_op jit(solution)/shard_map/all_to_all | solution.py:31
  67.1 0.5 settle.2
  67.6 3.9 %all_gather.20.got_ref.one_ref = bf16[128,128]{1,0:T(8,128)(2,1)S(1)} all-gather(bf16[64,128]{1,0:T(8,128)(2,1)S(1)} %settle.2), channel_id=1, replica_groups={{0,4},{8,12},{16,20},{24,28},{32,36},{40,44},{48,52},{56,60},{64,68},{7..., dimensions={0}, use_global_device_ids=true | all-gather | bytes 49152 | tf_op jit(solution)/shard_map/all_gather | solution.py:560
  71.5 0.2 output.2
  71.8 8.0 %all_to_all.54 = f32[4,4,128]{2,1,0:T(4,128)S(1)} all-to-all(f32[4,4,128]{2,1,0:T(4,128)S(1)} %bitcast.38), channel_id=1, replica_groups=mesh['rep'=4,'blk'=32,'tp'=4] {'tp'}, dimensions={0} | all-to-all | bytes 16384 | tf_op jit(solution)/shard_map/all_to_all | solution.py:31
  79.8 0.3 project.3
  80.1 3.4 %all-gather.1 = f32[464,128]{1,0:T(8,128)S(1)} all-gather(f32[232,128]{1,0:T(8,128)S(1)} %get-tuple-element.22), channel_id=3, replica_groups={{0,4},{8,12},{16,20},{24,28},{32,36},{40,44},{48,52},{56,60},{64,68},{7..., dimensions={0}, use_global_device_ids=true | all-gather | bytes 356352 | tf_op jit(solution)/shard_map/all_gather | solution.py:552
  83.5 0.2 pool.3
  83.7 14.5 %all_to_all.55 = bf16[16,8,2,128]{3,2,1,0:T(2,128)(2,1)S(1)} all-to-all(bf16[16,8,2,128]{3,2,1,0:T(2,128)(2,1)S(1)} %bitcast.33), channel_id=1, replica_groups={{0,8,16,24,32,40,48,56,64,72,80,88,96,104,112,120},{4,12,20,28,36,44,52..., dimensions={0} | all-to-all | bytes 131072 | tf_op jit(solution)/shard_map/all_to_all | solution.py:31
  98.1 0.3 finish.3
  98.4 9.0 %all_to_all.56.got_ref = bf16[8,8,128]{2,1,0:T(8,128)(2,1)S(1)} all-to-all(bf16[8,8,128]{2,1,0:T(8,128)(2,1)S(1)} %get-tuple-element.23), channel_id=1, replica_groups={{0,4,128,132,256,260,384,388},{8,12,136,140,264,268,392,396},{16,20,144..., dimensions={0} | all-to-all | bytes 32768 | tf_op jit(solution)/shard_map/all_to_all | solution.py:31
  107.4 1.1 attend.3
  108.6 7.9 %all_to_all.57.got_ref = f32[8,16,128]{2,1,0:T(8,128)S(1)} all-to-all(f32[8,16,128]{2,1,0:T(8,128)S(1)} %bitcast.34), channel_id=1, replica_groups={{0,4,128,132,256,260,384,388},{8,12,136,140,264,268,392,396},{16,20,144..., dimensions={0} | all-to-all | bytes 131072 | tf_op jit(solution)/shard_map/all_to_all | solution.py:31
  116.5 0.2 join.3
  116.7 14.3 %all_to_all.58 = bf16[16,10,2,128]{3,2,1,0:T(2,128)(2,1)S(1)} all-to-all(bf16[16,10,2,128]{3,2,1,0:T(2,128)(2,1)S(1)} %bitcast.30), channel_id=1, replica_groups={{0,8,16,24,32,40,48,56,64,72,80,88,96,104,112,120},{4,12,20,28,36,44,52..., dimensions={0} | all-to-all | bytes 163840 | tf_op jit(solution)/shard_map/all_to_all | solution.py:31
  131.0 0.5 settle.3
  131.5 3.9 %all_gather.23.got_ref.two_ref = bf16[128,128]{1,0:T(8,128)(2,1)S(1)} all-gather(bf16[64,128]{1,0:T(8,128)(2,1)S(1)} %settle.3), channel_id=1, replica_groups={{0,4},{8,12},{16,20},{24,28},{32,36},{40,44},{48,52},{56,60},{64,68},{7..., dimensions={0}, use_global_device_ids=true | all-gather | bytes 49152 | tf_op jit(solution)/shard_map/all_gather | solution.py:560
  135.4 0.9 output.3
  136.2 3.4 %all-to-all-start.9 = ((f32[4,4,128]{2,1,0:T(4,128)}), f32[4,4,128]{2,1,0:T(4,128)S(1)}, u32[]{:S(2)}, u32[]{:S(2)}) async-start(f32[4,4,128]{2,1,0:T(4,128)} %bitcast.18), calls=%async_computation.9 | async-start | bytes 16384 | tf_op jit(solution)/shard_map/all_to_all | solution.py:31
  139.6 1.7 %renew.1 = bf16[2,2,8,32,512]{4,3,2,1,0:T(8,128)(2,1)} custom-call(s32[8]{0:T(128)S(1)} %copy-done.5, s32[8]{0:T(128)S(1)} %copy-done.6, s32[8]{0:T(128)S(1)} %copy-done.8, bf16[128,128]{1,0:T(8,128)(2,1)S(1)} %all_gather.20.got_ref.one_ref, bf16[128,128]{1,0:T(8,128)(2,1)S(1)} %all_gather.23.got_ref.two_ref, bf16[2,2,8,32,512]{4,3,2,1,0:T(8,128)(2,1)S(1)} %copy-done), custom_call_target="tpu_custom_call" | custom-call | tf_op jit(solution)/shard_map/renew/pallas_call | solution.py:163
  141.3 2.5 %all-to-all-done.9 = f32[4,4,128]{2,1,0:T(4,128)S(1)} async-done(((f32[4,4,128]{2,1,0:T(4,128)}), f32[4,4,128]{2,1,0:T(4,128)S(1)}, u32[]{:S(2)}, u32[]{:S(2)}) %all-to-all-start.9) | async-done | bytes 8224 | tf_op jit(solution)/shard_map/all_to_all | solution.py:31
  143.7 0.6 add_convert_fusion
  (18 shorter events, 0.1 us)
Async XLA Ops:
  0.6 42.6 %copy-start = (bf16[2,2,8,32,512]{4,3,2,1,0:T(8,128)(2,1)S(1)}, bf16[2,2,8,32,512]{4,3,2,1,0:T(8,128)(2,1)}, u32[]{:S(2)}) copy-start(bf16[2,2,8,32,512]{4,3,2,1,0:T(8,128)(2,1)} %cache_ref.5) | copy-start | bytes 3145732
  32.2 11.1 %copy-start.5 = (s32[8]{0:T(128)S(1)}, s32[8]{0:T(128)}, u32[]{:S(2)}) copy-start(s32[8]{0:T(128)} %owner_ref.5) | copy-start | bytes 100
  32.2 11.1 %copy-start.6 = (s32[8]{0:T(128)S(1)}, s32[8]{0:T(128)}, u32[]{:S(2)}) copy-start(s32[8]{0:T(128)} %fill_ref.5) | copy-start | bytes 100
  32.2 11.1 %copy-start.7 = (s32[8]{0:T(128)S(1)}, s32[8]{0:T(128)}, u32[]{:S(2)}) copy-start(s32[8]{0:T(128)} %used_ref.3) | copy-start | bytes 100
  43.3 28.3 %copy-start.4 = (bf16[2,512,64]{1,2,0:T(8,128)(2,1)S(1)}, bf16[2,512,64]{1,2,0:T(8,128)(2,1)}, u32[]{:S(2)}) copy-start(bf16[2,512,64]{1,2,0:T(8,128)(2,1)} %param.16) | copy-start | bytes 393220
  43.3 36.5 %copy-start.3 = (bf16[2,64,3,512]{3,1,2,0:T(8,128)(2,1)S(1)}, bf16[2,64,3,512]{3,1,2,0:T(8,128)(2,1)}, u32[]{:S(2)}) copy-start(bf16[2,64,3,512]{3,1,2,0:T(8,128)(2,1)} %param.14) | copy-start | bytes 1179652
  44.5 27.1 %copy-start.2 = (bf16[2,2048,64]{1,2,0:T(8,128)(2,1)S(1)}, bf16[2,2048,64]{1,2,0:T(8,128)(2,1)}, u32[]{:S(2)}) copy-start(bf16[2,2048,64]{1,2,0:T(8,128)(2,1)} %param.17) | copy-start | bytes 1572868
  52.7 27.1 %copy-start.1 = (bf16[2,64,2048]{2,1,0:T(8,128)(2,1)S(1)}, bf16[2,64,2048]{2,1,0:T(8,128)(2,1)}, u32[]{:S(2)}) copy-start(bf16[2,64,2048]{2,1,0:T(8,128)(2,1)} %wf_ref.3) | copy-start | bytes 1572868
  136.2 3.4 %copy-start.8 = (s32[8]{0:T(128)S(1)}, s32[8]{0:T(128)}, u32[]{:S(2)}) copy-start(s32[8]{0:T(128)} %tail_ref.1) | copy-start | bytes 100
  136.2 7.5 %all-to-all-start.9 = ((f32[4,4,128]{2,1,0:T(4,128)}), f32[4,4,128]{2,1,0:T(4,128)S(1)}, u32[]{:S(2)}, u32[]{:S(2)}) async-start(f32[4,4,128]{2,1,0:T(4,128)} %bitcast.18), calls=%async_computation.9 | async-start | bytes 16384 | tf_op jit(solution)/shard_map/all_to_all | solution.py:31

commit v11 on v10

--- a/solution.py
+++ b/solution.py
@@ -100,16 +100,31 @@
     return jnp.sum(jnp.where(mine, row, 0.0), axis=1, keepdims=True)
 
 
+def page_holders(owners, used, fills):
+    page_of = iota((1, 256), 1) // PAGE
+    owner = jnp.zeros((1, 256), jnp.int32)
+    limit = jnp.zeros((1, 256), jnp.int32)
+    for page in range(8):
+        length = jnp.where(used[page] == 1, fills[page], 0)
+        owner = jnp.where(page_of == page, owners[page], owner)
+        limit = jnp.where(page_of == page, length, limit)
+    return jnp.where(iota((1, 256), 1) % PAGE < limit, owner, -1)
+
+
 def project_kernel(layer, x_ref, gain_ref, wq_ref, wf_ref, *refs):
     if layer == 0:
-        pos_ref, out_ref, state_ref, gain_held, factor_ref, q_held, f_held = refs[:7]
-        x_held, pos_held, sems = refs[7:]
+        pos_ref, *table_refs = refs[:4]
+        out_ref, state_ref, gain_held, factor_ref, holder_ref = refs[4:9]
+        q_held, f_held, x_held, pos_held, *tables, sems = refs[9:]
         copies = [
             pltpu.make_async_copy(x_ref, x_held, sems.at[0]),
             pltpu.make_async_copy(gain_ref, gain_held, sems.at[1]),
             pltpu.make_async_copy(wq_ref.at[0], q_held, sems.at[2]),
             pltpu.make_async_copy(wf_ref.at[0], f_held, sems.at[3]),
             pltpu.make_async_copy(pos_ref, pos_held, sems.at[4]),
+        ]
+        copies += [
+            pltpu.make_async_copy(table_refs[k], tables[k], sems.at[5 + k]) for k in range(3)
         ]
         for copy in copies:
             copy.start()
@@ -122,6 +137,9 @@
         mine = iota((4, 4), 0) == iota((4, 4), 1)
         places = jnp.sum(jnp.where(mine, places, 0.0), axis=1, keepdims=True)
         factor_ref[...] = rope_factors(places)
+        for copy in copies[5:]:
+            copy.wait()
+        holder_ref[...] = page_holders(*tables)
     else:
         branch_ref, out_ref, state_ref = refs
         x = x_ref[...] + branch_ref[0:4] + branch_ref[4:8] + branch_ref[8:12] + branch_ref[12:16]
@@ -178,12 +196,14 @@
     scratch = []
     if layer == 0:
         outs += [near_out(gain.shape, F32), near_out((4, 128), F32)]
+        outs += [near_out((1, 256), jnp.int32)]
         scratch = [
             pltpu.VMEM(wq.shape[1:], BF16),
             pltpu.VMEM(wf.shape[1:], BF16),
             pltpu.VMEM(x.shape, x.dtype),
             pltpu.VMEM((1, 4), jnp.int32),
-            pltpu.SemaphoreType.DMA((5,)),
+            *[pltpu.SMEM((8,), jnp.int32) for _ in range(3)],
+            pltpu.SemaphoreType.DMA((8,)),
         ]
     return call(
         functools.partial(project_kernel, layer),
@@ -196,7 +216,7 @@
         wq,
         wf,
         *more,
-        far=(0, 1, 2, 3, 4) if layer == 0 else (),
+        far=range(8) if layer == 0 else (),
     )
 
 
@@ -308,7 +328,7 @@
     )
 
 
-def attend_kernel(layer, owner_ref, used_ref, fill_ref, got_ref, cache_ref, out_ref):
+def attend_kernel(layer, got_ref, cache_ref, holder_ref, out_ref):
     tiles = []
     for tile in range(4):
         core, rows = tile // 2, 4 * (tile % 2)
@@ -328,16 +348,8 @@
     keys = cache_ref[layer, 0].reshape(8 * PAGE, 512)
     values = cache_ref[layer, 1].reshape(8 * PAGE, 512)
     scores = dot_t(wide, keys) * HD ** (-0.5)
-    page_of = iota((1, 256), 1) // PAGE
-    owner = jnp.zeros((1, 256), jnp.int32)
-    limit = jnp.zeros((1, 256), jnp.int32)
-    for page in range(8):
-        length = jnp.where(used_ref[page] == 1, fill_ref[page], 0)
-        owner = jnp.where(page_of == page, owner_ref[page], owner)
-        limit = jnp.where(page_of == page, length, limit)
-    owner = jnp.where(iota((1, 256), 1) % PAGE < limit, owner, -1)
     pair = iota((128, 256), 0)
-    allowed = 4 * (pair // 32) + pair % 16 // 4 == owner
+    allowed = 4 * (pair // 32) + pair % 16 // 4 == holder_ref[...]
     scores = jnp.where(allowed, scores, LOWEST)
     high = jnp.max(scores, axis=1, keepdims=True)
     weights = jnp.where(allowed, jnp.exp(scores - high), 0.0)
@@ -354,15 +366,16 @@
     )
 
 
-def attend(layer, tables, got, caches):
+def attend(layer, got, caches, holders):
     return call(
         functools.partial(attend_kernel, layer),
         "attend",
         (near_out((128, 128), F32),),
         [],
-        tables,
+        (),
         got,
         caches,
+        holders,
     )[0]
 
 
@@ -539,7 +552,7 @@
     pairs = [[2 * z, 2 * z + 1] for z in range(16)]
     rep_core = [[r * 32 + 2 * z + c for r in range(4) for c in range(2)] for z in range(16)]
 
-    more = (positions.reshape(1, 4),)
+    more = (positions.reshape(1, 4), page_owner, page_used, page_fill)
     w_qkv = w_qkv.transpose(0, 2, 1, 3)
     w_out = w_out.transpose(0, 2, 1)
     w_fc2 = w_fc2.transpose(0, 2, 1)
@@ -548,12 +561,12 @@
     for layer in range(LAYERS):
         parts, state, *kept = project(layer, state, gain, w_qkv, w_fc1, *more)
         if layer == 0:
-            gain, factors = kept
+            gain, factors, holders = kept
         parts = lax.all_gather(parts, "blk", axis_index_groups=pairs)
         got = exchange(pool(parts).reshape(16, FLOW // 2, 2, 128), "blk", zs)
         packed, query, extra = finish(got.reshape(16 * FLOW, 128), factors)
         got = exchange(packed, ("rep", "blk"), rep_core)
-        parts = attend(layer, (page_owner, page_used, page_fill), got, caches)
+        parts = attend(layer, got, caches, holders)
         parts = exchange(parts.reshape(8, 16, 128), ("rep", "blk"), rep_core)
         got = exchange(join(parts, extra).reshape(16, JOIN // 2, 2, 128), "blk", zs)
         got = settle(got.reshape(16 * JOIN, 128), query)
@@ -562,6 +575,7 @@
         out = output(layer, got, w_out, w_fc2).reshape(4, 4, 128)
         out = exchange(out, "tp")
         more = (out.reshape(16, 128),)
+    out, joined[1] = lax.optimization_barrier((out, joined[1]))
     result = (state[:, :HD] + jnp.sum(out, axis=0)[:, :HD]).astype(BF16)
     return (result, renew((page_owner, page_fill, page_tail), *joined, caches))
 

time: 145 us -> 144 us (level)
  blocking collectives: 128 us -> 134 us
  starting transfers between devices: 3.35 us -> 0 us
  waiting for transfers between devices: 2.46 us -> 0 us
  Pallas kernels: 9.18 us -> 7.62 us
    all_to_all x9 -> x10, blocking collectives: 108 us -> 115 us  [exchange(): lax.all_to_all(value, axis, 0, 0, tiled=True, axis_index_groups=groups)]
    all_to_all x1 -> x0, starting transfers between devices: 3.35 us -> none  [exchange(): lax.all_to_all(value, axis, 0, 0, tiled=True, axis_index_groups=groups)]
    all_to_all x1 -> x0, waiting for transfers between devices: 2.46 us -> none  [exchange(): lax.all_to_all(value, axis, 0, 0, tiled=True, axis_index_groups=groups)]
    pallas_call x15, Pallas kernels: 9.18 us -> 7.62 us  [call(): pl.pallas_call(kernel, in_specs=specs, out_specs=tuple((far_spec if k in...]
  transfers between devices with their start and end apart: 1 -> 0, of which waited for: 1 -> 0; matrix products, arithmetic and copies ran while one was open for 0% -> 0% of each run, Pallas kernels for 1% -> 0%
where the time goes in v11:
time: 144 us; the launch traced here: 143 us
  blocking collectives  134 us (93%)
  Pallas kernels  7.62 us (5%)
    all_to_all x10, blocking collectives, exchange(): lax.all_to_all(value, axis, 0, 0, tiled=True, axis_index_groups=groups)  115 us
    all_gather x2, blocking collectives, per_device(): parts = lax.all_gather(parts, 'blk', axis_index_groups=pairs)  11.9 us
    all_gather x2, blocking collectives, per_device(): got = lax.all_gather(got, 'blk', axis_index_groups=pairs, tiled=True)  7.8 us
    pallas_call x15, Pallas kernels, call(): pl.pallas_call(kernel, in_specs=specs, out_specs=tuple((far_spec if k in...  7.62 us

profile of v11, /device:TPU:1, one launch (start us, length us, event | category | flops | bytes accessed | tf_op | source)
XLA Modules:
  0.0 143.4 jit_solution(10144958881941470996)
XLA Ops:
  0.6 1.7 %project.2 = (f32[232,128]{1,0:T(8,128)S(1)}, f32[4,128]{1,0:T(4,128)S(1)}, f32[2,64]{1,0:T(2,128)S(1)}, f32[4,128]{1,0:T(4,128)S(1)}, s32[1,256]{1,0:T(1,128)S(1)}) custom-call(bf16[4,64]{1,0:T(4,128)(2,1)} %x_ref.1, f32[2,64]{1,0:T(2,128)} %gain_ref.1, bf16[2,3,64,512]{3,2,1,0:T(8,128)(2,1)} %bitcast.21, bf16[2,64,2048]{2,1,0:T(8,128)(2,1)} %wf_ref.3, ...), custom_call_target="tpu_custom_call" | custom-call | tf_op jit(solution)/shard_map/project/pallas_call | solution.py:181
  2.3 8.5 %all-gather = f32[464,128]{1,0:T(8,128)S(1)} all-gather(f32[232,128]{1,0:T(8,128)S(1)} %get-tuple-element.19), channel_id=2, replica_groups={{0,4},{8,12},{16,20},{24,28},{32,36},{40,44},{48,52},{56,60},{64,68},{7..., dimensions={0}, use_global_device_ids=true | all-gather | bytes 356352 | tf_op jit(solution)/shard_map/all_gather | solution.py:565
  10.8 0.2 pool.2
  11.0 21.0 %all_to_all.50 = bf16[16,8,2,128]{3,2,1,0:T(2,128)(2,1)S(1)} all-to-all(bf16[16,8,2,128]{3,2,1,0:T(2,128)(2,1)S(1)} %bitcast.32), channel_id=1, replica_groups={{0,8,16,24,32,40,48,56,64,72,80,88,96,104,112,120},{4,12,20,28,36,44,52..., dimensions={0} | all-to-all | bytes 131072 | tf_op jit(solution)/shard_map/all_to_all | solution.py:31
  32.1 0.3 finish.2
  32.4 10.9 %all_to_all.51.got_ref = bf16[8,8,128]{2,1,0:T(8,128)(2,1)S(1)} all-to-all(bf16[8,8,128]{2,1,0:T(8,128)(2,1)S(1)} %get-tuple-element.21), channel_id=1, replica_groups={{0,4,128,132,256,260,384,388},{8,12,136,140,264,268,392,396},{16,20,144..., dimensions={0} | all-to-all | bytes 32768 | tf_op jit(solution)/shard_map/all_to_all | solution.py:31
  43.3 0.6 attend.2
  43.9 8.1 %all_to_all.52.got_ref = f32[8,16,128]{2,1,0:T(8,128)S(1)} all-to-all(f32[8,16,128]{2,1,0:T(8,128)S(1)} %bitcast.33), channel_id=1, replica_groups={{0,4,128,132,256,260,384,388},{8,12,136,140,264,268,392,396},{16,20,144..., dimensions={0} | all-to-all | bytes 131072 | tf_op jit(solution)/shard_map/all_to_all | solution.py:31
  52.0 0.2 join.2
  52.2 14.4 %all_to_all.53 = bf16[16,10,2,128]{3,2,1,0:T(2,128)(2,1)S(1)} all-to-all(bf16[16,10,2,128]{3,2,1,0:T(2,128)(2,1)S(1)} %bitcast.29), channel_id=1, replica_groups={{0,8,16,24,32,40,48,56,64,72,80,88,96,104,112,120},{4,12,20,28,36,44,52..., dimensions={0} | all-to-all | bytes 163840 | tf_op jit(solution)/shard_map/all_to_all | solution.py:31
  66.6 0.5 settle.2
  67.1 3.9 %all_gather.20.got_ref.one_ref = bf16[128,128]{1,0:T(8,128)(2,1)S(1)} all-gather(bf16[64,128]{1,0:T(8,128)(2,1)S(1)} %settle.2), channel_id=1, replica_groups={{0,4},{8,12},{16,20},{24,28},{32,36},{40,44},{48,52},{56,60},{64,68},{7..., dimensions={0}, use_global_device_ids=true | all-gather | bytes 49152 | tf_op jit(solution)/shard_map/all_gather | solution.py:573
  71.0 0.2 output.2
  71.2 8.0 %all_to_all.54 = f32[4,4,128]{2,1,0:T(4,128)S(1)} all-to-all(f32[4,4,128]{2,1,0:T(4,128)S(1)} %bitcast.38), channel_id=1, replica_groups=mesh['rep'=4,'blk'=32,'tp'=4] {'tp'}, dimensions={0} | all-to-all | bytes 16384 | tf_op jit(solution)/shard_map/all_to_all | solution.py:31
  79.2 0.3 project.3
  79.5 3.4 %all-gather.1 = f32[464,128]{1,0:T(8,128)S(1)} all-gather(f32[232,128]{1,0:T(8,128)S(1)} %get-tuple-element.26), channel_id=3, replica_groups={{0,4},{8,12},{16,20},{24,28},{32,36},{40,44},{48,52},{56,60},{64,68},{7..., dimensions={0}, use_global_device_ids=true | all-gather | bytes 356352 | tf_op jit(solution)/shard_map/all_gather | solution.py:565
  82.9 0.2 pool.3
  83.1 14.5 %all_to_all.55 = bf16[16,8,2,128]{3,2,1,0:T(2,128)(2,1)S(1)} all-to-all(bf16[16,8,2,128]{3,2,1,0:T(2,128)(2,1)S(1)} %bitcast.34), channel_id=1, replica_groups={{0,8,16,24,32,40,48,56,64,72,80,88,96,104,112,120},{4,12,20,28,36,44,52..., dimensions={0} | all-to-all | bytes 131072 | tf_op jit(solution)/shard_map/all_to_all | solution.py:31
  97.6 0.3 finish.3
  97.9 9.0 %all_to_all.56.got_ref = bf16[8,8,128]{2,1,0:T(8,128)(2,1)S(1)} all-to-all(bf16[8,8,128]{2,1,0:T(8,128)(2,1)S(1)} %get-tuple-element.27), channel_id=1, replica_groups={{0,4,128,132,256,260,384,388},{8,12,136,140,264,268,392,396},{16,20,144..., dimensions={0} | all-to-all | bytes 32768 | tf_op jit(solution)/shard_map/all_to_all | solution.py:31
  106.9 0.6 attend.3
  107.5 7.9 %all_to_all.57.got_ref = f32[8,16,128]{2,1,0:T(8,128)S(1)} all-to-all(f32[8,16,128]{2,1,0:T(8,128)S(1)} %bitcast.31), channel_id=1, replica_groups={{0,4,128,132,256,260,384,388},{8,12,136,140,264,268,392,396},{16,20,144..., dimensions={0} | all-to-all | bytes 131072 | tf_op jit(solution)/shard_map/all_to_all | solution.py:31
  115.4 0.2 join.3
  115.6 14.3 %all_to_all.58 = bf16[16,10,2,128]{3,2,1,0:T(2,128)(2,1)S(1)} all-to-all(bf16[16,10,2,128]{3,2,1,0:T(2,128)(2,1)S(1)} %bitcast.30), channel_id=1, replica_groups={{0,8,16,24,32,40,48,56,64,72,80,88,96,104,112,120},{4,12,20,28,36,44,52..., dimensions={0} | all-to-all | bytes 163840 | tf_op jit(solution)/shard_map/all_to_all | solution.py:31
  129.8 0.5 settle.3
  130.3 3.9 %all_gather.23.got_ref.two_ref = bf16[128,128]{1,0:T(8,128)(2,1)S(1)} all-gather(bf16[64,128]{1,0:T(8,128)(2,1)S(1)} %settle.3), channel_id=1, replica_groups={{0,4},{8,12},{16,20},{24,28},{32,36},{40,44},{48,52},{56,60},{64,68},{7..., dimensions={0}, use_global_device_ids=true | all-gather | bytes 49152 | tf_op jit(solution)/shard_map/all_gather | solution.py:573
  134.2 0.2 output.3
  134.5 6.5 %all_to_all.59 = f32[4,4,128]{2,1,0:T(4,128)S(1)} all-to-all(f32[4,4,128]{2,1,0:T(4,128)S(1)} %bitcast.39), channel_id=1, replica_groups=mesh['rep'=4,'blk'=32,'tp'=4] {'tp'}, dimensions={0} | all-to-all | bytes 16384 | tf_op jit(solution)/shard_map/all_to_all | solution.py:31
  141.0 0.6 add_convert_fusion
  141.6 0.1 copy-done.5
  141.7 0.0 copy-done.7
  141.7 1.6 %renew.1 = bf16[2,2,8,32,512]{4,3,2,1,0:T(8,128)(2,1)} custom-call(s32[8]{0:T(128)S(1)} %copy-done.5, s32[8]{0:T(128)S(1)} %copy-done.6, s32[8]{0:T(128)S(1)} %copy-done.7, bf16[128,128]{1,0:T(8,128)(2,1)S(1)} %all_gather.20.got_ref.one_ref, bf16[128,128]{1,0:T(8,128)(2,1)S(1)} %all_gather.23.got_ref.two_ref, bf16[2,2,8,32,512]{4,3,2,1,0:T(8,128)(2,1)S(1)} %copy-done), custom_call_target="tpu_custom_call" | custom-call | tf_op jit(solution)/shard_map/renew/pallas_call | solution.py:181
  (15 shorter events, 0.1 us)
Async XLA Ops:
  0.6 42.7 %copy-start = (bf16[2,2,8,32,512]{4,3,2,1,0:T(8,128)(2,1)S(1)}, bf16[2,2,8,32,512]{4,3,2,1,0:T(8,128)(2,1)}, u32[]{:S(2)}) copy-start(bf16[2,2,8,32,512]{4,3,2,1,0:T(8,128)(2,1)} %cache_ref.5) | copy-start | bytes 3145732
  43.3 27.7 %copy-start.4 = (bf16[2,512,64]{1,2,0:T(8,128)(2,1)S(1)}, bf16[2,512,64]{1,2,0:T(8,128)(2,1)}, u32[]{:S(2)}) copy-start(bf16[2,512,64]{1,2,0:T(8,128)(2,1)} %param.16) | copy-start | bytes 393220
  43.3 35.9 %copy-start.3 = (bf16[2,64,3,512]{3,1,2,0:T(8,128)(2,1)S(1)}, bf16[2,64,3,512]{3,1,2,0:T(8,128)(2,1)}, u32[]{:S(2)}) copy-start(bf16[2,64,3,512]{3,1,2,0:T(8,128)(2,1)} %param.14) | copy-start | bytes 1179652
  43.9 27.1 %copy-start.2 = (bf16[2,2048,64]{1,2,0:T(8,128)(2,1)S(1)}, bf16[2,2048,64]{1,2,0:T(8,128)(2,1)}, u32[]{:S(2)}) copy-start(bf16[2,2048,64]{1,2,0:T(8,128)(2,1)} %param.17) | copy-start | bytes 1572868
  52.1 27.1 %copy-start.1 = (bf16[2,64,2048]{2,1,0:T(8,128)(2,1)S(1)}, bf16[2,64,2048]{2,1,0:T(8,128)(2,1)}, u32[]{:S(2)}) copy-start(bf16[2,64,2048]{2,1,0:T(8,128)(2,1)} %wf_ref.3) | copy-start | bytes 1572868
  141.0 0.7 copy-start.5
  141.0 0.7 copy-start.6
  141.0 0.7 copy-start.7
